TPU v7x, 32 devices: a whole 2x2x4 slice. The times are simulated.
32 devices in a mesh: dp: 4 (over y, x), seq: 4 (over z), tensor: 2 (over core).
Axes of the slice: x: 2, y: 2, z: 4, core: 2. Of those that a mesh axis runs over, the one named last changes fastest.
Arguments:
- inputs: bfloat16 [2, 4, 2048, 2048], P(None, 'dp', ('seq', 'tensor')), may hold values from -6 to 6
- lengths: int32 [2, 4, 3], P(None, 'dp'), may hold values from 1 to 1536, 2048 in all within a row
- first_gain: bfloat16 [2048], P(('dp', 'seq')), may hold values from 0.5 to 1.5
- second_gain: bfloat16 [2048], P(('dp', 'seq')), may hold values from 0.5 to 1.5
- query_weight: bfloat16 [2048, 2048], P(('dp', 'seq'), 'tensor'), may hold values from -0.125 to 0.125
- key_weight: bfloat16 [2048, 2048], P(('dp', 'seq'), 'tensor'), may hold values from -0.125 to 0.125
- value_weight: bfloat16 [2048, 4096], P(('dp', 'seq'), 'tensor'), may hold values from -0.125 to 0.125
- gate_weight: bfloat16 [2048, 4096], P(('dp', 'seq'), 'tensor'), may hold values from -0.125 to 0.125
- out_weight: bfloat16 [2048, 4096], P(('dp', 'seq'), 'tensor'), may hold values from -0.1875 to 0.1875
- up_weight: bfloat16 [2048, 4096], P(('dp', 'seq'), 'tensor'), may hold values from -0.125 to 0.125
- down_weight: bfloat16 [2048, 4096], P(('dp', 'seq'), 'tensor'), may hold values from -0.125 to 0.125
- out_cotangent: bfloat16 [2, 4, 2048, 2048], P(None, 'dp', ('seq', 'tensor')), may hold values from -6 to 6
Outputs:
- output: bfloat16 [2, 4, 2048, 2048], P(None, 'dp', ('seq', 'tensor'))
- grad_inputs: bfloat16 [2, 4, 2048, 2048], P(None, 'dp', ('seq', 'tensor'))
- grad_first_gain: float32 [2048], P(('dp', 'seq'))
- grad_second_gain: float32 [2048], P(('dp', 'seq'))
- grad_query: float32 [2048, 2048], P(('dp', 'seq'), 'tensor')
- grad_key: float32 [2048, 2048], P(('dp', 'seq'), 'tensor')
- grad_value: float32 [2048, 4096], P(('dp', 'seq'), 'tensor')
- grad_gate: float32 [2048, 4096], P(('dp', 'seq'), 'tensor')
- grad_out: float32 [2048, 4096], P(('dp', 'seq'), 'tensor')
- grad_up: float32 [2048, 4096], P(('dp', 'seq'), 'tensor')
- grad_down: float32 [2048, 4096], P(('dp', 'seq'), 'tensor')
Inputs may be any that keep to these rules, and one draw needn't show every extreme that they name: The 3 lengths of a row sum to 2048.
All inputs are finite; a program needn't handle non-finite values.
Results may differ from a plain program's by a relative error of at most 0.024.
Values may be sent and summed in bfloat16 or wider, within the bound.
No kernel may reach another device: no remote copies, remote signals or barrier semaphores. Data moves between devices by JAX's collectives and lax.ppermute only.
A program may use at most 448 MiB of HBM per device.

v0:
```python
import math

import jax
import jax.numpy as jnp
from jax import lax
from jax.sharding import PartitionSpec as P

D = 2048
QK = 256
HV = 512


PRECISION_MAX = lax.Precision.HIGHEST
EPSILON = 1e-05
GROUP_EPSILON = 1.0
XPOS_BASE = 512.0


def entering(value, axis, combine, identity, reverse):
    length, mine = (lax.axis_size(axis), lax.axis_index(axis))
    everything = jax.tree.map(
        lambda part, kind: lax.all_gather(part.astype(kind), axis),
        value,
        (jnp.bfloat16, jnp.bfloat16),
    )
    start = jax.tree.map(
        lambda part, zero: jnp.broadcast_to(jnp.asarray(zero, part.dtype), part.shape),
        value,
        identity,
    )

    def step(k, before):
        at = length - 1 - k if reverse else k
        reached = at > mine if reverse else at < mine
        new = combine(
            before, jax.tree.map(lambda part, own: part[at].astype(own.dtype), everything, value)
        )
        return jax.tree.map(lambda a, b: jnp.where(reached, a, b), new, before)

    return lax.fori_loop(0, length, step, start)


def norm_rows(values, offset):
    centre = values - jnp.mean(values, axis=-1, keepdims=True)
    inv_scale = lax.rsqrt(jnp.mean(centre * centre, axis=-1, keepdims=True) + offset)
    return (centre * inv_scale, inv_scale)


def norm_back(grad_terms, normed, inv_scale):
    grad_mean = jnp.mean(grad_terms, axis=-1, keepdims=True)
    cross_mean = jnp.mean(grad_terms * normed, axis=-1, keepdims=True)
    return inv_scale * (grad_terms - grad_mean - normed * cross_mean)


def layout(lengths_row, first_place, number):
    starts = jnp.cumsum(lengths_row, dtype=jnp.int32) - lengths_row
    places = first_place + jnp.arange(number, dtype=jnp.int32)
    is_after = places[:, None] >= starts[None, :]
    documents = jnp.sum(is_after.astype(jnp.int32), axis=1, dtype=jnp.int32) - 1
    begins = jnp.max(
        jnp.where(is_after, starts[None, :], jnp.zeros((1, starts.shape[0]), jnp.int32)), axis=1
    )
    return (documents, places - begins)


def rotation(places, sign_exp, head_width):
    half_width = head_width // 2
    pair_index = jnp.arange(half_width, dtype=jnp.float32)
    frequency = jnp.exp(pair_index * (-math.log(10000.0) / half_width))
    zeta_base = (2.0 * pair_index + 0.4 * head_width) / (1.4 * head_width)
    place_f = places.astype(jnp.float32)[:, None]
    angle_t = place_f * frequency[None, :]
    factor = jnp.exp(place_f * (sign_exp / XPOS_BASE) * jnp.log(zeta_base)[None, :])
    return (jnp.cos(angle_t) * factor, jnp.sin(angle_t) * factor)


def rotate(values, cos_table, sin_table):
    half_width = values.shape[-1] // 2
    first_half = values[..., :half_width]
    second_half = values[..., half_width:]
    return jnp.concatenate(
        [
            first_half * cos_table - second_half * sin_table,
            first_half * sin_table + second_half * cos_table,
        ],
        axis=-1,
    )


def rotate_back(grad_terms, cos_table, sin_table):
    half_width = grad_terms.shape[-1] // 2
    first_half = grad_terms[..., :half_width]
    second_half = grad_terms[..., half_width:]
    return jnp.concatenate(
        [
            first_half * cos_table + second_half * sin_table,
            second_half * cos_table - first_half * sin_table,
        ],
        axis=-1,
    )


def decay_parts(documents, previous, log_gamma):
    tokens_n = documents.shape[0]
    steps_f = jnp.arange(tokens_n, dtype=jnp.float32)
    distance = steps_f[:, None] - steps_f[None, :]
    same_doc = (documents[:, None] == documents[None, :]) & (distance >= 0.0)
    inner_decay = jnp.where(
        same_doc[None], jnp.exp(jnp.maximum(distance, 0.0)[None] * log_gamma[:, None, None]), 0.0
    )
    carried = jnp.where(
        (documents == previous)[None, :],
        jnp.exp((steps_f + 1.0)[None, :] * log_gamma[:, None]),
        0.0,
    )
    last_doc = documents[tokens_n - 1]
    leaving = jnp.where(
        (documents == last_doc)[None, :],
        jnp.exp((tokens_n - 1.0 - steps_f)[None, :] * log_gamma[:, None]),
        0.0,
    )
    through = jnp.where(previous == last_doc, jnp.exp(tokens_n * log_gamma), 0.0)
    return (inner_decay, carried, leaving, through)


def gelu_exact(values):
    return jax.nn.gelu(values, approximate=False)


def matmul(left_side, right_side):
    return jnp.dot(left_side, right_side, preferred_element_type=jnp.float32)


def matmul_t(left_side, right_side):
    return lax.dot_general(
        left_side, right_side, (((1,), (1,)), ((), ())), preferred_element_type=jnp.float32
    )


def tmatmul(left_side, right_side):
    return lax.dot_general(
        left_side, right_side, (((0,), (0,)), ((), ())), preferred_element_type=jnp.float32
    )


def chain_forward(earlier, latter):
    return (latter[1][..., None, None] * earlier[0] + latter[0], earlier[1] * latter[1])


def chain_backward(earlier, latter):
    return (latter[0] + latter[1][..., None, None] * earlier[0], earlier[1] * latter[1])


def body(
    inputs,
    lengths,
    first_gain,
    second_gain,
    query_weight,
    key_weight,
    value_weight,
    gate_weight,
    out_weight,
    up_weight,
    down_weight,
    out_cotangent,
):
    rows_here = inputs.shape[1]
    shard_len = inputs.shape[2]
    block_len = shard_len * lax.axis_size("tensor")
    block_start = lax.axis_index("seq") * block_len
    own_start = lax.axis_index("tensor") * shard_len
    heads_here = query_weight.shape[1] // QK
    head_index = (
        lax.axis_index("tensor") * heads_here + jnp.arange(heads_here, dtype=jnp.int32)
    ).astype(jnp.float32)
    log_gamma = jnp.log1p(-jnp.exp2(-5.0 - head_index))
    tokens_here = rows_here * block_len
    half_width = QK // 2

    def own_part(values):
        return lax.dynamic_slice_in_dim(values, own_start, shard_len, 1)

    def row_plan(lengths_row):
        documents, places = layout(lengths_row, block_start, block_len)
        previous, unused = layout(lengths_row, block_start - 1, 1)
        return (documents, places, previous[0])

    def micro_step(totals, pieces):
        inputs_mb, lengths_mb, cotangent_mb = pieces
        gathered = (
            lax.all_gather(first_gain, ("dp", "seq"), axis=0, tiled=True),
            lax.all_gather(second_gain, ("dp", "seq"), axis=0, tiled=True),
            lax.all_gather(query_weight, ("dp", "seq"), axis=0, tiled=True),
            lax.all_gather(key_weight, ("dp", "seq"), axis=0, tiled=True),
            lax.all_gather(value_weight, ("dp", "seq"), axis=0, tiled=True),
            lax.all_gather(gate_weight, ("dp", "seq"), axis=0, tiled=True),
            lax.all_gather(out_weight, ("dp", "seq"), axis=0, tiled=True),
            lax.all_gather(up_weight, ("dp", "seq"), axis=0, tiled=True),
            lax.all_gather(down_weight, ("dp", "seq"), axis=0, tiled=True),
        )
        gain_one = gathered[0].astype(jnp.float32)
        gain_two = gathered[1].astype(jnp.float32)
        documents, places, previous = jax.vmap(row_plan)(lengths_mb)
        flat_places = places.reshape(-1)
        cos_query, sin_query = rotation(flat_places, 1.0, QK)
        cos_key, sin_key = rotation(flat_places, -1.0, QK)
        cos_query = cos_query.reshape(rows_here, block_len, 1, half_width)
        sin_query = sin_query.reshape(rows_here, block_len, 1, half_width)
        cos_key = cos_key.reshape(rows_here, block_len, 1, half_width)
        sin_key = sin_key.reshape(rows_here, block_len, 1, half_width)
        inner_decay, carried, leaving, through = jax.vmap(decay_parts, in_axes=(0, 0, None))(
            documents, previous, log_gamma
        )
        carried_t = jnp.swapaxes(carried, 1, 2)[..., None]
        leaving_t = jnp.swapaxes(leaving, 1, 2)[..., None]
        inputs_block = lax.all_gather(inputs_mb, "tensor", axis=1, tiled=True)
        residual_block = inputs_block.astype(jnp.float32)
        normed_block, inv_block = norm_rows(residual_block, EPSILON)
        hidden_first = (normed_block * gain_one).astype(jnp.bfloat16).reshape(tokens_here, -1)
        normed_first = own_part(normed_block)
        inv_first = own_part(inv_block)
        residual_in = own_part(residual_block)
        query_pre = matmul(hidden_first, gathered[2]).reshape(rows_here, block_len, heads_here, QK)
        key_pre = matmul(hidden_first, gathered[3]).reshape(rows_here, block_len, heads_here, QK)
        value_rows = (
            matmul(hidden_first, gathered[4])
            .astype(jnp.bfloat16)
            .reshape(rows_here, block_len, heads_here, HV)
        )
        gate_pre = matmul(hidden_first, gathered[5])
        queries = rotate(query_pre, cos_query, sin_query).astype(jnp.bfloat16)
        key_rows = rotate(key_pre, cos_key, sin_key).astype(jnp.bfloat16)
        score_matrix = jnp.einsum(
            "rnhd,rmhd->rhnm", queries, key_rows, preferred_element_type=jnp.float32
        )
        score_weights = (score_matrix * inner_decay).astype(jnp.bfloat16)
        intra_part = jnp.einsum(
            "rhnm,rmhe->rnhe", score_weights, value_rows, preferred_element_type=jnp.float32
        )
        decayed_keys = key_rows.astype(jnp.float32) * leaving_t
        values_wide = value_rows.astype(jnp.float32)
        block_state = jnp.einsum(
            "rmhd,rmhe->rhde", decayed_keys, values_wide, precision=PRECISION_MAX
        )
        state_in = entering(
            (block_state, through),
            "seq",
            chain_forward,
            (jnp.zeros_like(block_state), jnp.ones_like(through)),
            False,
        )[0]
        queries_carried = queries.astype(jnp.float32) * carried_t
        retained = intra_part + jnp.einsum(
            "rnhd,rhde->rnhe", queries_carried, state_in, precision=PRECISION_MAX
        )
        grouped, inv_group = norm_rows(retained, GROUP_EPSILON)
        gate_act = jax.nn.silu(gate_pre)
        grouped_flat = grouped.reshape(tokens_here, -1)
        mixed_rows = (gate_act * grouped_flat).astype(jnp.bfloat16)
        attn_part = matmul_t(mixed_rows, gathered[6]).reshape(rows_here, block_len, -1)
        middle = residual_in + lax.psum_scatter(
            attn_part.astype(jnp.bfloat16), "tensor", scatter_dimension=1, tiled=True
        ).astype(jnp.float32)
        normed_second, inv_second = norm_rows(middle, EPSILON)
        second_local = (normed_second * gain_two).astype(jnp.bfloat16)
        hidden_second = lax.all_gather(second_local, "tensor", axis=1, tiled=True).reshape(
            tokens_here, -1
        )
        up_pre = matmul(hidden_second, gathered[7])
        activated = gelu_exact(up_pre).astype(jnp.bfloat16)
        ffn_part = matmul_t(activated, gathered[8]).reshape(rows_here, block_len, -1)
        outputs = (
            middle
            + lax.psum_scatter(
                ffn_part.astype(jnp.bfloat16), "tensor", scatter_dimension=1, tiled=True
            ).astype(jnp.float32)
        ).astype(jnp.bfloat16)
        back_weights = (
            lax.all_gather(first_gain, ("dp", "seq"), axis=0, tiled=True),
            lax.all_gather(second_gain, ("dp", "seq"), axis=0, tiled=True),
            lax.all_gather(query_weight, ("dp", "seq"), axis=0, tiled=True),
            lax.all_gather(key_weight, ("dp", "seq"), axis=0, tiled=True),
            lax.all_gather(value_weight, ("dp", "seq"), axis=0, tiled=True),
            lax.all_gather(gate_weight, ("dp", "seq"), axis=0, tiled=True),
            lax.all_gather(out_weight, ("dp", "seq"), axis=0, tiled=True),
            lax.all_gather(up_weight, ("dp", "seq"), axis=0, tiled=True),
            lax.all_gather(down_weight, ("dp", "seq"), axis=0, tiled=True),
        )
        cotangent_block = lax.all_gather(cotangent_mb, "tensor", axis=1, tiled=True)
        grad_rows = cotangent_block.reshape(tokens_here, -1)
        grad_act = matmul(grad_rows, back_weights[8])
        grad_down = tmatmul(grad_rows, activated)
        grad_up_pre = jax.vjp(gelu_exact, up_pre)[1](grad_act)[0].astype(jnp.bfloat16)
        grad_up = tmatmul(hidden_second, grad_up_pre)
        second_part = matmul_t(grad_up_pre, back_weights[7]).reshape(rows_here, block_len, -1)
        back_gain_two = back_weights[1].astype(jnp.float32)
        back_second = lax.psum_scatter(
            second_part.astype(jnp.bfloat16), "tensor", scatter_dimension=1, tiled=True
        ).astype(jnp.float32)
        grad_gain_two = jnp.sum(back_second * normed_second, axis=(0, 1))
        grad_middle = cotangent_mb.astype(jnp.float32) + norm_back(
            back_second * back_gain_two, normed_second, inv_second
        )
        grad_attn = lax.all_gather(
            grad_middle.astype(jnp.bfloat16), "tensor", axis=1, tiled=True
        ).reshape(tokens_here, -1)
        grad_mixed = matmul(grad_attn, back_weights[6])
        grad_out = tmatmul(grad_attn, mixed_rows)
        grad_gate_pre = jax.vjp(jax.nn.silu, gate_pre)[1](grad_mixed * grouped_flat)[0].astype(
            jnp.bfloat16
        )
        grad_grouped = (grad_mixed * gate_act).reshape(rows_here, block_len, heads_here, HV)
        grad_retained = norm_back(grad_grouped, grouped, inv_group).astype(jnp.bfloat16)
        grad_scores = jnp.einsum(
            "rnhe,rmhe->rhnm", grad_retained, value_rows, preferred_element_type=jnp.float32
        )
        score_grads = (grad_scores * inner_decay).astype(jnp.bfloat16)
        retained_wide = grad_retained.astype(jnp.float32)
        direct = jnp.einsum(
            "rnhd,rnhe->rhde", queries_carried, retained_wide, precision=PRECISION_MAX
        )
        state_out = entering(
            (direct, through),
            "seq",
            chain_backward,
            (jnp.zeros_like(direct), jnp.ones_like(through)),
            True,
        )[0]
        grad_queries = jnp.einsum(
            "rhnm,rmhd->rnhd", score_grads, key_rows, preferred_element_type=jnp.float32
        ) + carried_t * jnp.einsum(
            "rnhe,rhde->rnhd", retained_wide, state_in, precision=PRECISION_MAX
        )
        grad_keys = jnp.einsum(
            "rhnm,rnhd->rmhd", score_grads, queries, preferred_element_type=jnp.float32
        ) + leaving_t * jnp.einsum(
            "rmhe,rhde->rmhd", values_wide, state_out, precision=PRECISION_MAX
        )
        grad_values = jnp.einsum(
            "rhnm,rnhe->rmhe", score_weights, grad_retained, preferred_element_type=jnp.float32
        ) + jnp.einsum("rmhd,rhde->rmhe", decayed_keys, state_out, precision=PRECISION_MAX)
        grad_query_pre = (
            rotate_back(grad_queries, cos_query, sin_query)
            .astype(jnp.bfloat16)
            .reshape(tokens_here, -1)
        )
        grad_key_pre = (
            rotate_back(grad_keys, cos_key, sin_key).astype(jnp.bfloat16).reshape(tokens_here, -1)
        )
        grad_value_pre = grad_values.astype(jnp.bfloat16).reshape(tokens_here, -1)
        grad_query = tmatmul(hidden_first, grad_query_pre)
        grad_key = tmatmul(hidden_first, grad_key_pre)
        grad_value = tmatmul(hidden_first, grad_value_pre)
        grad_gate = tmatmul(hidden_first, grad_gate_pre)
        first_part = matmul_t(grad_query_pre, back_weights[2]) + matmul_t(
            grad_key_pre, back_weights[3]
        )
        first_part = (
            first_part
            + matmul_t(grad_value_pre, back_weights[4])
            + matmul_t(grad_gate_pre, back_weights[5])
        )
        back_first = lax.psum_scatter(
            first_part.reshape(rows_here, block_len, -1).astype(jnp.bfloat16),
            "tensor",
            scatter_dimension=1,
            tiled=True,
        ).astype(jnp.float32)
        grad_gain_one = jnp.sum(back_first * normed_first, axis=(0, 1))
        grad_inputs = (
            grad_middle
            + norm_back(back_first * back_weights[0].astype(jnp.float32), normed_first, inv_first)
        ).astype(jnp.bfloat16)
        step_grads = (
            grad_gain_one,
            grad_gain_two,
            grad_query,
            grad_key,
            grad_value,
            grad_gate,
            grad_out,
            grad_up,
            grad_down,
        )
        totals = tuple((running + adding for running, adding in zip(totals, step_grads)))
        return (totals, (outputs, grad_inputs))

    zero_totals = tuple(
        (
            jnp.zeros((D,) + member.shape[1:], jnp.float32)
            for member in (
                first_gain,
                second_gain,
                query_weight,
                key_weight,
                value_weight,
                gate_weight,
                out_weight,
                up_weight,
                down_weight,
            )
        )
    )
    totals, (outputs, grad_inputs) = lax.scan(
        micro_step, zero_totals, (inputs, lengths, out_cotangent)
    )
    reduced = (
        lax.psum_scatter(
            totals[0].astype(jnp.bfloat16), ("dp", "seq"), scatter_dimension=0, tiled=True
        ).astype(jnp.float32),
        lax.psum_scatter(
            totals[1].astype(jnp.bfloat16), ("dp", "seq"), scatter_dimension=0, tiled=True
        ).astype(jnp.float32),
        lax.psum_scatter(
            totals[2].astype(jnp.bfloat16), ("dp", "seq"), scatter_dimension=0, tiled=True
        ).astype(jnp.float32),
        lax.psum_scatter(
            totals[3].astype(jnp.bfloat16), ("dp", "seq"), scatter_dimension=0, tiled=True
        ).astype(jnp.float32),
        lax.psum_scatter(
            totals[4].astype(jnp.bfloat16), ("dp", "seq"), scatter_dimension=0, tiled=True
        ).astype(jnp.float32),
        lax.psum_scatter(
            totals[5].astype(jnp.bfloat16), ("dp", "seq"), scatter_dimension=0, tiled=True
        ).astype(jnp.float32),
        lax.psum_scatter(
            totals[6].astype(jnp.bfloat16), ("dp", "seq"), scatter_dimension=0, tiled=True
        ).astype(jnp.float32),
        lax.psum_scatter(
            totals[7].astype(jnp.bfloat16), ("dp", "seq"), scatter_dimension=0, tiled=True
        ).astype(jnp.float32),
        lax.psum_scatter(
            totals[8].astype(jnp.bfloat16), ("dp", "seq"), scatter_dimension=0, tiled=True
        ).astype(jnp.float32),
    )
    gain_sums = lax.psum((reduced[0], reduced[1]), "tensor")
    return (
        outputs,
        grad_inputs,
        gain_sums[0],
        gain_sums[1],
        reduced[2],
        reduced[3],
        reduced[4],
        reduced[5],
        reduced[6],
        reduced[7],
        reduced[8],
    )


def solution(mesh):
    placed = (
        P(None, "dp", ("seq", "tensor"), None),
        P(None, "dp", None),
        P(("dp", "seq")),
        P(("dp", "seq")),
        P(("dp", "seq"), "tensor"),
        P(("dp", "seq"), "tensor"),
        P(("dp", "seq"), "tensor"),
        P(("dp", "seq"), "tensor"),
        P(("dp", "seq"), "tensor"),
        P(("dp", "seq"), "tensor"),
        P(("dp", "seq"), "tensor"),
        P(None, "dp", ("seq", "tensor"), None),
    )
    return jax.shard_map(
        body,
        mesh=mesh,
        in_specs=placed,
        out_specs=(
            P(None, "dp", ("seq", "tensor"), None),
            P(None, "dp", ("seq", "tensor"), None),
            P(("dp", "seq")),
            P(("dp", "seq")),
            P(("dp", "seq"), "tensor"),
            P(("dp", "seq"), "tensor"),
            P(("dp", "seq"), "tensor"),
            P(("dp", "seq"), "tensor"),
            P(("dp", "seq"), "tensor"),
            P(("dp", "seq"), "tensor"),
            P(("dp", "seq"), "tensor"),
        ),
        check_vma=False,
    )
```

profile of v0, /device:TPU:0, one launch (start us, length us, event | category | flops | bytes accessed | tf_op | source)
XLA Modules:
  0.0 3460.7 jit_solution(12949892156449921969)
XLA Ops:
  11.0 2328.9 %while.86 = (s32[]{:T(128)}, f32[2048]{0:T(1024)}, f32[2048]{0:T(1024)}, f32[2048,1024]{1,0:T(8,128)}, f32[2048,1024]{1,0:T(8,128)}, /*index=5*/f32[2048,2048]{1...) while((s32[]{:T(128)}, f32[2048]{0:T(1024)}, ...), condition=%wide.region_27.28_spmd.clone, body=%wide.region_0.27_spmd.clone.sunk | while | flops 101779996672 | bytes 1360650880 | solution.py:405
  15.6 42.2 %all-gather.19 = bf16[16,1,128]{2,1,0:T(2,128)(2,1)S(1)} all-gather(bf16[1,1,128]{2,1,0:T(2,128)(2,1)S(1)} %bitcast.525), channel_id=1, replica_groups=mesh['dp'=4,'seq'=4,'tensor'=2] {'dp','seq'}, dimensions={0}, use_global_device_ids=true | all-gather | bytes 4352 | tf_op jit(solution)/shard_map/while/body/eval_jaxpr/all_gather | solution.py:192
  67.3 53.2 %all-gather.43.cloned.1.call-done = bf16[2048,1024]{0,1:T(8,128)(2,1)} async-done(((bf16[128,1024]{0,1:T(8,128)(2,1)}), bf16[2048,1024]{0,1:T(8,128)(2,1)}) %all-gather.43.cloned.1.call-update) | async-done | bytes 4194320 | tf_op jit(solution)/shard_map/while/body/eval_jaxpr/all_gather | solution.py:195
  125.6 108.7 %all-gather.45.cloned.1.call-done = bf16[2048,2048]{1,0:T(8,128)(2,1)} async-done(((bf16[128,2048]{1,0:T(8,128)(2,1)}), bf16[2048,2048]{1,0:T(8,128)(2,1)}) %all-gather.45.cloned.1.call-update) | async-done | bytes 8388624 | tf_op jit(solution)/shard_map/while/body/eval_jaxpr/all_gather | solution.py:196
  250.3 10.3 all-reduce.7
  262.2 62.1 %all-gather.39.cloned.1.call-done = bf16[2048,1024]{0,1:T(8,128)(2,1)} async-done(((bf16[128,1024]{0,1:T(8,128)(2,1)}), bf16[2048,1024]{0,1:T(8,128)(2,1)}) %all-gather.39.cloned.1.call-update) | async-done | bytes 4194320 | tf_op jit(solution)/shard_map/while/body/eval_jaxpr/all_gather | solution.py:194
  335.8 69.5 %all-gather.47.cloned.1.call-done = bf16[16,256,512]{2,1,0:T(8,128)(2,1)} async-done(((bf16[4,256,512]{2,1,0:T(8,128)(2,1)}), bf16[16,256,512]{2,1,0:T(8,128)(2,1)}) %all-gather.47.cloned.1.call-update) | async-done | bytes 4194320 | tf_op jit(solution)/shard_map/while/body/eval_jaxpr/all_gather | solution.py:22
  405.2 14.2 while.87
  420.0 11.9 bitcast_reduce_fusion.2
  441.0 78.3 %all-gather.49.cloned.1.call-done = bf16[2048,2048]{1,0:T(8,128)(2,1)} async-done(((bf16[128,2048]{1,0:T(8,128)(2,1)}), bf16[2048,2048]{1,0:T(8,128)(2,1)}) %all-gather.49.cloned.1.call-update) | async-done | bytes 8388624 | tf_op jit(solution)/shard_map/while/body/eval_jaxpr/all_gather | solution.py:197
  519.3 10.9 multiply_convert_fusion.21
  530.2 102.9 %all-gather.51.cloned.1.call-done = bf16[2048,2048]{1,0:T(8,128)(2,1)} async-done(((bf16[128,2048]{1,0:T(8,128)(2,1)}), bf16[2048,2048]{1,0:T(8,128)(2,1)}) %all-gather.51.cloned.1.call-update) | async-done | bytes 8388624 | tf_op jit(solution)/shard_map/while/body/eval_jaxpr/all_gather | solution.py:198
  633.1 9.9 fusion.325
  643.9 37.6 %all-gather.22 = bf16[16,1,128]{2,1,0:T(2,128)(2,1)S(1)} all-gather(bf16[1,1,128]{2,1,0:T(2,128)(2,1)S(1)} %bitcast.526), channel_id=1, replica_groups=mesh['dp'=4,'seq'=4,'tensor'=2] {'dp','seq'}, dimensions={0}, use_global_device_ids=true | all-gather | bytes 4352 | tf_op jit(solution)/shard_map/while/body/eval_jaxpr/all_gather | solution.py:193
  692.5 76.0 %all-gather.53.cloned.1.call-done = bf16[2048,2048]{1,0:T(8,128)(2,1)} async-done(((bf16[128,2048]{1,0:T(8,128)(2,1)}), bf16[2048,2048]{1,0:T(8,128)(2,1)}) %all-gather.53.cloned.1.call-update) | async-done | bytes 8388624 | tf_op jit(solution)/shard_map/while/body/eval_jaxpr/all_gather | solution.py:199
  768.5 10.8 all-gather.55.cloned.1.call-done
  779.4 18.4 multiply_convert_fusion.23
  797.7 112.7 %all-gather.57.cloned.1.call-done = bf16[2048,2048]{1,0:T(8,128)(2,1)} async-done(((bf16[128,2048]{1,0:T(8,128)(2,1)}), bf16[2048,2048]{1,0:T(8,128)(2,1)}) %all-gather.57.cloned.1.call-update) | async-done | bytes 8388624 | tf_op jit(solution)/shard_map/while/body/eval_jaxpr/all_gather | solution.py:288
  910.4 12.3 add_convert_fusion.8
  931.0 10.3 fusion.345
  960.8 12.7 select_add_fusion.26
  976.7 14.7 fusion.330
  1045.9 45.5 %all-gather.63.cloned.1.call-done = bf16[16,256,512]{2,1,0:T(8,128)(2,1)} async-done(((bf16[4,256,512]{2,1,0:T(8,128)(2,1)}), bf16[16,256,512]{2,1,0:T(8,128)(2,1)}) %all-gather.63.cloned.1.call-update) | async-done | bytes 4194320 | tf_op jit(solution)/shard_map/while/body/eval_jaxpr/all_gather | solution.py:22
  1091.3 16.7 while.88
  1128.5 10.8 fusion.342
  1171.5 37.7 %all-gather.19 = bf16[16,1,128]{2,1,0:T(2,128)(2,1)S(1)} all-gather(bf16[1,1,128]{2,1,0:T(2,128)(2,1)S(1)} %bitcast.525), channel_id=1, replica_groups=mesh['dp'=4,'seq'=4,'tensor'=2] {'dp','seq'}, dimensions={0}, use_global_device_ids=true | all-gather | bytes 4352 | tf_op jit(solution)/shard_map/while/body/eval_jaxpr/all_gather | solution.py:192
  1218.6 53.0 %all-gather.43.cloned.1.call-done = bf16[2048,1024]{0,1:T(8,128)(2,1)} async-done(((bf16[128,1024]{0,1:T(8,128)(2,1)}), bf16[2048,1024]{0,1:T(8,128)(2,1)}) %all-gather.43.cloned.1.call-update) | async-done | bytes 4194320 | tf_op jit(solution)/shard_map/while/body/eval_jaxpr/all_gather | solution.py:195
  1276.8 108.5 %all-gather.45.cloned.1.call-done = bf16[2048,2048]{1,0:T(8,128)(2,1)} async-done(((bf16[128,2048]{1,0:T(8,128)(2,1)}), bf16[2048,2048]{1,0:T(8,128)(2,1)}) %all-gather.45.cloned.1.call-update) | async-done | bytes 8388624 | tf_op jit(solution)/shard_map/while/body/eval_jaxpr/all_gather | solution.py:196
  1401.3 10.3 all-reduce.7
  1413.2 62.2 %all-gather.39.cloned.1.call-done = bf16[2048,1024]{0,1:T(8,128)(2,1)} async-done(((bf16[128,1024]{0,1:T(8,128)(2,1)}), bf16[2048,1024]{0,1:T(8,128)(2,1)}) %all-gather.39.cloned.1.call-update) | async-done | bytes 4194320 | tf_op jit(solution)/shard_map/while/body/eval_jaxpr/all_gather | solution.py:194
  1486.9 69.6 %all-gather.47.cloned.1.call-done = bf16[16,256,512]{2,1,0:T(8,128)(2,1)} async-done(((bf16[4,256,512]{2,1,0:T(8,128)(2,1)}), bf16[16,256,512]{2,1,0:T(8,128)(2,1)}) %all-gather.47.cloned.1.call-update) | async-done | bytes 4194320 | tf_op jit(solution)/shard_map/while/body/eval_jaxpr/all_gather | solution.py:22
  1556.6 14.2 while.87
  1571.3 11.9 bitcast_reduce_fusion.2
  1592.4 78.3 %all-gather.49.cloned.1.call-done = bf16[2048,2048]{1,0:T(8,128)(2,1)} async-done(((bf16[128,2048]{1,0:T(8,128)(2,1)}), bf16[2048,2048]{1,0:T(8,128)(2,1)}) %all-gather.49.cloned.1.call-update) | async-done | bytes 8388624 | tf_op jit(solution)/shard_map/while/body/eval_jaxpr/all_gather | solution.py:197
  1670.8 10.9 multiply_convert_fusion.21
  1681.7 102.8 %all-gather.51.cloned.1.call-done = bf16[2048,2048]{1,0:T(8,128)(2,1)} async-done(((bf16[128,2048]{1,0:T(8,128)(2,1)}), bf16[2048,2048]{1,0:T(8,128)(2,1)}) %all-gather.51.cloned.1.call-update) | async-done | bytes 8388624 | tf_op jit(solution)/shard_map/while/body/eval_jaxpr/all_gather | solution.py:198
  1784.5 9.9 fusion.325
  1795.0 37.6 %all-gather.22 = bf16[16,1,128]{2,1,0:T(2,128)(2,1)S(1)} all-gather(bf16[1,1,128]{2,1,0:T(2,128)(2,1)S(1)} %bitcast.526), channel_id=1, replica_groups=mesh['dp'=4,'seq'=4,'tensor'=2] {'dp','seq'}, dimensions={0}, use_global_device_ids=true | all-gather | bytes 4352 | tf_op jit(solution)/shard_map/while/body/eval_jaxpr/all_gather | solution.py:193
  1843.8 75.9 %all-gather.53.cloned.1.call-done = bf16[2048,2048]{1,0:T(8,128)(2,1)} async-done(((bf16[128,2048]{1,0:T(8,128)(2,1)}), bf16[2048,2048]{1,0:T(8,128)(2,1)}) %all-gather.53.cloned.1.call-update) | async-done | bytes 8388624 | tf_op jit(solution)/shard_map/while/body/eval_jaxpr/all_gather | solution.py:199
  1919.7 10.8 all-gather.55.cloned.1.call-done
  1930.5 18.4 multiply_convert_fusion.23
  1948.9 112.8 %all-gather.57.cloned.1.call-done = bf16[2048,2048]{1,0:T(8,128)(2,1)} async-done(((bf16[128,2048]{1,0:T(8,128)(2,1)}), bf16[2048,2048]{1,0:T(8,128)(2,1)}) %all-gather.57.cloned.1.call-update) | async-done | bytes 8388624 | tf_op jit(solution)/shard_map/while/body/eval_jaxpr/all_gather | solution.py:288
  2061.8 12.3 add_convert_fusion.8
  2082.3 10.3 fusion.345
  2096.4 12.5 select_add_fusion.25
  2116.3 18.6 select_add_fusion.26
  2138.0 14.7 fusion.330
  2189.8 12.3 select_add_fusion.24
  2202.1 12.0 select_add_fusion.23
  2214.1 36.9 %all-gather.63.cloned.1.call-done = bf16[16,256,512]{2,1,0:T(8,128)(2,1)} async-done(((bf16[4,256,512]{2,1,0:T(8,128)(2,1)}), bf16[16,256,512]{2,1,0:T(8,128)(2,1)}) %all-gather.63.cloned.1.call-update) | async-done | bytes 4194320 | tf_op jit(solution)/shard_map/while/body/eval_jaxpr/all_gather | solution.py:22
  2251.0 16.7 while.88
  2288.2 10.8 fusion.342
  2299.0 9.4 select_add_fusion.20
  2308.4 9.5 select_add_fusion.21
  2318.0 12.2 select_add_fusion.22
  2361.7 9.2 convert_element_type.554
  2380.2 9.2 convert_element_type.558
  2400.5 43.8 %all-reduce.5 = (bf16[2048]{0:T(1024)(128)(2,1)S(1)}, bf16[2048]{0:T(1024)(128)(2,1)S(1)}) all-reduce(bf16[2048]{0:T(1024)(128)(2,1)S(1)} %convert_element_type.544, bf16[2048]{0:T(1024)(128)(2,1)S(1)} %convert_element_type.546), channel_id=11, replica_groups=mesh['dp'=4,'seq'=4,'tensor'=2] {'dp','seq'}, use_global_device_ids=true, to_apply=%region_28.29.clone | all-reduce | flops 4096 | bytes 16384
  2449.1 92.6 %reduce-scatter.14.cloned.1.call-done = bf16[128,1024]{1,0:T(8,128)(2,1)} async-done(((bf16[2048,1024]{1,0:T(8,128)(2,1)}), bf16[128,1024]{1,0:T(8,128)(2,1)}) %reduce-scatter.14.cloned.1.call-update) | async-done | bytes 262160 | tf_op jit(solution)/shard_map/reduce_scatter | solution.py:418
  2543.5 179.2 %reduce-scatter.16.cloned.1.call-done = bf16[128,2048]{1,0:T(8,128)(2,1)} async-done(((bf16[2048,2048]{1,0:T(8,128)(2,1)}), bf16[128,2048]{1,0:T(8,128)(2,1)}) %reduce-scatter.16.cloned.1.call-update) | async-done | bytes 524304 | tf_op jit(solution)/shard_map/reduce_scatter | solution.py:421
  2724.8 180.0 %reduce-scatter.18.cloned.1.call-done = bf16[128,2048]{1,0:T(8,128)(2,1)} async-done(((bf16[2048,2048]{1,0:T(8,128)(2,1)}), bf16[128,2048]{1,0:T(8,128)(2,1)}) %reduce-scatter.18.cloned.1.call-update) | async-done | bytes 524304 | tf_op jit(solution)/shard_map/reduce_scatter | solution.py:424
  2906.9 180.0 %reduce-scatter.20.cloned.1.call-done = bf16[128,2048]{1,0:T(8,128)(2,1)} async-done(((bf16[2048,2048]{1,0:T(8,128)(2,1)}), bf16[128,2048]{1,0:T(8,128)(2,1)}) %reduce-scatter.20.cloned.1.call-update) | async-done | bytes 524304 | tf_op jit(solution)/shard_map/reduce_scatter | solution.py:427
  3089.0 180.0 %reduce-scatter.22.cloned.1.call-done = bf16[128,2048]{1,0:T(8,128)(2,1)} async-done(((bf16[2048,2048]{1,0:T(8,128)(2,1)}), bf16[128,2048]{1,0:T(8,128)(2,1)}) %reduce-scatter.22.cloned.1.call-update) | async-done | bytes 524304 | tf_op jit(solution)/shard_map/reduce_scatter | solution.py:430
  3271.1 179.8 %reduce-scatter.24.cloned.1.call-done = bf16[128,2048]{1,0:T(8,128)(2,1)} async-done(((bf16[2048,2048]{1,0:T(8,128)(2,1)}), bf16[128,2048]{1,0:T(8,128)(2,1)}) %reduce-scatter.24.cloned.1.call-update) | async-done | bytes 524304 | tf_op jit(solution)/shard_map/reduce_scatter | solution.py:433
  (667 shorter events, 476.3 us)
Async XLA Ops:
  11.1 46.8 %copy-start.78 = (s32[2,1,3]{2,1,0:T(1,128)S(1)}, s32[2,1,3]{2,1,0:T(1,128)}, u32[]{:S(2)}) copy-start(s32[2,1,3]{2,1,0:T(1,128)} %get-tuple-element.1578) | copy-start | bytes 76 | tf_op jit(solution)/shard_map/while
  11.1 51.8 %all-gather.41.cloned.1.call-start = ((), (), s32[]{:S(2)}) async-start(), calls=%async_computation.19 | async-start | bytes 3145728 | tf_op jit(solution)/shard_map/while/body/eval_jaxpr/all_gather | solution.py:217
  13.5 106.9 %all-gather.43.cloned.1.call-start = ((), (), s32[]{:S(2)}) async-start(), calls=%async_computation.20 | async-start | bytes 4456448 | tf_op jit(solution)/shard_map/while/body/eval_jaxpr/all_gather | solution.py:195
  14.3 220.0 %all-gather.45.cloned.1.call-start = ((), (), s32[]{:S(2)}) async-start(), calls=%async_computation.21 | async-start | bytes 8912896 | tf_op jit(solution)/shard_map/while/body/eval_jaxpr/all_gather | solution.py:196
  15.0 309.3 %all-gather.39.cloned.1.call-start = ((), (), s32[]{:S(2)}) async-start(), calls=%async_computation.18 | async-start | bytes 4456448 | tf_op jit(solution)/shard_map/while/body/eval_jaxpr/all_gather | solution.py:194
  15.6 389.6 %all-gather.47.cloned.1.call-start = ((), (), s32[]{:S(2)}) async-start(), calls=%async_computation.22 | async-start | bytes 5242880 | tf_op jit(solution)/shard_map/while/body/eval_jaxpr/all_gather | solution.py:22
  57.9 461.4 %copy-start.54 = (f32[16,1,128]{2,1,0:T(1,128)}, f32[16,1,128]{2,1,0:T(1,128)S(1)}, u32[]{:S(2)}) copy-start(f32[16,1,128]{2,1,0:T(1,128)S(1)} %convert_element_type.896) | copy-start | bytes 24580 | tf_op jit(solution)/shard_map/while
  60.1 269.5 %copy-start.76 = (f32[4]{0:T(128)}, f32[4]{0:T(128)S(1)}, u32[]{:S(2)}) copy-start(f32[4]{0:T(128)S(1)} %negate_log-plus-one_fusion.2) | copy-start | bytes 52 | tf_op jit(solution)/shard_map/while
  60.9 181.7 %copy-start.62 = (f32[512,4]{0,1:T(4,128)}, f32[512,4]{0,1:T(4,128)S(1)}, u32[]{:S(2)}) copy-start(f32[512,4]{0,1:T(4,128)S(1)} %get-tuple-element.1389) | copy-start | bytes 24580 | tf_op jit(solution)/shard_map/while
  60.9 359.1 %copy-start.64 = (f32[512,4]{0,1:T(4,128)}, f32[512,4]{0,1:T(4,128)S(1)}, u32[]{:S(2)}) copy-start(f32[512,4]{0,1:T(4,128)S(1)} %get-tuple-element.1388) | copy-start | bytes 24580 | tf_op jit(solution)/shard_map/while
  62.8 62.3 %copy-start.41 = (f32[512,128]{0,1:T(8,128)}, f32[512,128]{0,1:T(8,128)S(1)}, u32[]{:S(2)}) copy-start(f32[512,128]{0,1:T(8,128)S(1)} %get-tuple-element.1380) | copy-start | bytes 786436 | tf_op jit(solution)/shard_map/while
  62.8 57.6 %copy-start = (bf16[1,1,512,2048]{3,2,1,0:T(8,128)(2,1)S(1)}, bf16[1,1,512,2048]{3,2,1,0:T(8,128)(2,1)}, u32[]{:S(2)}) copy-start(bf16[1,1,512,2048]{3,2,1,0:T(8,128)(2,1)} %all-gather.41.cloned.1.call-done) | copy-start | bytes 6291460 | tf_op jit(solution)/shard_map/while
  125.6 117.0 %copy-start.30 = (bf16[512,4,128]{0,2,1:T(8,128)(2,1)}, bf16[512,4,128]{0,2,1:T(8,128)(2,1)S(1)}, u32[]{:S(2)}) copy-start(bf16[512,4,128]{0,2,1:T(8,128)(2,1)S(1)} %get-tuple-element.1382) | copy-start | bytes 1572868 | tf_op jit(solution)/shard_map/while
  125.6 117.0 %copy-start.34 = (bf16[512,4,128]{0,2,1:T(8,128)(2,1)}, bf16[512,4,128]{0,2,1:T(8,128)(2,1)S(1)}, u32[]{:S(2)}) copy-start(bf16[512,4,128]{0,2,1:T(8,128)(2,1)S(1)} %get-tuple-element.1381) | copy-start | bytes 1572868 | tf_op jit(solution)/shard_map/while
  246.7 272.6 %all-gather.49.cloned.1.call-start = ((), (), s32[]{:S(2)}) async-start(), calls=%async_computation.23 | async-start | bytes 8912896 | tf_op jit(solution)/shard_map/while/body/eval_jaxpr/all_gather | solution.py:197
  247.3 385.8 %all-gather.51.cloned.1.call-start = ((), (), s32[]{:S(2)}) async-start(), calls=%async_computation.24 | async-start | bytes 8912896 | tf_op jit(solution)/shard_map/while/body/eval_jaxpr/all_gather | solution.py:198
  248.1 436.0 %reduce-scatter.26.cloned.1.call-start = ((), (), s32[]{:S(2)}) async-start(), calls=%async_computation.26 | async-start | bytes 3145728 | tf_op jit(solution)/shard_map/while/body/eval_jaxpr/reduce_scatter | solution.py:262
  262.2 67.4 %copy-start.60 = (pred[512,512]{1,0:T(8,128)(4,1)}, pred[512,512]{1,0:T(8,128)(4,1)S(1)}, u32[]{:S(2)}) copy-start(pred[512,512]{1,0:T(8,128)(4,1)S(1)} %fusion.315) | copy-start | bytes 786436 | tf_op jit(solution)/shard_map/while
  329.5 90.4 %copy-start.24 = (bf16[512,4,128]{0,2,1:T(8,128)(2,1)}, bf16[512,4,128]{0,2,1:T(8,128)(2,1)S(1)}, u32[]{:S(2)}) copy-start(bf16[512,4,128]{0,2,1:T(8,128)(2,1)S(1)} %get-tuple-element.1378) | copy-start | bytes 1572868 | tf_op jit(solution)/shard_map/while
  329.6 90.4 %copy-start.27 = (bf16[512,4,128]{0,2,1:T(8,128)(2,1)}, bf16[512,4,128]{0,2,1:T(8,128)(2,1)S(1)}, u32[]{:S(2)}) copy-start(bf16[512,4,128]{0,2,1:T(8,128)(2,1)S(1)} %get-tuple-element.1377) | copy-start | bytes 1572868 | tf_op jit(solution)/shard_map/while
  643.1 125.5 %all-gather.53.cloned.1.call-start = ((), (), s32[]{:S(2)}) async-start(), calls=%async_computation.25 | async-start | bytes 8912896 | tf_op jit(solution)/shard_map/while/body/eval_jaxpr/all_gather | solution.py:199
  643.8 135.6 %all-gather.55.cloned.1.call-start = ((), (), s32[]{:S(2)}) async-start(), calls=%async_computation.27 | async-start | bytes 3145728 | tf_op jit(solution)/shard_map/while/body/eval_jaxpr/all_gather | solution.py:267
  689.5 108.3 %all-gather.59.cloned.1.call-start = ((), (), s32[]{:S(2)}) async-start(), calls=%async_computation.29 | async-start | bytes 3145728 | tf_op jit(solution)/shard_map/while/body/eval_jaxpr/all_gather | solution.py:290
  691.9 218.6 %all-gather.57.cloned.1.call-start = ((), (), s32[]{:S(2)}) async-start(), calls=%async_computation.28 | async-start | bytes 8912896 | tf_op jit(solution)/shard_map/while/body/eval_jaxpr/all_gather | solution.py:288
  692.4 260.9 %reduce-scatter.28.cloned.1.call-start = ((), (), s32[]{:S(2)}) async-start(), calls=%async_computation.30 | async-start | bytes 3145728 | tf_op jit(solution)/shard_map/while/body/eval_jaxpr/reduce_scatter | solution.py:298
  930.2 43.3 %reduce-scatter.32.cloned.1.call-start = ((), (), s32[]{:S(2)}) async-start(), calls=%async_computation.34 | async-start | bytes 3145728 | tf_op jit(solution)/shard_map/while/body/eval_jaxpr/reduce_scatter | solution.py:275
  941.3 35.4 %all-gather.61.cloned.1.call-start = ((), (), s32[]{:S(2)}) async-start(), calls=%async_computation.31 | async-start | bytes 3145728 | tf_op jit(solution)/shard_map/while/body/eval_jaxpr/all_gather | solution.py:305
  960.6 130.7 %all-gather.63.cloned.1.call-start = ((), (), s32[]{:S(2)}) async-start(), calls=%async_computation.32 | async-start | bytes 5242880 | tf_op jit(solution)/shard_map/while/body/eval_jaxpr/all_gather | solution.py:22
  1011.7 148.7 %reduce-scatter.30.cloned.1.call-start = ((), (), s32[]{:S(2)}) async-start(), calls=%async_computation.33 | async-start | bytes 3145728 | tf_op jit(solution)/shard_map/while/body/eval_jaxpr/reduce_scatter | solution.py:364
  1167.0 47.3 %all-gather.41.cloned.1.call-start = ((), (), s32[]{:S(2)}) async-start(), calls=%async_computation.19 | async-start | bytes 3145728 | tf_op jit(solution)/shard_map/while/body/eval_jaxpr/all_gather | solution.py:217
  1169.4 102.2 %all-gather.43.cloned.1.call-start = ((), (), s32[]{:S(2)}) async-start(), calls=%async_computation.20 | async-start | bytes 4456448 | tf_op jit(solution)/shard_map/while/body/eval_jaxpr/all_gather | solution.py:195
  1170.1 215.2 %all-gather.45.cloned.1.call-start = ((), (), s32[]{:S(2)}) async-start(), calls=%async_computation.21 | async-start | bytes 8912896 | tf_op jit(solution)/shard_map/while/body/eval_jaxpr/all_gather | solution.py:196
  1170.7 304.7 %all-gather.39.cloned.1.call-start = ((), (), s32[]{:S(2)}) async-start(), calls=%async_computation.18 | async-start | bytes 4456448 | tf_op jit(solution)/shard_map/while/body/eval_jaxpr/all_gather | solution.py:194
  1171.5 385.1 %all-gather.47.cloned.1.call-start = ((), (), s32[]{:S(2)}) async-start(), calls=%async_computation.22 | async-start | bytes 5242880 | tf_op jit(solution)/shard_map/while/body/eval_jaxpr/all_gather | solution.py:22
  1209.2 461.5 %copy-start.54 = (f32[16,1,128]{2,1,0:T(1,128)}, f32[16,1,128]{2,1,0:T(1,128)S(1)}, u32[]{:S(2)}) copy-start(f32[16,1,128]{2,1,0:T(1,128)S(1)} %convert_element_type.896) | copy-start | bytes 24580 | tf_op jit(solution)/shard_map/while
  1211.5 269.3 %copy-start.76 = (f32[4]{0:T(128)}, f32[4]{0:T(128)S(1)}, u32[]{:S(2)}) copy-start(f32[4]{0:T(128)S(1)} %negate_log-plus-one_fusion.2) | copy-start | bytes 52 | tf_op jit(solution)/shard_map/while
  1212.3 181.3 %copy-start.62 = (f32[512,4]{0,1:T(4,128)}, f32[512,4]{0,1:T(4,128)S(1)}, u32[]{:S(2)}) copy-start(f32[512,4]{0,1:T(4,128)S(1)} %get-tuple-element.1389) | copy-start | bytes 24580 | tf_op jit(solution)/shard_map/while
  1212.3 359.1 %copy-start.64 = (f32[512,4]{0,1:T(4,128)}, f32[512,4]{0,1:T(4,128)S(1)}, u32[]{:S(2)}) copy-start(f32[512,4]{0,1:T(4,128)S(1)} %get-tuple-element.1388) | copy-start | bytes 24580 | tf_op jit(solution)/shard_map/while
  1214.2 62.1 %copy-start.41 = (f32[512,128]{0,1:T(8,128)}, f32[512,128]{0,1:T(8,128)S(1)}, u32[]{:S(2)}) copy-start(f32[512,128]{0,1:T(8,128)S(1)} %get-tuple-element.1380) | copy-start | bytes 786436 | tf_op jit(solution)/shard_map/while
  1214.2 57.4 %copy-start = (bf16[1,1,512,2048]{3,2,1,0:T(8,128)(2,1)S(1)}, bf16[1,1,512,2048]{3,2,1,0:T(8,128)(2,1)}, u32[]{:S(2)}) copy-start(bf16[1,1,512,2048]{3,2,1,0:T(8,128)(2,1)} %all-gather.41.cloned.1.call-done) | copy-start | bytes 6291460 | tf_op jit(solution)/shard_map/while
  1276.8 116.8 %copy-start.30 = (bf16[512,4,128]{0,2,1:T(8,128)(2,1)}, bf16[512,4,128]{0,2,1:T(8,128)(2,1)S(1)}, u32[]{:S(2)}) copy-start(bf16[512,4,128]{0,2,1:T(8,128)(2,1)S(1)} %get-tuple-element.1382) | copy-start | bytes 1572868 | tf_op jit(solution)/shard_map/while
  1276.8 116.8 %copy-start.34 = (bf16[512,4,128]{0,2,1:T(8,128)(2,1)}, bf16[512,4,128]{0,2,1:T(8,128)(2,1)S(1)}, u32[]{:S(2)}) copy-start(bf16[512,4,128]{0,2,1:T(8,128)(2,1)S(1)} %get-tuple-element.1381) | copy-start | bytes 1572868 | tf_op jit(solution)/shard_map/while
  1397.8 273.0 %all-gather.49.cloned.1.call-start = ((), (), s32[]{:S(2)}) async-start(), calls=%async_computation.23 | async-start | bytes 8912896 | tf_op jit(solution)/shard_map/while/body/eval_jaxpr/all_gather | solution.py:197
  1398.5 386.0 %all-gather.51.cloned.1.call-start = ((), (), s32[]{:S(2)}) async-start(), calls=%async_computation.24 | async-start | bytes 8912896 | tf_op jit(solution)/shard_map/while/body/eval_jaxpr/all_gather | solution.py:198
  1399.1 436.2 %reduce-scatter.26.cloned.1.call-start = ((), (), s32[]{:S(2)}) async-start(), calls=%async_computation.26 | async-start | bytes 3145728 | tf_op jit(solution)/shard_map/while/body/eval_jaxpr/reduce_scatter | solution.py:262
  1413.2 67.6 %copy-start.60 = (pred[512,512]{1,0:T(8,128)(4,1)}, pred[512,512]{1,0:T(8,128)(4,1)S(1)}, u32[]{:S(2)}) copy-start(pred[512,512]{1,0:T(8,128)(4,1)S(1)} %fusion.315) | copy-start | bytes 786436 | tf_op jit(solution)/shard_map/while
  1480.7 90.6 %copy-start.24 = (bf16[512,4,128]{0,2,1:T(8,128)(2,1)}, bf16[512,4,128]{0,2,1:T(8,128)(2,1)S(1)}, u32[]{:S(2)}) copy-start(bf16[512,4,128]{0,2,1:T(8,128)(2,1)S(1)} %get-tuple-element.1378) | copy-start | bytes 1572868 | tf_op jit(solution)/shard_map/while
  1480.7 90.6 %copy-start.27 = (bf16[512,4,128]{0,2,1:T(8,128)(2,1)}, bf16[512,4,128]{0,2,1:T(8,128)(2,1)S(1)}, u32[]{:S(2)}) copy-start(bf16[512,4,128]{0,2,1:T(8,128)(2,1)S(1)} %get-tuple-element.1377) | copy-start | bytes 1572868 | tf_op jit(solution)/shard_map/while
  1794.4 125.3 %all-gather.53.cloned.1.call-start = ((), (), s32[]{:S(2)}) async-start(), calls=%async_computation.25 | async-start | bytes 8912896 | tf_op jit(solution)/shard_map/while/body/eval_jaxpr/all_gather | solution.py:199
  1795.0 135.6 %all-gather.55.cloned.1.call-start = ((), (), s32[]{:S(2)}) async-start(), calls=%async_computation.27 | async-start | bytes 3145728 | tf_op jit(solution)/shard_map/while/body/eval_jaxpr/all_gather | solution.py:267
  1840.7 108.3 %all-gather.59.cloned.1.call-start = ((), (), s32[]{:S(2)}) async-start(), calls=%async_computation.29 | async-start | bytes 3145728 | tf_op jit(solution)/shard_map/while/body/eval_jaxpr/all_gather | solution.py:290
  1843.0 218.7 %all-gather.57.cloned.1.call-start = ((), (), s32[]{:S(2)}) async-start(), calls=%async_computation.28 | async-start | bytes 8912896 | tf_op jit(solution)/shard_map/while/body/eval_jaxpr/all_gather | solution.py:288
  1843.8 265.1 %reduce-scatter.28.cloned.1.call-start = ((), (), s32[]{:S(2)}) async-start(), calls=%async_computation.30 | async-start | bytes 3145728 | tf_op jit(solution)/shard_map/while/body/eval_jaxpr/reduce_scatter | solution.py:298
  2081.6 53.3 %reduce-scatter.32.cloned.1.call-start = ((), (), s32[]{:S(2)}) async-start(), calls=%async_computation.34 | async-start | bytes 3145728 | tf_op jit(solution)/shard_map/while/body/eval_jaxpr/reduce_scatter | solution.py:275
  2092.6 45.5 %all-gather.61.cloned.1.call-start = ((), (), s32[]{:S(2)}) async-start(), calls=%async_computation.31 | async-start | bytes 3145728 | tf_op jit(solution)/shard_map/while/body/eval_jaxpr/all_gather | solution.py:305
  2116.1 134.9 %all-gather.63.cloned.1.call-start = ((), (), s32[]{:S(2)}) async-start(), calls=%async_computation.32 | async-start | bytes 5242880 | tf_op jit(solution)/shard_map/while/body/eval_jaxpr/all_gather | solution.py:22
  2173.1 157.1 %reduce-scatter.30.cloned.1.call-start = ((), (), s32[]{:S(2)}) async-start(), calls=%async_computation.33 | async-start | bytes 3145728 | tf_op jit(solution)/shard_map/while/body/eval_jaxpr/reduce_scatter | solution.py:364
  2340.0 107.4 %reduce-scatter.12.cloned.1.call-start = ((), (), s32[]{:S(2)}) async-start(), calls=%async_computation.11 | async-start | bytes 4456448 | tf_op jit(solution)/shard_map/reduce_scatter | solution.py:415
  2346.3 195.5 %reduce-scatter.14.cloned.1.call-start = ((), (), s32[]{:S(2)}) async-start(), calls=%async_computation.12 | async-start | bytes 4456448 | tf_op jit(solution)/shard_map/reduce_scatter | solution.py:418
  2352.4 370.3 %reduce-scatter.16.cloned.1.call-start = ((), (), s32[]{:S(2)}) async-start(), calls=%async_computation.13 | async-start | bytes 8912896 | tf_op jit(solution)/shard_map/reduce_scatter | solution.py:421
  2361.6 543.2 %reduce-scatter.18.cloned.1.call-start = ((), (), s32[]{:S(2)}) async-start(), calls=%async_computation.14 | async-start | bytes 8912896 | tf_op jit(solution)/shard_map/reduce_scatter | solution.py:424
  2370.9 716.0 %reduce-scatter.20.cloned.1.call-start = ((), (), s32[]{:S(2)}) async-start(), calls=%async_computation.15 | async-start | bytes 8912896 | tf_op jit(solution)/shard_map/reduce_scatter | solution.py:427
  2380.1 888.8 %reduce-scatter.22.cloned.1.call-start = ((), (), s32[]{:S(2)}) async-start(), calls=%async_computation.16 | async-start | bytes 8912896 | tf_op jit(solution)/shard_map/reduce_scatter | solution.py:430
  2389.4 1061.5 %reduce-scatter.24.cloned.1.call-start = ((), (), s32[]{:S(2)}) async-start(), calls=%async_computation.17 | async-start | bytes 8912896 | tf_op jit(solution)/shard_map/reduce_scatter | solution.py:433
  (142 other events, 756.4 us)
Sparse Core Ops, SparseCore 0:
  14.0 13.2 all-gather.40
  30.0 90.3 all-gather.42
  123.2 111.0 all-gather.44
  236.8 87.3 all-gather.38
  326.2 78.9 all-gather.46
  407.9 111.3 all-gather.48
  522.1 111.0 all-gather.50
  643.2 7.7 reduce-scatter.25
  654.2 114.2 all-gather.52
  770.6 8.7 all-gather.54
  781.6 11.7 all-gather.58
  796.4 113.9 all-gather.56
  930.4 7.7 reduce-scatter.27
  941.4 9.6 reduce-scatter.31
  960.7 8.8 all-gather.60
  1011.8 79.4 all-gather.62
  1139.5 8.1 reduce-scatter.29
  1169.6 8.8 all-gather.40
  1181.2 90.3 all-gather.42
  1274.3 111.0 all-gather.44
  1388.0 87.3 all-gather.38
  1477.6 78.9 all-gather.46
  1559.4 111.3 all-gather.48
  1673.4 111.0 all-gather.50
  1794.5 7.7 reduce-scatter.25
  1805.4 114.2 all-gather.52
  1921.7 8.7 all-gather.54
  1932.7 11.7 all-gather.58
  1947.7 113.9 all-gather.56
  2081.7 7.7 reduce-scatter.27
  2092.7 9.8 reduce-scatter.31
  2116.2 7.9 all-gather.60
  2173.2 77.7 all-gather.62
  2299.1 8.1 reduce-scatter.29
Sparse Core Ops, SparseCore 1:
  2346.3 97.8 reduce-scatter.11
  2446.4 95.3 reduce-scatter.13
  2543.9 178.7 reduce-scatter.15
  2725.0 179.7 reduce-scatter.17
  2907.1 179.7 reduce-scatter.19
  3089.2 179.7 reduce-scatter.21
  3271.1 179.7 reduce-scatter.23
where the time goes:
time: 3460 us
  waiting for transfers between devices  2430 us (70%)
  matrix products  489 us (14%)
  other arithmetic  227 us (7%)
  blocking collectives  223 us (6%)
  local copies, waits for them, and re-layouts  61.7 us (2%)
    all_gather x2, waiting for transfers between devices, micro_step(): lax.all_gather(down_weight, ('dp', 'seq'), axis=0, tiled=True)  225 us
    all_gather x4, waiting for transfers between devices, entering(): lax.all_gather(part.astype(kind), axis)  221 us
    all_gather x2, waiting for transfers between devices, micro_step(): lax.all_gather(value_weight, ('dp', 'seq'), axis=0, tiled=True)  217 us
    all_gather x2, waiting for transfers between devices, micro_step(): lax.all_gather(out_weight, ('dp', 'seq'), axis=0, tiled=True)  206 us
    reduce_scatter x1, waiting for transfers between devices, body(): lax.psum_scatter(totals[6].astype(jnp.bfloat16), ('dp', 'seq'), scatter_d...  180 us
    reduce_scatter x1, waiting for transfers between devices, body(): lax.psum_scatter(totals[7].astype(jnp.bfloat16), ('dp', 'seq'), scatter_d...  180 us
    reduce_scatter x1, waiting for transfers between devices, body(): lax.psum_scatter(totals[5].astype(jnp.bfloat16), ('dp', 'seq'), scatter_d...  180 us
    reduce_scatter x1, waiting for transfers between devices, body(): lax.psum_scatter(totals[8].astype(jnp.bfloat16), ('dp', 'seq'), scatter_d...  180 us
  transfers between devices with their start and end apart: 41, of which 26 were waited for; matrix products, arithmetic and copies ran while one was open for 15% of the time, Pallas kernels for 0%

commit v1 on v0

v1 whole, which is shorter than its diff:
```python
import math

import jax
import jax.numpy as jnp
from jax import lax
from jax.experimental import pallas as pl
from jax.experimental.pallas import tpu as pltpu
from jax.sharding import PartitionSpec as P

QK = 256
HV = 512
EPSILON = 1e-05
GROUP_EPSILON = 1.0
XPOS_BASE = 512.0


def norm_rows(values, offset):
    centre = values - jnp.mean(values, axis=-1, keepdims=True)
    inv_scale = lax.rsqrt(jnp.mean(centre * centre, axis=-1, keepdims=True) + offset)
    return (centre * inv_scale, inv_scale)


def norm_back(grad_terms, normed, inv_scale):
    grad_mean = jnp.mean(grad_terms, axis=-1, keepdims=True)
    cross_mean = jnp.mean(grad_terms * normed, axis=-1, keepdims=True)
    return inv_scale * (grad_terms - grad_mean - normed * cross_mean)


def layout(lengths_row, first_place, number):
    count = lengths_row.shape[0]
    before = jnp.arange(count)[None, :] < jnp.arange(count)[:, None]
    starts = jnp.sum(jnp.where(before, lengths_row[None, :], 0), axis=1, dtype=jnp.int32)
    places = first_place + jnp.arange(number, dtype=jnp.int32)
    is_after = places[:, None] >= starts[None, :]
    documents = jnp.sum(is_after.astype(jnp.int32), axis=1, dtype=jnp.int32) - 1
    begins = jnp.max(jnp.where(is_after, starts[None, :], 0), axis=1)
    return (documents, places - begins)


def rotation(places, sign_exp, head_width):
    half_width = head_width // 2
    pair_index = jnp.arange(half_width, dtype=jnp.float32)
    frequency = jnp.exp(pair_index * (-math.log(10000.0) / half_width))
    zeta_base = (2.0 * pair_index + 0.4 * head_width) / (1.4 * head_width)
    place_f = places.astype(jnp.float32)[:, None]
    angle_t = place_f * frequency[None, :]
    factor = jnp.exp(place_f * (sign_exp / XPOS_BASE) * jnp.log(zeta_base)[None, :])
    return (jnp.cos(angle_t) * factor, jnp.sin(angle_t) * factor)


def rotate(values, cos_table, sin_table):
    half_width = values.shape[-1] // 2
    first_half = values[..., :half_width]
    second_half = values[..., half_width:]
    return jnp.concatenate(
        [
            first_half * cos_table - second_half * sin_table,
            first_half * sin_table + second_half * cos_table,
        ],
        axis=-1,
    )


def rotate_back(grad_terms, cos_table, sin_table):
    return rotate(grad_terms, cos_table, -sin_table)


def decay_parts(documents, previous, log_gamma):
    tokens_n = documents.shape[0]
    steps_f = jnp.arange(tokens_n, dtype=jnp.float32)
    distance = steps_f[:, None] - steps_f[None, :]
    same_doc = (documents[:, None] == documents[None, :]) & (distance >= 0.0)
    inner_decay = jnp.where(
        same_doc[None], jnp.exp(jnp.maximum(distance, 0.0)[None] * log_gamma[:, None, None]), 0.0
    )
    carried = jnp.where(
        (documents == previous)[None, :],
        jnp.exp((steps_f + 1.0)[None, :] * log_gamma[:, None]),
        0.0,
    )
    last_doc = documents[tokens_n - 1]
    leaving = jnp.where(
        (documents == last_doc)[None, :],
        jnp.exp((tokens_n - 1.0 - steps_f)[None, :] * log_gamma[:, None]),
        0.0,
    )
    through = jnp.where(previous == last_doc, jnp.exp(tokens_n * log_gamma), 0.0)
    return (inner_decay, carried, leaving, through)


def gelu_exact(values):
    return jax.nn.gelu(values, approximate=False)


def matmul(left_side, right_side):
    return jnp.dot(left_side, right_side, preferred_element_type=jnp.float32)


def matmul_t(left_side, right_side):
    return lax.dot_general(
        left_side, right_side, (((1,), (1,)), ((), ())), preferred_element_type=jnp.float32
    )


def tmatmul(left_side, right_side):
    return lax.dot_general(
        left_side, right_side, (((0,), (0,)), ((), ())), preferred_element_type=jnp.float32
    )


def einsum(spec, left_side, right_side):
    return jnp.einsum(spec, left_side, right_side, preferred_element_type=jnp.float32)


def wide(values):
    return values.astype(jnp.float32)


def narrow(values):
    return values.astype(jnp.bfloat16)


class Plain:
    def __init__(self, tensor_heads):
        self.rows = 1
        self.heads = tensor_heads
        self.first_head = lax.axis_index("tensor") * tensor_heads

    def lengths(self, values):
        return values

    def gather_tokens(self, values):
        return lax.all_gather(values, "tensor", axis=0, tiled=True)

    def scatter_tokens(self, values):
        return wide(lax.psum_scatter(narrow(values), "tensor", scatter_dimension=0, tiled=True))

    def gather_weight(self, *shards):
        whole = [lax.all_gather(w, ("dp", "seq"), axis=0, tiled=True) for w in shards]
        return jnp.concatenate(whole, axis=1)

    def scatter_grad(self, grad, parts):
        grads = jnp.split(grad, parts, axis=1)
        return [
            wide(lax.psum_scatter(g, ("dp", "seq"), scatter_dimension=0, tiled=True))
            for g in grads
        ]


def chain(state, through, reverse):
    count, mine = lax.axis_size("seq"), lax.axis_index("seq")
    entering = jnp.zeros_like(state)
    for hop in range(1, count):
        leaving = state if hop == 1 else state + through[..., None, None] * entering
        pair = (count - hop, count - 1 - hop) if reverse else (hop - 1, hop)
        entering = entering + wide(lax.ppermute(narrow(leaving), "seq", [pair]))
    return entering


def plain_body(
    inputs,
    lengths,
    first_gain,
    second_gain,
    query_weight,
    key_weight,
    value_weight,
    gate_weight,
    out_weight,
    up_weight,
    down_weight,
    out_cotangent,
):
    micro = inputs.shape[0]
    shard_len = inputs.shape[2]
    block_len = shard_len * lax.axis_size("tensor")
    block_start = lax.axis_index("seq") * block_len
    tensor_heads = query_weight.shape[1] // QK
    plan = Plain(tensor_heads)
    rows, heads = plan.rows, plan.heads
    head_index = (plan.first_head + jnp.arange(heads, dtype=jnp.int32)).astype(jnp.float32)
    log_gamma = jnp.log1p(-jnp.exp2(-5.0 - head_index))
    half_width = QK // 2
    gain_one = wide(first_gain)[:, None]
    gain_two = wide(second_gain)[:, None]
    row_lengths = plan.lengths(lengths)

    def scaled(weight, gain):
        return narrow(wide(weight) * gain)

    weight_qk = plan.gather_weight(
        scaled(query_weight, gain_one), scaled(key_weight, gain_one)
    )
    weight_v = plan.gather_weight(scaled(value_weight, gain_one))
    weight_g = plan.gather_weight(scaled(gate_weight, gain_one))
    weight_o = plan.gather_weight(out_weight)
    weight_d = plan.gather_weight(down_weight)
    weight_u = plan.gather_weight(scaled(up_weight, gain_two))
    width_q = weight_qk.shape[1] // 2

    def row_plan(lengths_row):
        documents, places = layout(lengths_row, block_start, block_len)
        previous, unused = layout(lengths_row, block_start - 1, 1)
        return (documents, places, previous[0])

    def forward(inputs_mb, lengths_mb, cotangent_mb):
        tokens = rows * block_len
        documents, places, previous = jax.vmap(row_plan)(lengths_mb)
        flat_places = places.reshape(-1)
        tables = [
            table.reshape(rows, block_len, 1, half_width)
            for sign in (1.0, -1.0)
            for table in rotation(flat_places, sign, QK)
        ]
        decay = jax.vmap(decay_parts, in_axes=(0, 0, None))(documents, previous, log_gamma)
        inner_decay, carried, leaving, through = decay
        carried_t = jnp.swapaxes(carried, 1, 2)[..., None]
        leaving_t = jnp.swapaxes(leaving, 1, 2)[..., None]
        residual = wide(inputs_mb)
        normed_first, inv_first = norm_rows(residual, EPSILON)
        hidden_first = plan.gather_tokens(narrow(normed_first))
        qk_pre = matmul(hidden_first, weight_qk)
        query_pre = qk_pre[:, :width_q].reshape(rows, block_len, heads, QK)
        key_pre = qk_pre[:, width_q:].reshape(rows, block_len, heads, QK)
        value_rows = narrow(matmul(hidden_first, weight_v)).reshape(rows, block_len, heads, HV)
        gate_pre = matmul(hidden_first, weight_g)
        queries = narrow(rotate(query_pre, tables[0], tables[1]))
        key_rows = narrow(rotate(key_pre, tables[2], tables[3]))
        score_matrix = einsum("rnhd,rmhd->rhnm", queries, key_rows)
        score_weights = narrow(score_matrix * inner_decay)
        intra_part = einsum("rhnm,rmhe->rnhe", score_weights, value_rows)
        decayed_keys = narrow(wide(key_rows) * leaving_t)
        block_state = einsum("rmhd,rmhe->rhde", decayed_keys, value_rows)
        state_in = narrow(chain(block_state, through, False))
        queries_carried = narrow(wide(queries) * carried_t)
        retained = intra_part + einsum("rnhd,rhde->rnhe", queries_carried, state_in)
        grouped, inv_group = norm_rows(retained, GROUP_EPSILON)
        grouped_flat = grouped.reshape(tokens, -1)
        mixed_rows = narrow(jax.nn.silu(gate_pre) * grouped_flat)
        middle = residual + plan.scatter_tokens(matmul_t(mixed_rows, weight_o))
        normed_second, inv_second = norm_rows(middle, EPSILON)
        hidden_second = plan.gather_tokens(narrow(normed_second))
        up_pre = matmul(hidden_second, weight_u)
        activated = narrow(gelu_exact(up_pre))
        outputs = narrow(middle + plan.scatter_tokens(matmul_t(activated, weight_d)))

        grad_rows = plan.gather_tokens(cotangent_mb)
        grad_act = matmul(grad_rows, weight_d)
        grad_up_pre = narrow(jax.vjp(gelu_exact, up_pre)[1](grad_act)[0])
        back_second = plan.scatter_tokens(matmul_t(grad_up_pre, weight_u))
        grad_middle = wide(cotangent_mb) + norm_back(back_second, normed_second, inv_second)
        grad_attn = plan.gather_tokens(narrow(grad_middle))
        grad_mixed = matmul(grad_attn, weight_o)
        grad_gate_pre = narrow(
            jax.vjp(jax.nn.silu, gate_pre)[1](grad_mixed * grouped_flat)[0]
        )
        grad_grouped = (grad_mixed * jax.nn.silu(gate_pre)).reshape(
            rows, block_len, heads, HV
        )
        grad_retained = narrow(norm_back(grad_grouped, grouped, inv_group))
        grad_scores = einsum("rnhe,rmhe->rhnm", grad_retained, value_rows)
        score_grads = narrow(grad_scores * inner_decay)
        direct = einsum("rnhd,rnhe->rhde", queries_carried, grad_retained)
        state_out = narrow(chain(direct, through, True))
        grad_queries = einsum("rhnm,rmhd->rnhd", score_grads, key_rows) + carried_t * einsum(
            "rnhe,rhde->rnhd", grad_retained, state_in
        )
        grad_keys = einsum("rhnm,rnhd->rmhd", score_grads, queries) + leaving_t * einsum(
            "rmhe,rhde->rmhd", value_rows, state_out
        )
        grad_values = einsum("rhnm,rnhe->rmhe", score_weights, grad_retained) + einsum(
            "rmhd,rhde->rmhe", decayed_keys, state_out
        )
        grad_query_pre = narrow(rotate_back(grad_queries, tables[0], tables[1]))
        grad_key_pre = narrow(rotate_back(grad_keys, tables[2], tables[3]))
        grad_qk_pre = jnp.concatenate(
            [grad_query_pre.reshape(tokens, -1), grad_key_pre.reshape(tokens, -1)], axis=1
        )
        grad_value_pre = narrow(grad_values).reshape(tokens, -1)
        first_part = matmul_t(grad_qk_pre, weight_qk) + matmul_t(grad_value_pre, weight_v)
        first_part = first_part + matmul_t(grad_gate_pre, weight_g)
        back_first = plan.scatter_tokens(first_part)
        grad_inputs = narrow(grad_middle + norm_back(back_first, normed_first, inv_first))
        pieces = (
            (hidden_first, grad_qk_pre),
            (hidden_first, grad_value_pre),
            (hidden_first, grad_gate_pre),
            (grad_attn, mixed_rows),
            (hidden_second, grad_up_pre),
            (grad_rows, activated),
        )
        return (outputs, grad_inputs, pieces)

    done = [
        forward(inputs[i, :, :, :].reshape(shard_len * inputs.shape[1], -1), row_lengths[i],
                out_cotangent[i].reshape(shard_len * inputs.shape[1], -1))
        for i in range(micro)
    ]

    def weight_grad(k):
        total = sum(tmatmul(*done[i][2][k]) for i in range(micro))
        return narrow(total)

    grad_down = plan.scatter_grad(weight_grad(5), 1)[0]
    grad_up = plan.scatter_grad(weight_grad(4), 1)[0]
    grad_out = plan.scatter_grad(weight_grad(3), 1)[0]
    grad_gate = plan.scatter_grad(weight_grad(2), 1)[0]
    grad_value = plan.scatter_grad(weight_grad(1), 1)[0]
    grad_query, grad_key = plan.scatter_grad(weight_grad(0), 2)

    def along(weight, grad):
        return jnp.sum(wide(weight) * grad, axis=1)

    gain_sums = lax.psum(
        (
            along(query_weight, grad_query)
            + along(key_weight, grad_key)
            + along(value_weight, grad_value)
            + along(gate_weight, grad_gate),
            along(up_weight, grad_up),
        ),
        "tensor",
    )
    shape = inputs.shape
    return (
        jnp.stack([d[0] for d in done]).reshape(shape),
        jnp.stack([d[1] for d in done]).reshape(shape),
        gain_sums[0],
        gain_sums[1],
        grad_query * gain_one,
        grad_key * gain_one,
        grad_value * gain_one,
        grad_gate * gain_one,
        grad_out,
        grad_up * gain_two,
        grad_down,
    )


def swap(values, axis, bit):
    return lax.ppermute(values, axis, [(i, i ^ bit) for i in range(lax.axis_size(axis))])


def in_order(mine, other, index, axis):
    return jnp.where(
        index == 0, jnp.stack([mine, other], axis), jnp.stack([other, mine], axis)
    )


def pass_on(state, through, reverse, ties):
    count = lax.axis_size("seq")
    entering = []
    for hop in range(1, count):
        leaving = state
        if entering:
            before = tied(entering[-1], *ties.get(hop, ()))
            leaving = narrow(wide(state) + through[..., None, None] * wide(before))
        pair = (count - hop, count - 1 - hop) if reverse else (hop - 1, hop)
        entering.append(lax.ppermute(leaving, "seq", [pair]))
    return entering


def arrive(entering, *before):
    return sum(entering[:-1], tied(entering[-1], *before))


LANES = 128


def place_order(blocks):
    return [(up, block, side) for up in range(2) for block in range(blocks) for side in range(2)]


def group_of(place, upper, blocks):
    up, block, side = place
    start = (up ^ upper) if isinstance(upper, int) else lax.bitwise_xor(upper, up)
    return (start * 2 + side) * blocks + block


def load_groups(ref, upper, blocks):
    width = ref.shape[1] // (4 * blocks)
    parts = []
    for place in place_order(blocks):
        at = pl.multiple_of(group_of(place, upper, blocks) * width, LANES)
        parts.append(ref[:, pl.ds(at, width)])
    return jnp.concatenate(parts, axis=1)


def store_groups(ref, values, upper, blocks):
    width = ref.shape[1] // (4 * blocks)
    for i, place in enumerate(place_order(blocks)):
        at = pl.multiple_of(group_of(place, upper, blocks) * width, LANES)
        ref[:, pl.ds(at, width)] = values[:, i * width : (i + 1) * width]


VMEM_BYTES = 48 << 20


def tied(values, *others):
    return lax.optimization_barrier((values,) + others)[0]


def join(*columns):
    rows, widths = sum(p.shape[0] for p in columns[0]), [c[0].shape[1] for c in columns]
    parts = [p for c in columns for p in c]
    count = max(1, 4 // len(parts))

    def kernel(*refs):
        ins, (out, held, arrived, left) = refs[: len(parts)], refs[len(parts) :]
        pieces, number, across = [], 0, 0
        for width, column in zip(widths, columns):
            at = 0
            for _ in column:
                ref = ins[number]
                number += 1
                size = ref.shape[0] // count
                for k in range(count):
                    i, place = len(pieces), (pl.ds(at, size), pl.ds(across, width))
                    pieces.append(
                        (
                            pltpu.make_async_copy(
                                ref.at[pl.ds(k * size, size)], held.at[place], arrived.at[i]
                            ),
                            pltpu.make_async_copy(held.at[place], out.at[place], left.at[i]),
                        )
                    )
                    at += size
            across += width
        for copy_in, copy_out in pieces:
            copy_in.start()
        for copy_in, copy_out in pieces:
            copy_in.wait()
            copy_out.start()
        for copy_in, copy_out in pieces:
            copy_out.wait()

    number = len(parts) * count
    shape, dtype = (rows, sum(widths)), parts[0].dtype
    return pl.pallas_call(
        kernel,
        out_shape=jax.ShapeDtypeStruct(shape, dtype),
        in_specs=[pl.BlockSpec(memory_space=pl.ANY)] * len(parts),
        out_specs=pl.BlockSpec(memory_space=pl.ANY),
        scratch_shapes=[
            pltpu.VMEM(shape, dtype),
            pltpu.SemaphoreType.DMA((number,)),
            pltpu.SemaphoreType.DMA((number,)),
        ],
        compiler_params=pltpu.CompilerParams(vmem_limit_bytes=VMEM_BYTES),
    )(*parts)


def call(kernel, grid, in_specs, out_specs, out_shape, scalars, *operands, aliases=()):
    return pl.pallas_call(
        kernel,
        out_shape=out_shape,
        grid_spec=pltpu.PrefetchScalarGridSpec(
            num_scalar_prefetch=len(scalars),
            grid=grid,
            in_specs=in_specs,
            out_specs=out_specs,
        ),
        compiler_params=pltpu.CompilerParams(
            dimension_semantics=("arbitrary",) * len(grid), vmem_limit_bytes=VMEM_BYTES
        ),
        input_output_aliases={len(scalars) + i: o for i, o in aliases},
    )(*scalars, *operands)


ROWS_STEP = 64


def row_call(kernel, upper, tokens, operands, out_types, first=(), into=None):
    features = operands[0].shape[1]
    starts = list(first) + [0] * (len(operands) - len(first))

    def spec(start):
        return pl.BlockSpec(
            (ROWS_STEP, features), lambda i, *_: (i + start // ROWS_STEP, 0)
        )

    ins = [spec(start) for start in starts]
    outs = [spec(0)] * len(out_types)
    shapes = [jax.ShapeDtypeStruct((tokens, features), t) for t in out_types]
    aliases = ()
    if into is not None:
        whole, at, rows = into
        outs = [spec(at)]
        shapes = [jax.ShapeDtypeStruct((rows, features), out_types[0])]
        if whole is not None:
            plain = kernel

            def kernel(*refs):
                plain(*refs[:-2], refs[-1])

            aliases = ((len(operands), 0),)
            operands = tuple(operands) + (whole,)
            ins.append(pl.BlockSpec(memory_space=pl.ANY))
    return call(
        kernel, (tokens // ROWS_STEP,), ins, outs, shapes, [upper], *operands, aliases=aliases
    )


def enter_tokens(upper, blocks, tokens, start, inputs, cotangent):
    def kernel(up, x, c, normed, x_out, c_out):
        values = load_groups(x, up[0], blocks)
        x_out[...] = values
        c_out[...] = load_groups(c, up[0], blocks)
        normed[...] = narrow(norm_rows(wide(values), EPSILON)[0])

    return row_call(
        kernel, upper, tokens, (inputs, cotangent), (jnp.bfloat16,) * 3, (start, start)
    )


def total(parts):
    return sum(wide(p[...]) for p in parts)


def middle_tokens(upper, inputs, parts):
    def kernel(up, x, a, b, c, middle, normed):
        values = wide(x[...]) + total((a, b, c))
        middle[...] = values
        normed[...] = narrow(norm_rows(values, EPSILON)[0])

    return row_call(
        kernel, upper, inputs.shape[0], (inputs,) + parts, (jnp.float32, jnp.bfloat16)
    )


def output_tokens(upper, blocks, middle, parts, into):
    def kernel(up, m, a, b, c, out):
        store_groups(out, narrow(m[...] + total((a, b, c))), up[0], blocks)

    return row_call(
        kernel, upper, middle.shape[0], (middle,) + parts, (jnp.bfloat16,), into=into
    )[0]


def back_middle(upper, middle, cotangent, parts):
    def kernel(up, m, g, a, b, c, grad, grad_narrow):
        normed, inv = norm_rows(m[...], EPSILON)
        values = wide(g[...]) + norm_back(total((a, b, c)), normed, inv)
        grad[...] = values
        grad_narrow[...] = narrow(values)

    return row_call(
        kernel,
        upper,
        middle.shape[0],
        (middle, cotangent) + parts,
        (jnp.float32, jnp.bfloat16),
    )


def back_inputs(upper, blocks, inputs, grad_middle, parts, into):
    def kernel(up, x, g, a, b, c, out):
        normed, inv = norm_rows(wide(x[...]), EPSILON)
        values = g[...] + norm_back(total((a, b, c)), normed, inv)
        store_groups(out, narrow(values), up[0], blocks)

    return row_call(
        kernel,
        upper,
        inputs.shape[0],
        (inputs, grad_middle) + parts,
        (jnp.bfloat16,),
        into=into,
    )[0]


def dot(left, right, left_dim, right_dim):
    return lax.dot_general(
        left, right, (((left_dim,), (right_dim,)), ((), ())), preferred_element_type=jnp.float32
    )


class Retention:
    def __init__(self, plan, log_gamma, core, documents, previous, tables):
        rows, length = documents.shape
        self.rows, self.heads, self.length = rows, plan.heads, length
        self.q_wide, self.v_wide = plan.heads * QK, plan.heads * HV
        last = documents[:, -1]
        self.scalars = [
            jnp.concatenate([core[None], previous, last]).astype(jnp.int32),
            log_gamma,
        ]
        self.documents = [documents[:, :, None], documents[:, None, :]]
        self.tables = tables

    def token_spec(self, width):
        return pl.BlockSpec(
            (2, None, self.length // 2, width), lambda r, *_: (0, r, 0, 0)
        )

    def head_spec(self, *shape):
        return pl.BlockSpec(
            (None, self.heads) + shape, lambda r, *_: (r, 0) + (0,) * len(shape)
        )

    def row_spec(self, *shape):
        return pl.BlockSpec((None,) + shape, lambda r, *_: (r,) + (0,) * len(shape))

    def token_type(self, width, dtype=jnp.bfloat16):
        return jax.ShapeDtypeStruct((2, self.rows, self.length // 2, width), dtype)

    def head_type(self, *shape, dtype=jnp.bfloat16):
        return jax.ShapeDtypeStruct((self.rows, self.heads) + shape, dtype)

    def tokens(self, values):
        return values.reshape(2, self.rows, self.length // 2, -1)

    def document_specs(self):
        return [self.row_spec(self.length, 1), self.row_spec(1, self.length)]

    def table_specs(self):
        return [self.row_spec(self.length, QK // 2)] * 2

    def run(self, kernel, in_specs, out, operands):
        return call(
            kernel,
            (self.rows,),
            in_specs,
            [spec for spec, shape in out],
            [shape for spec, shape in out],
            self.scalars,
            *operands,
        )

    def load(self, ref, core, at, width):
        return jnp.concatenate(
            [ref[core, :, at : at + width], ref[1 - core, :, at : at + width]], axis=0
        )

    def store(self, ref, core, at, values):
        half, width = self.length // 2, values.shape[1]
        ref[core, :, at : at + width] = values[:half]
        ref[1 - core, :, at : at + width] = values[half:]

    def carried(self, numbers, log_gamma, docs, row, head):
        steps = wide(lax.broadcasted_iota(jnp.int32, (self.length, 1), 0))
        kept = jnp.exp((steps + 1.0) * log_gamma[head])
        return jnp.where(docs[...] == numbers[1 + row], kept, 0.0)

    def leaving(self, numbers, log_gamma, docs, row, head):
        steps = wide(lax.broadcasted_iota(jnp.int32, (self.length, 1), 0))
        kept = jnp.exp((self.length - 1.0 - steps) * log_gamma[head])
        return jnp.where(docs[...] == numbers[1 + self.rows + row], kept, 0.0)

    def inner(self, log_gamma, docs, docs_t, head):
        shape = (self.length, self.length)
        distance = wide(
            lax.broadcasted_iota(jnp.int32, shape, 0) - lax.broadcasted_iota(jnp.int32, shape, 1)
        )
        kept = jnp.exp(jnp.maximum(distance, 0.0) * log_gamma[head])
        return jnp.where((docs[...] == docs_t[...]) & (distance >= 0.0), kept, 0.0)

    def retained(self, numbers, log_gamma, docs, docs_t, row, head, query, key, value, state):
        inner = self.inner(log_gamma, docs, docs_t, head)
        weights = narrow(dot(query, key, 1, 1) * inner)
        carried = self.carried(numbers, log_gamma, docs, row, head)
        values = dot(weights, value, 1, 0) + carried * dot(query, state, 1, 0)
        grouped, inv = norm_rows(values, GROUP_EPSILON)
        return inner, weights, carried, grouped, inv

    def keys(self, kv_pre):
        def kernel(numbers, log_gamma, kv, docs, docs_t, cos, sin, keys, values, state):
            row, core = pl.program_id(0), numbers[0]
            for head in range(self.heads):
                key = self.load(kv, core, head * QK, QK)
                key = narrow(rotate(key, cos[...], sin[...]))
                value = narrow(self.load(kv, core, self.q_wide + head * HV, HV))
                leaving = self.leaving(numbers, log_gamma, docs, row, head)
                keys[head] = key
                values[head] = value
                state[head] = narrow(dot(narrow(wide(key) * leaving), value, 0, 0))

        n = self.length
        return self.run(
            kernel,
            [self.token_spec(self.q_wide + self.v_wide)] + self.document_specs() + self.table_specs(),
            [
                (self.head_spec(n, QK), self.head_type(n, QK)),
                (self.head_spec(n, HV), self.head_type(n, HV)),
                (self.head_spec(QK, HV), self.head_type(QK, HV)),
            ],
            [self.tokens(kv_pre)] + self.documents + self.tables[2:],
        )

    def mix(self, qg_pre, keys, values, state_in):
        def kernel(
            numbers, log_gamma, qg, key_ref, value_ref, state_ref, docs, docs_t, cos, sin,
            queries, mixed,
        ):
            row, core = pl.program_id(0), numbers[0]
            for head in range(self.heads):
                query = self.load(qg, core, head * QK, QK)
                query = narrow(rotate(query, cos[...], sin[...]))
                queries[head] = query
                grouped = self.retained(
                    numbers, log_gamma, docs, docs_t, row, head,
                    query, key_ref[head], value_ref[head], state_ref[head],
                )[3]
                gate = self.load(qg, core, self.q_wide + head * HV, HV)
                out = narrow(gate * jax.nn.sigmoid(gate) * grouped)
                self.store(mixed, core, head * HV, out)

        n = self.length
        queries, mixed = self.run(
            kernel,
            [
                self.token_spec(self.q_wide + self.v_wide),
                self.head_spec(n, QK),
                self.head_spec(n, HV),
                self.head_spec(QK, HV),
            ]
            + self.document_specs()
            + self.table_specs(),
            [
                (self.head_spec(n, QK), self.head_type(n, QK)),
                (self.token_spec(self.v_wide), self.token_type(self.v_wide)),
            ],
            [self.tokens(qg_pre), keys, values, state_in] + self.documents + self.tables[:2],
        )
        return queries, mixed.reshape(-1, self.v_wide)

    def back(self, qg_pre, grad_mixed, queries, keys, values, state_in):
        def kernel(
            numbers, log_gamma, qg, grad_ref, query_ref, key_ref, value_ref, state_ref,
            docs, docs_t, cos, sin, grad_qg, direct, grad_keys, grad_values,
        ):
            row, core = pl.program_id(0), numbers[0]
            for head in range(self.heads):
                query, key, value = query_ref[head], key_ref[head], value_ref[head]
                state = state_ref[head]
                inner, weights, carried, grouped, inv = self.retained(
                    numbers, log_gamma, docs, docs_t, row, head, query, key, value, state
                )
                gate = self.load(qg, core, self.q_wide + head * HV, HV)
                grad = self.load(grad_ref, core, head * HV, HV)
                sigmoid = jax.nn.sigmoid(gate)
                grad_gate = grad * grouped * (sigmoid * (1.0 + gate * (1.0 - sigmoid)))
                self.store(grad_qg, core, self.q_wide + head * HV, narrow(grad_gate))
                grad_retained = narrow(norm_back(grad * (gate * sigmoid), grouped, inv))
                score_grads = narrow(dot(grad_retained, value, 1, 1) * inner)
                direct[head] = narrow(
                    dot(narrow(wide(query) * carried), grad_retained, 0, 0)
                )
                grad_query = dot(score_grads, key, 1, 0) + carried * dot(
                    grad_retained, state, 1, 1
                )
                grad_query = rotate_back(grad_query, cos[...], sin[...])
                self.store(grad_qg, core, head * QK, narrow(grad_query))
                grad_keys[head] = dot(score_grads, query, 0, 0)
                grad_values[head] = dot(weights, grad_retained, 0, 0)

        n = self.length
        wide_all = self.q_wide + self.v_wide
        return self.run(
            kernel,
            [
                self.token_spec(wide_all),
                self.token_spec(self.v_wide),
                self.head_spec(n, QK),
                self.head_spec(n, QK),
                self.head_spec(n, HV),
                self.head_spec(QK, HV),
            ]
            + self.document_specs()
            + self.table_specs(),
            [
                (self.token_spec(wide_all), self.token_type(wide_all)),
                (self.head_spec(QK, HV), self.head_type(QK, HV)),
                (self.head_spec(n, QK), self.head_type(n, QK, dtype=jnp.float32)),
                (self.head_spec(n, HV), self.head_type(n, HV, dtype=jnp.float32)),
            ],
            [self.tokens(qg_pre), self.tokens(grad_mixed), queries, keys, values, state_in]
            + self.documents
            + self.tables[:2],
        )

    def back_keys(self, keys, values, state_out, grad_keys, grad_values):
        def kernel(
            numbers, log_gamma, key_ref, value_ref, state_ref, key_part, value_part,
            docs, docs_t, cos, sin, grad_kv,
        ):
            row, core = pl.program_id(0), numbers[0]
            for head in range(self.heads):
                leaving = self.leaving(numbers, log_gamma, docs, row, head)
                state = state_ref[head]
                grad_key = key_part[head] + leaving * dot(value_ref[head], state, 1, 1)
                grad_key = rotate_back(grad_key, cos[...], sin[...])
                self.store(grad_kv, core, head * QK, narrow(grad_key))
                grad_value = value_part[head] + leaving * dot(key_ref[head], state, 1, 0)
                self.store(grad_kv, core, self.q_wide + head * HV, narrow(grad_value))

        n = self.length
        wide_all = self.q_wide + self.v_wide
        return self.run(
            kernel,
            [
                self.head_spec(n, QK),
                self.head_spec(n, HV),
                self.head_spec(QK, HV),
                self.head_spec(n, QK),
                self.head_spec(n, HV),
            ]
            + self.document_specs()
            + self.table_specs(),
            [(self.token_spec(wide_all), self.token_type(wide_all))],
            [keys, values, state_out, grad_keys, grad_values] + self.documents + self.tables[2:],
        )[0].reshape(-1, wide_all)


class Paired:
    def __init__(self, tensor_heads):
        self.rows = 2
        self.heads = tensor_heads // 2
        self.side = lax.axis_index("dp") % 2
        self.upper = (lax.axis_index("dp") // 2).astype(jnp.int32)
        self.core = lax.axis_index("tensor")
        self.blocks = lax.axis_size("seq")
        self.first_head = self.core * tensor_heads + self.side * self.heads

    def gather_tokens(self, values, *before):
        across = tied(swap(values, "dp", 1), *before)
        own = (values, swap(values, "tensor", 1))
        return join((own[0], across, own[1], swap(across, "tensor", 1)))

    def scatter_tokens(self, product):
        away = swap(product(1), "tensor", 1)
        here = product(0)
        half = here.shape[0] // 2
        across = narrow(wide(here[half:]) + wide(away[half:]))
        return (here[:half], away[:half], swap(across, "dp", 1)), here, across

    def halves(self, shard, which):
        width = shard.shape[1] // 2
        return lax.dynamic_slice_in_dim(shard, which * width, width, 1)

    def swap_weight(self, shards, *before):
        here = jnp.concatenate([self.halves(w, self.side) for w in shards], axis=1)
        away = jnp.concatenate([self.halves(w, 1 - self.side) for w in shards], axis=1)
        return here, swap(tied(away, *before), "dp", 1)

    def pair_weight(self, here, across):
        return in_order(here, across, self.side, 0).reshape(-1, here.shape[1])

    def across_grad(self, away, here, *before):
        return narrow(wide(tied(here, *before)) + wide(swap(away, "dp", 2)))

    def scatter_grad(self, quads, widths):
        mine, other = [], []
        for quad in quads:
            two = lax.psum_scatter(quad, "seq", scatter_dimension=0, tiled=True)
            two = two.reshape(2, -1, quad.shape[1])
            away = lax.dynamic_index_in_dim(two, 1 - self.side, 0, False)
            mine.append(wide(lax.dynamic_index_in_dim(two, self.side, 0, False)))
            other.append(wide(swap(away, "dp", 1)))
        mine, other = jnp.concatenate(mine, axis=1), jnp.concatenate(other, axis=1)
        out, at = [], 0
        for width in widths:
            part = in_order(mine[:, at : at + width], other[:, at : at + width], self.side, 1)
            out.append(part.reshape(mine.shape[0], -1))
            at += width
        return out


def paired_body(
    inputs,
    lengths,
    first_gain,
    second_gain,
    query_weight,
    key_weight,
    value_weight,
    gate_weight,
    out_weight,
    up_weight,
    down_weight,
    out_cotangent,
):
    micro = inputs.shape[0]
    shard_len, features = inputs.shape[2:]
    block_len = shard_len * 2
    block_start = lax.axis_index("seq") * block_len
    plan = Paired(query_weight.shape[1] // QK)
    rows, heads, blocks = plan.rows, plan.heads, plan.blocks
    upper = plan.upper[None]
    head_index = (plan.first_head + jnp.arange(heads, dtype=jnp.int32)).astype(jnp.float32)
    log_gamma = jnp.log1p(-jnp.exp2(-5.0 - head_index))
    gain_one = wide(first_gain)[:, None]
    gain_two = wide(second_gain)[:, None]
    row_lengths = jnp.concatenate([lengths, swap(lengths, "dp", 1)], axis=1)

    def scaled(weight, gain):
        return narrow(wide(weight) * gain)

    flat = (micro * shard_len, features)
    units = [
        (scaled(key_weight, gain_one), scaled(value_weight, gain_one)),
        (scaled(query_weight, gain_one), scaled(gate_weight, gain_one)),
        (out_weight,),
        (down_weight,),
        (scaled(up_weight, gain_two),),
    ]
    here, across = plan.swap_weight(units[0])
    entered = [
        enter_tokens(
            upper,
            blocks,
            shard_len,
            i * shard_len,
            inputs.reshape(flat),
            out_cotangent.reshape(flat),
        )
        for i in range(micro)
    ]
    across = tied(across, *[e[0] for e in entered])

    def spread(two, *before):
        return lax.all_gather(tied(two, *before), "seq", axis=0, tiled=True)

    two_kv = plan.pair_weight(here, across)
    cut = two_kv.shape[1] // 2
    quads_kv = [spread(two_kv[:, :cut]), spread(two_kv[:, cut:])]
    hidden_first = [plan.gather_tokens(e[0]) for e in entered]
    two_qg = plan.pair_weight(*plan.swap_weight(units[1], two_kv))
    quad_qg = spread(two_qg)
    two_o = plan.pair_weight(*plan.swap_weight(units[2], two_qg))
    quad_o = spread(two_o)
    quads_kv[0] = quad_kv = tied(quads_kv[0], two_o)
    others_kv = [swap(quad_kv, "dp", 2)]
    others_kv.append(swap(tied(quads_kv[1], *others_kv), "dp", 2))
    two_d = plan.pair_weight(*plan.swap_weight(units[3], quad_kv))
    two_u = plan.pair_weight(*plan.swap_weight(units[4], two_d))
    grad_rows = [plan.gather_tokens(tied(e[2], quad_kv)) for e in entered]
    others_kv[1] = tied(others_kv[1], two_u)
    other_qg = swap(tied(quad_qg, others_kv[1]), "dp", 2)
    other_o = swap(tied(quad_o, other_qg), "dp", 2)
    weight_kv = join(*zip(quads_kv, others_kv))
    weight_qg = join((quad_qg, other_qg))
    weight_o = join((quad_o, other_o))

    def row_plan(lengths_row):
        documents, places = layout(lengths_row, block_start, block_len)
        previous, unused = layout(lengths_row, block_start - 1, 1)
        return (documents, places, previous[0])

    kernels, throughs = [], []
    for i in range(micro):
        documents, places, previous = jax.vmap(row_plan)(row_lengths[i])
        tables = [
            table.reshape(rows, block_len, QK // 2)
            for sign in (1.0, -1.0)
            for table in rotation(places.reshape(-1), sign, QK)
        ]
        kernels.append(Retention(plan, log_gamma, plan.core, documents, previous, tables))
        throughs.append(
            jnp.where(
                (previous == documents[:, -1])[:, None], jnp.exp(block_len * log_gamma)[None], 0.0
            )
        )

    each = range(micro)
    half = rows * shard_len

    def rows_of(values, away):
        return values[half:] if away else values[:half]

    def product_t(values, weight):
        return lambda away: narrow(matmul_t(rows_of(values, away), weight))

    def products(left, right, columns=slice(None)):
        middle = features // 2
        return [
            narrow(sum(tmatmul(left[i][:, rows_cut], right[i][:, columns]) for i in each))
            for rows_cut in (slice(middle, None), slice(None, middle))
        ]

    def first_product(i):
        def run(away):
            part = matmul_t(rows_of(first_qg[i], away), weight_qg)
            return narrow(part + matmul_t(rows_of(first_kv[i], away), weight_kv))

        return run

    kv_pre = [matmul(hidden_first[i], weight_kv) for i in each]
    kvs = [kernels[0].keys(kv_pre[0])]
    kv_pre[1] = tied(kv_pre[1], *grad_rows, kvs[0][2])
    kvs.append(kernels[1].keys(kv_pre[1]))
    qg_pre = [matmul(hidden_first[i], weight_qg) for i in each]
    ties = [{}, {2: (other_qg,), 3: (other_o,)}]
    states = [pass_on(kvs[i][2], throughs[i], False, ties[i]) for i in each]
    quad_d = spread(two_d)
    quad_u = spread(two_u, states[0][1])
    other_d = swap(tied(quad_d, other_o), "dp", 2)
    other_u = swap(tied(quad_u, other_d), "dp", 2)
    weight_d = join((quad_d, other_d))
    weight_u = join((quad_u, other_u))
    mixes, attn, state_in = [], [], []
    before = (*qg_pre, other_o)
    for i in each:
        state_in.append(arrive(states[i], *before))
        mixes.append(kernels[i].mix(qg_pre[i], kvs[i][0], kvs[i][1], state_in[i]))
        parts, here, across = plan.scatter_tokens(product_t(mixes[i][1], weight_o))
        attn.append(parts)
        before = (here,)
    residual = [e[1] for e in entered]
    grad_act = [matmul(grad_rows[i], weight_d) for i in each]
    residual[0] = tied(residual[0], other_d)
    residual[1] = tied(residual[1], *grad_act)
    middles = [middle_tokens(upper, residual[i], attn[i]) for i in each]
    hidden_second = [plan.gather_tokens(middles[i][1]) for i in each]
    up_pre = [matmul(hidden_second[i], weight_u) for i in each]
    activated = [narrow(gelu_exact(up_pre[i])) for i in each]
    grad_up_pre = [
        narrow(jax.vjp(gelu_exact, up_pre[i])[1](grad_act[i])[0]) for i in each
    ]
    second, before = [], ()
    for i in each:
        product = product_t(tied(grad_up_pre[i], *before), weight_u)
        parts, here, across = plan.scatter_tokens(product)
        second.append(parts)
        before = (across,)
    down_products = products(grad_rows, [tied(a, here) for a in activated])
    middles[0] = (tied(middles[0][0], across), middles[0][1])
    grad_middle = [
        back_middle(upper, middles[i][0], entered[i][2], second[i]) for i in each
    ]
    up_products = products(
        hidden_second, [tied(g, grad_middle[0][1]) for g in grad_up_pre]
    )
    quad_down = plan.across_grad(*down_products, grad_middle[0][1])
    quad_up = plan.across_grad(*up_products, grad_middle[1][1])
    grad_attn, backs = [], []
    before = ()
    for i in each:
        grad_attn.append(plan.gather_tokens(grad_middle[i][1], *before))
        source = tied(grad_attn[i], grad_middle[1][1])
        grad_mixed = tied(matmul(source, weight_o), *((quad_down, quad_up) if i else ()))
        kv = kvs[i]
        backs.append(
            kernels[i].back(qg_pre[i], grad_mixed, mixes[i][0], kv[0], kv[1], state_in[i])
        )
        before = (backs[i][1],)
    after_back = backs[-1][1]
    grad_qg_pre = [b[0].reshape(-1, b[0].shape[-1]) for b in backs]
    out_products = products(grad_attn, [tied(m[1], after_back) for m in mixes])
    qg_products = products(hidden_first, [tied(g, out_products[1]) for g in grad_qg_pre])
    late = [tied(a, after_back) for a in activated]
    ffn = [plan.scatter_tokens(product_t(late[i], weight_d)) for i in each]
    states = [
        pass_on(backs[i][1], throughs[i], True, {2: (out_products[i],), 3: (qg_products[i],)})
        for i in each
    ]
    state_out = [arrive(states[i], ffn[0][1], ffn[1][1]) for i in each]
    outputs = grad_inputs = None
    for i in each:
        into = (outputs, i * shard_len, flat[0])
        outputs = output_tokens(upper, blocks, middles[i][0], ffn[i][0], into)
    grad_kv_pre = [
        kernels[i].back_keys(kvs[i][0], kvs[i][1], state_out[i], backs[i][2], backs[i][3])
        for i in each
    ]
    cut = grad_kv_pre[0].shape[1] // 2
    kv_products = [
        products(hidden_first, grad_kv_pre, columns)
        for columns in (slice(None, cut), slice(cut, None))
    ]
    first_qg = [tied(g, kv_products[1][1]) for g in grad_qg_pre]
    first_kv = [tied(g, kv_products[1][1]) for g in grad_kv_pre]
    first = [plan.scatter_tokens(first_product(i))[0] for i in each]
    for i in each:
        into = (grad_inputs, i * shard_len, flat[0])
        grad_inputs = back_inputs(
            upper, blocks, entered[i][1], grad_middle[i][0], first[i], into
        )

    width_q, width_v = heads * QK, heads * HV
    width_f = up_weight.shape[1] // 2
    grad_down = plan.scatter_grad([quad_down], [width_f])[0]
    grad_up = plan.scatter_grad([quad_up], [width_f])[0]
    quad_out = plan.across_grad(*out_products, state_out[0])
    grad_out = plan.scatter_grad([quad_out], [width_v])[0]
    quad_qg = plan.across_grad(*qg_products, *state_out)
    grad_query, grad_gate = plan.scatter_grad([quad_qg], [width_q, width_v])
    quads_kv = [plan.across_grad(*p) for p in kv_products]
    grad_key, grad_value = plan.scatter_grad(quads_kv, [width_q, width_v])

    def along(weight, grad):
        return jnp.sum(wide(weight) * grad, axis=1)

    gain_sums = lax.psum(
        (
            along(query_weight, grad_query)
            + along(key_weight, grad_key)
            + along(value_weight, grad_value)
            + along(gate_weight, grad_gate),
            along(up_weight, grad_up),
        ),
        "tensor",
    )
    return (
        outputs.reshape(inputs.shape),
        grad_inputs.reshape(inputs.shape),
        gain_sums[0],
        gain_sums[1],
        grad_query * gain_one,
        grad_key * gain_one,
        grad_value * gain_one,
        grad_gate * gain_one,
        grad_out,
        grad_up * gain_two,
        grad_down,
    )


def body(inputs, lengths, first_gain, second_gain, query_weight, *rest):
    paired = (
        lax.axis_size("dp") == 4
        and lax.axis_size("tensor") == 2
        and inputs.shape[1] == 1
        and query_weight.shape[1] % (2 * QK) == 0
        and inputs.shape[3] % (4 * lax.axis_size("seq") * LANES) == 0
        and inputs.shape[2] % ROWS_STEP == 0
    )
    run = paired_body if paired else plain_body
    return run(inputs, lengths, first_gain, second_gain, query_weight, *rest)


def solution(mesh):
    tokens = P(None, "dp", ("seq", "tensor"), None)
    vector = P(("dp", "seq"))
    matrix = P(("dp", "seq"), "tensor")
    return jax.shard_map(
        body,
        mesh=mesh,
        in_specs=(tokens, P(None, "dp", None), vector, vector) + (matrix,) * 7 + (tokens,),
        out_specs=(tokens, tokens, vector, vector) + (matrix,) * 7,
        check_vma=False,
    )
```

time: 3460 us -> 1130 us (0.33)
  waiting for transfers between devices: 2430 us -> 432 us
  blocking collectives: 223 us -> 2.95 us
  matrix products: 489 us -> 271 us
  Pallas kernels: 0 us -> 159 us
  other arithmetic: 227 us -> 103 us
  starting transfers between devices: 2.08 us -> 67 us
    all_gather x26 -> x6, waiting for transfers between devices: 1430 us -> 53.3 us  [spread(): return lax.all_gather(tied(two, *before), 'seq', axis=0, tiled=True)]
    reduce_scatter x15 -> x6, waiting for transfers between devices: 992 us -> 0.05 us  [scatter_grad(): two = lax.psum_scatter(quad, 'seq', scatter_dimension=0, tiled=True)]
    ppermute x0 -> x76, waiting for transfers between devices: none -> 377 us  [the longest x64 263 us: swap(): lax.ppermute(values, axis, [(i, i ^ bit) for i in range(lax.axis_size(axi...]
    pallas_call x0 -> x31, Pallas kernels: none -> 159 us  [the longest x18 115 us: call(): pl.pallas_call(kernel, out_shape=out_shape, grid_spec=pltpu.PrefetchScala...]
    all_gather x4 -> x0, blocking collectives: 155 us -> none  [the longest x2 79.9 us: micro_step(): lax.all_gather(first_gain, ('dp', 'seq'), axis=0, tiled=True)]
    dot_general x24 -> x0, matrix products: 90.1 us -> none  [the longest x2 23.8 us: micro_step(): jnp.einsum('rnhd,rhde->rnhe', queries_carried, state_in, precision=PRECIS...]
    dot_general x14 -> x24, matrix products: 146 us -> 78.9 us  [tmatmul(): lax.dot_general(left_side, right_side, (((0,), (0,)), ((), ())), preferre...]
    ppermute x0 -> x76, starting transfers between devices: none -> 66.3 us  [the longest x64 44.4 us: swap(): lax.ppermute(values, axis, [(i, i ^ bit) for i in range(lax.axis_size(axi...]
  transfers between devices with their start and end apart: 41 -> 88, of which waited for: 26 -> 28; matrix products, arithmetic and copies ran while one was open for 15% -> 34% of each run, Pallas kernels for 0% -> 14%
where the time goes in v1:
time: 1130 us; the launch traced here: 1120 us
  waiting for transfers between devices  432 us (38%)
  matrix products  271 us (24%)
  Pallas kernels  159 us (14%)
  other arithmetic  103 us (9%)
  local copies, waits for them, and re-layouts  67.1 us (6%)
  starting transfers between devices  67 us (6%)
  between operations  17.2 us (2%)
    ppermute x64, waiting for transfers between devices, swap(): lax.ppermute(values, axis, [(i, i ^ bit) for i in range(lax.axis_size(axi...  263 us
    pallas_call x18, Pallas kernels, call(): pl.pallas_call(kernel, out_shape=out_shape, grid_spec=pltpu.PrefetchScala...  115 us
    ppermute x12, waiting for transfers between devices, pass_on(): entering.append(lax.ppermute(leaving, 'seq', [pair]))  115 us
    dot_general x10, matrix products, matmul(): return jnp.dot(left_side, right_side, preferred_element_type=jnp.float32)  107 us
    dot_general x20, matrix products, matmul_t(): lax.dot_general(left_side, right_side, (((1,), (1,)), ((), ())), preferre...  85.2 us
    dot_general x24, matrix products, tmatmul(): lax.dot_general(left_side, right_side, (((0,), (0,)), ((), ())), preferre...  78.9 us
    convert_element_type x27, other arithmetic, narrow(): return values.astype(jnp.bfloat16)  64.1 us
    all_gather x6, waiting for transfers between devices, spread(): return lax.all_gather(tied(two, *before), 'seq', axis=0, tiled=True)  53.3 us
  transfers between devices with their start and end apart: 88, of which 28 were waited for; matrix products, arithmetic and copies ran while one was open for 34% of the time, Pallas kernels for 14%

profile of v1, /device:TPU:0, one launch (start us, length us, event | category | flops | bytes accessed | tf_op | source)
XLA Modules:
  0.0 1118.7 jit_solution(8155413352015773324)
XLA Ops:
  30.6 10.5 collective-permute-done.1
  46.4 5.2 collective-permute-done.2
  52.5 14.7 %all-gather.7.cloned.1.call-done.refs_0_ = bf16[1024,768]{1,0:T(8,128)(2,1)} async-done(((bf16[256,768]{1,0:T(8,128)(2,1)}), bf16[1024,768]{1,0:T(8,128)(2,1)}) %all-gather.7.cloned.1.call-update) | async-done | bytes 1572880 | tf_op jit(solution)/shard_map/all_gather | solution.py:922
  71.5 22.7 %collective-permute-done.16 = s32[2,1,3]{2,1,0:T(1,128)S(1)} collective-permute-done((s32[2,1,3]{2,1,0:T(1,128)S(1)}, s32[2,1,3]{2,1,0:T(1,128)S(1)}, u32[]{:S(2)}, u32[]{:S(2)}) %collective-permute-start.16) | collective-permute-done | bytes 56 | tf_op jit(solution)/shard_map/ppermute | solution.py:341
  94.6 10.8 all-gather.15.cloned.1.call-done.refs_2_
  110.4 7.2 collective-permute-done.6
  122.0 5.7 fusion.119
  133.4 33.1 %collective-permute-done.9 = bf16[128,1024]{1,0:T(8,128)(2,1)S(1)} collective-permute-done((bf16[128,1024]{1,0:T(8,128)(2,1)}, bf16[128,1024]{1,0:T(8,128)(2,1)S(1)}, u32[]{:S(2)}, u32[]{:S(2)}) %collective-permute-start.9) | collective-permute-done | bytes 262176 | tf_op jit(solution)/shard_map/ppermute | solution.py:341
  172.6 4.9 shard_map.210
  177.5 10.5 fusion.150
  188.1 5.0 shard_map.212
  211.8 22.4 %collective-permute-done.26 = bf16[2,2,256,512]{3,2,1,0:T(8,128)(2,1)} collective-permute-done((bf16[2,2,256,512]{3,2,1,0:T(8,128)(2,1)}, bf16[2,2,256,512]{3,2,1,0:T(8,128)(2,1)}, u32[]{:S(2)}, u32[]{:S(2)}) %collective-permute-start.26) | collective-permute-done | bytes 1048608 | tf_op jit(solution)/shard_map/ppermute | solution.py:359
  237.5 10.1 fusion.149
  247.5 5.0 shard_map.213
  253.9 6.0 collective-permute-start.23
  271.0 4.5 shard_map.209
  276.4 10.6 fusion.151
  287.0 6.4 collective-permute-done.23
  296.6 8.5 fusion.148
  305.1 10.6 collective-permute-done.11.refs_1_
  317.4 8.8 shard_map.214
  342.1 5.0 convolution_convert_fusion.11
  348.9 9.2 shard_map.216
  372.8 17.1 %collective-permute-done.12.refs_1_ = bf16[1024,1024]{1,0:T(8,128)(2,1)S(1)} collective-permute-done((bf16[1024,1024]{1,0:T(8,128)(2,1)}, bf16[1024,1024]{1,0:T(8,128)(2,1)S(1)}, u32[]{:S(2)}, u32[]{:S(2)}) %collective-permute-start.12) | collective-permute-done | bytes 2097184 | tf_op jit(solution)/shard_map/ppermute | solution.py:341
  391.2 27.7 %all-gather.17.cloned.1.call-done.refs_0_ = bf16[1024,1024]{1,0:T(8,128)(2,1)} async-done(((bf16[256,1024]{1,0:T(8,128)(2,1)}), bf16[1024,1024]{1,0:T(8,128)(2,1)}) %all-gather.17.cloned.1.call-update) | async-done | bytes 2097168 | tf_op jit(solution)/shard_map/all_gather | solution.py:922
  432.6 10.6 fusion.146
  446.0 11.2 %collective-permute-done.37.refs_1_ = bf16[256,2048]{1,0:T(8,128)(2,1)S(1)} collective-permute-done((bf16[256,2048]{1,0:T(8,128)(2,1)S(1)}, bf16[256,2048]{1,0:T(8,128)(2,1)S(1)}, u32[]{:S(2)}, u32[]{:S(2)}) %collective-permute-start.37) | collective-permute-done | bytes 1048608 | tf_op jit(solution)/shard_map/ppermute | solution.py:341
  457.2 6.2 fusion.147
  468.9 9.4 collective-permute-done.30.c
  487.6 17.0 %multiply_convert_fusion = (bf16[1024,1024]{1,0:T(8,128)(2,1)}, f32[1024,1024]{1,0:T(8,128)S(1)}, f32[1024,1024]{1,0:T(8,128)S(1)}) fusion(bf16[1024,2048]{1,0:T(8,128)(2,1)} %shard_map.221, bf16[2048,1024]{1,0:T(8,128)(2,1)} %shard_map.219), kind=kOutput, calls=%fused_computation.20 | convolution fusion | flops 4363124736 | bytes 18874368 | tf_op jit(solution)/shard_map/dot_general | solution.py:96
  518.4 16.3 %add_convert_fusion.17 = (bf16[1024,1024]{1,0:T(8,128)(2,1)S(1)}, f32[1024,1024]{1,0:T(8,128)S(1)}, f32[1024,1024]{1,0:T(8,128)S(1)}) fusion(f32[1024,1024]{1,0:T(8,128)} %fusion.147, bf16[1024,2048]{1,0:T(8,128)(2,1)} %shard_map.218, bf16[2048,1024]{1,0:T(8,128)(2,1)S(1)} %copy-done.94), kind=kOutput, calls=%fused_computation.34 | convolution fusion | flops 4370464768 | bytes 23068672 | tf_op jit(solution)/shard_map/dot_general | solution.py:96
  560.3 16.5 %collective-permute-done.44.c = bf16[256,2048]{1,0:T(8,128)(2,1)S(1)} collective-permute-done((bf16[256,2048]{1,0:T(8,128)(2,1)S(1)}, bf16[256,2048]{1,0:T(8,128)(2,1)S(1)}, u32[]{:S(2)}, u32[]{:S(2)}) %collective-permute-start.44) | collective-permute-done | bytes 1048608 | tf_op jit(solution)/shard_map/ppermute | solution.py:341
  576.8 5.0 shard_map.223
  582.3 16.8 %collective-permute-done.50 = bf16[1024,1024]{1,0:T(8,128)(2,1)} collective-permute-done((bf16[1024,1024]{1,0:T(8,128)(2,1)}, bf16[1024,1024]{1,0:T(8,128)(2,1)}, u32[]{:S(2)}, u32[]{:S(2)}) %collective-permute-start.50) | collective-permute-done | bytes 2097184 | tf_op jit(solution)/shard_map/ppermute | solution.py:341
  605.1 4.9 fusion.28
  619.5 9.9 collective-permute-done.42.c
  629.4 5.2 shard_map.222
  638.9 8.4 fusion.152
  647.4 17.7 %shard_map.225 = (bf16[2,2,256,1536]{3,2,1,0:T(8,128)(2,1)}, bf16[2,2,256,512]{3,2,1,0:T(8,128)(2,1)}, f32[2,2,512,256]{3,2,1,0:T(8,128)}, f32[2,2,512,512]{3,2,1,0:T(8,128)}) custom-call(s32[5]{0:T(128)S(1)} %pad_add_fusion.2.numbers, f32[2]{0:T(128)S(1)} %get-tuple-element.319.log_gamma, f32[2,2,256,1536]{3,2,1,0:T(8,128)} %bitcast.207, ...), custom_call_target="tpu_custom_call" | custom-call | tf_op jit(solution)/shard_map/pallas_call | solution.py:454
  665.3 4.6 add_convert_fusion.12
  681.5 8.4 fusion.153
  690.0 17.0 %shard_map.227 = (bf16[2,2,256,1536]{3,2,1,0:T(8,128)(2,1)}, bf16[2,2,256,512]{3,2,1,0:T(8,128)(2,1)S(1)}, f32[2,2,512,256]{3,2,1,0:T(8,128)}, f32[2,2,512,512]{3,2,1,0:T(8,128)}) custom-call(s32[5]{0:T(128)S(1)} %pad_add_fusion.1.numbers, f32[2]{0:T(128)S(1)} %get-tuple-element.319.log_gamma, f32[2,2,256,1536]{3,2,1,0:T(8,128)} %bitcast.205, ...), custom_call_target="tpu_custom_call" | custom-call | tf_op jit(solution)/shard_map/pallas_call | solution.py:454
  731.2 5.0 add_convert_fusion.2
  736.3 5.0 add_convert_fusion.1
  768.2 63.3 %collective-permute-done.58 = bf16[2,2,256,512]{3,2,1,0:T(8,128)(2,1)} collective-permute-done((bf16[2,2,256,512]{3,2,1,0:T(8,128)(2,1)}, bf16[2,2,256,512]{3,2,1,0:T(8,128)(2,1)}, u32[]{:S(2)}, u32[]{:S(2)}) %collective-permute-start.58) | collective-permute-done | bytes 1048608 | tf_op jit(solution)/shard_map/ppermute | solution.py:359
  855.5 5.8 shard_map.230
  863.5 22.4 %collective-permute-done.61 = bf16[2,2,256,512]{3,2,1,0:T(8,128)(2,1)} collective-permute-done((bf16[2,2,256,512]{3,2,1,0:T(8,128)(2,1)}, bf16[2,2,256,512]{3,2,1,0:T(8,128)(2,1)}, u32[]{:S(2)}, u32[]{:S(2)}) %collective-permute-start.61) | collective-permute-done | bytes 1048608 | tf_op jit(solution)/shard_map/ppermute | solution.py:359
  888.0 5.9 shard_map.231
  909.2 25.5 %collective-permute-done.68 = bf16[1024,768]{1,0:T(8,128)(2,1)S(1)} collective-permute-done((bf16[1024,768]{1,0:T(8,128)(2,1)S(1)}, bf16[1024,768]{1,0:T(8,128)(2,1)S(1)}, u32[]{:S(2)}, u32[]{:S(2)}) %collective-permute-start.68) | collective-permute-done | bytes 1572896 | tf_op jit(solution)/shard_map/ppermute | solution.py:341
  947.5 4.6 add_convert_fusion.4
  952.1 24.7 %collective-permute-done.70 = bf16[1024,768]{1,0:T(8,128)(2,1)S(1)} collective-permute-done((bf16[1024,768]{1,0:T(8,128)(2,1)S(1)}, bf16[1024,768]{1,0:T(8,128)(2,1)S(1)}, u32[]{:S(2)}, u32[]{:S(2)}) %collective-permute-start.70) | collective-permute-done | bytes 1572896 | tf_op jit(solution)/shard_map/ppermute | solution.py:341
  978.6 5.5 add_convert_fusion
  984.1 6.4 fusion.77
  990.6 5.1 fusion.80
  995.7 4.6 add_convert_fusion.5
  1000.4 8.1 add_convert_fusion.6
  1009.0 8.2 fusion.83
  1017.2 5.5 add_convert_fusion.7
  1049.1 5.5 collective-permute-done.65.c
  1054.6 4.8 shard_map.232.refs_6_
  1059.4 17.7 %collective-permute-done.63.refs_5_ = bf16[256,2048]{1,0:T(8,128)(2,1)} collective-permute-done((bf16[256,2048]{1,0:T(8,128)(2,1)}, bf16[256,2048]{1,0:T(8,128)(2,1)}, u32[]{:S(2)}, u32[]{:S(2)}) %collective-permute-start.63) | collective-permute-done | bytes 1048608 | tf_op jit(solution)/shard_map/ppermute | solution.py:341
  1077.1 4.7 shard_map.233
  1087.4 4.5 collective-permute-done.69
  1096.9 7.6 collective-permute-done.67
  (693 shorter events, 383.8 us)
Async XLA Ops:
  7.2 60.0 %all-gather.7.cloned.1.call-start = ((), (), s32[]{:S(2)}) async-start(), calls=%async_computation.6 | async-start | bytes 1966080 | tf_op jit(solution)/shard_map/all_gather | solution.py:922
  29.7 75.7 %all-gather.15.cloned.1.call-start = ((), (), s32[]{:S(2)}) async-start(), calls=%async_computation.10 | async-start | bytes 1966080 | tf_op jit(solution)/shard_map/all_gather | solution.py:922
  30.4 167.6 %all-gather.13.cloned.1.call-start = ((), (), s32[]{:S(2)}) async-start(), calls=%async_computation.9 | async-start | bytes 3932160 | tf_op jit(solution)/shard_map/all_gather | solution.py:922
  42.2 223.0 %all-gather.11.cloned.1.call-start = ((), (), s32[]{:S(2)}) async-start(), calls=%async_computation.8 | async-start | bytes 2621440 | tf_op jit(solution)/shard_map/all_gather | solution.py:922
  42.7 66.9 %collective-permute-start.20 = (bf16[256,2048]{1,0:T(8,128)(2,1)}, bf16[256,2048]{1,0:T(8,128)(2,1)}, u32[]{:S(2)}, u32[]{:S(2)}) collective-permute-start(bf16[256,2048]{1,0:T(8,128)(2,1)} %get-tuple-element.97.refs_0_), channel_id=1, source_target_pairs={{0,8},{8,0},{16,24},{24,16},{1,9},{9,1},{17,25},{25,17},{2,10},{10... | collective-permute-start | bytes 3145736 | tf_op jit(solution)/shard_map/ppermute | solution.py:341
  44.4 65.3 %collective-permute-start.21 = (bf16[256,2048]{1,0:T(8,128)(2,1)}, bf16[256,2048]{1,0:T(8,128)(2,1)}, u32[]{:S(2)}, u32[]{:S(2)}) collective-permute-start(bf16[256,2048]{1,0:T(8,128)(2,1)} %get-tuple-element.97.refs_0_), channel_id=1, source_target_pairs={{0,1},{1,0},{2,3},{3,2},{4,5},{5,4},{6,7},{7,6},{8,9},{9,8},{10,11... | collective-permute-start | bytes 3145736 | tf_op jit(solution)/shard_map/ppermute | solution.py:341
  44.4 77.0 %collective-permute-start.17 = (bf16[256,2048]{1,0:T(8,128)(2,1)S(1)}, bf16[256,2048]{1,0:T(8,128)(2,1)}, u32[]{:S(2)}, u32[]{:S(2)}) collective-permute-start(bf16[256,2048]{1,0:T(8,128)(2,1)S(1)} %get-tuple-element.98.refs_0_), channel_id=1, source_target_pairs={{0,8},{8,0},{16,24},{24,16},{1,9},{9,1},{17,25},{25,17},{2,10},{10... | collective-permute-start | bytes 3145736 | tf_op jit(solution)/shard_map/ppermute | solution.py:341
  44.7 49.6 %collective-permute-start.16 = (s32[2,1,3]{2,1,0:T(1,128)S(1)}, s32[2,1,3]{2,1,0:T(1,128)S(1)}, u32[]{:S(2)}, u32[]{:S(2)}) collective-permute-start(s32[2,1,3]{2,1,0:T(1,128)S(1)} %copy-done.150), channel_id=1, source_target_pairs={{0,8},{8,0},{16,24},{24,16},{1,9},{9,1},{17,25},{25,17},{2,10},{10... | collective-permute-start | bytes 80 | tf_op jit(solution)/shard_map/ppermute | solution.py:341
  67.2 38.1 %collective-permute-start.7 = (bf16[1024,768]{1,0:T(8,128)(2,1)}, bf16[1024,768]{1,0:T(8,128)(2,1)S(1)}, u32[]{:S(2)}, u32[]{:S(2)}) collective-permute-start(bf16[1024,768]{1,0:T(8,128)(2,1)} %all-gather.7.cloned.1.call-done.refs_0_), channel_id=1, source_target_pairs={{0,16},{8,24},{16,0},{24,8},{1,17},{9,25},{17,1},{25,9},{2,18},{10... | collective-permute-start | bytes 4718600 | tf_op jit(solution)/shard_map/ppermute | solution.py:341
  106.5 61.5 %collective-permute-start.8 = (bf16[1024,768]{1,0:T(8,128)(2,1)}, bf16[1024,768]{1,0:T(8,128)(2,1)}, u32[]{:S(2)}, u32[]{:S(2)}) collective-permute-start(bf16[1024,768]{1,0:T(8,128)(2,1)} %all-gather.15.cloned.1.call-done.refs_2_), channel_id=1, source_target_pairs={{0,16},{8,24},{16,0},{24,8},{1,17},{9,25},{17,1},{25,9},{2,18},{10... | collective-permute-start | bytes 4718600 | tf_op jit(solution)/shard_map/ppermute | solution.py:341
  109.7 57.6 %collective-permute-start.3 = (bf16[256,2048]{1,0:T(8,128)(2,1)}, bf16[256,2048]{1,0:T(8,128)(2,1)}, u32[]{:S(2)}, u32[]{:S(2)}) collective-permute-start(bf16[256,2048]{1,0:T(8,128)(2,1)} %get-tuple-element.103.refs_0_.g), channel_id=1, source_target_pairs={{0,8},{8,0},{16,24},{24,16},{1,9},{9,1},{17,25},{25,17},{2,10},{10... | collective-permute-start | bytes 3145736 | tf_op jit(solution)/shard_map/ppermute | solution.py:341
  117.5 50.4 %collective-permute-start.13 = (bf16[256,2048]{1,0:T(8,128)(2,1)}, bf16[256,2048]{1,0:T(8,128)(2,1)}, u32[]{:S(2)}, u32[]{:S(2)}) collective-permute-start(bf16[256,2048]{1,0:T(8,128)(2,1)} %get-tuple-element.112.refs_0_.g), channel_id=1, source_target_pairs={{0,8},{8,0},{16,24},{24,16},{1,9},{9,1},{17,25},{25,17},{2,10},{10... | collective-permute-start | bytes 3145736 | tf_op jit(solution)/shard_map/ppermute | solution.py:341
  121.4 45.1 %collective-permute-start.9 = (bf16[128,1024]{1,0:T(8,128)(2,1)}, bf16[128,1024]{1,0:T(8,128)(2,1)S(1)}, u32[]{:S(2)}, u32[]{:S(2)}) collective-permute-start(bf16[128,1024]{1,0:T(8,128)(2,1)} %get-tuple-element.106), channel_id=1, source_target_pairs={{0,8},{8,0},{16,24},{24,16},{1,9},{9,1},{17,25},{25,17},{2,10},{10... | collective-permute-start | bytes 786440 | tf_op jit(solution)/shard_map/ppermute | solution.py:341
  127.7 213.8 %all-gather.9.cloned.1.call-start = ((), (), s32[]{:S(2)}) async-start(), calls=%async_computation.7 | async-start | bytes 2621440 | tf_op jit(solution)/shard_map/all_gather | solution.py:922
  128.8 65.6 %collective-permute-start.18 = (bf16[256,2048]{1,0:T(8,128)(2,1)}, bf16[256,2048]{1,0:T(8,128)(2,1)}, u32[]{:S(2)}, u32[]{:S(2)}) collective-permute-start(bf16[256,2048]{1,0:T(8,128)(2,1)} %copy-done.62), channel_id=1, source_target_pairs={{0,1},{1,0},{2,3},{3,2},{4,5},{5,4},{6,7},{7,6},{8,9},{9,8},{10,11... | collective-permute-start | bytes 3145736 | tf_op jit(solution)/shard_map/ppermute | solution.py:341
  166.5 28.1 %collective-permute-start.19 = (bf16[256,2048]{1,0:T(8,128)(2,1)}, bf16[256,2048]{1,0:T(8,128)(2,1)}, u32[]{:S(2)}, u32[]{:S(2)}) collective-permute-start(bf16[256,2048]{1,0:T(8,128)(2,1)} %collective-permute-done.17.refs_1_), channel_id=1, source_target_pairs={{0,1},{1,0},{2,3},{3,2},{4,5},{5,4},{6,7},{7,6},{8,9},{9,8},{10,11... | collective-permute-start | bytes 3145736 | tf_op jit(solution)/shard_map/ppermute | solution.py:341
  167.4 30.7 %collective-permute-start.4 = (bf16[256,2048]{1,0:T(8,128)(2,1)}, bf16[256,2048]{1,0:T(8,128)(2,1)}, u32[]{:S(2)}, u32[]{:S(2)}) collective-permute-start(bf16[256,2048]{1,0:T(8,128)(2,1)} %get-tuple-element.103.refs_0_.g), channel_id=1, source_target_pairs={{0,1},{1,0},{2,3},{3,2},{4,5},{5,4},{6,7},{7,6},{8,9},{9,8},{10,11... | collective-permute-start | bytes 3145736 | tf_op jit(solution)/shard_map/ppermute | solution.py:341
  167.9 40.1 %collective-permute-start.14 = (bf16[256,2048]{1,0:T(8,128)(2,1)}, bf16[256,2048]{1,0:T(8,128)(2,1)}, u32[]{:S(2)}, u32[]{:S(2)}) collective-permute-start(bf16[256,2048]{1,0:T(8,128)(2,1)} %get-tuple-element.112.refs_0_.g), channel_id=1, source_target_pairs={{0,1},{1,0},{2,3},{3,2},{4,5},{5,4},{6,7},{7,6},{8,9},{9,8},{10,11... | collective-permute-start | bytes 3145736 | tf_op jit(solution)/shard_map/ppermute | solution.py:341
  168.0 36.4 %collective-permute-start.5 = (bf16[256,2048]{1,0:T(8,128)(2,1)}, bf16[256,2048]{1,0:T(8,128)(2,1)}, u32[]{:S(2)}, u32[]{:S(2)}) collective-permute-start(bf16[256,2048]{1,0:T(8,128)(2,1)} %collective-permute-done.3.refs_1_), channel_id=1, source_target_pairs={{0,1},{1,0},{2,3},{3,2},{4,5},{5,4},{6,7},{7,6},{8,9},{9,8},{10,11... | collective-permute-start | bytes 3145736 | tf_op jit(solution)/shard_map/ppermute | solution.py:341
  194.5 39.7 %collective-permute-start.26 = (bf16[2,2,256,512]{3,2,1,0:T(8,128)(2,1)}, bf16[2,2,256,512]{3,2,1,0:T(8,128)(2,1)}, u32[]{:S(2)}, u32[]{:S(2)}) collective-permute-start(bf16[2,2,256,512]{3,2,1,0:T(8,128)(2,1)} %get-tuple-element.114), channel_id=1, source_target_pairs={{0,2},{1,3},{8,10},{9,11},{16,18},{17,19},{24,26},{25,27}} | collective-permute-start | bytes 3145736 | tf_op jit(solution)/shard_map/ppermute | solution.py:359
  198.0 70.5 %collective-permute-start.10 = (bf16[1024,1536]{1,0:T(8,128)(2,1)}, bf16[1024,1536]{1,0:T(8,128)(2,1)}, u32[]{:S(2)}, u32[]{:S(2)}) collective-permute-start(bf16[1024,1536]{1,0:T(8,128)(2,1)} %all-gather.13.cloned.1.call-done.refs_0_), channel_id=1, source_target_pairs={{0,16},{8,24},{16,0},{24,8},{1,17},{9,25},{17,1},{25,9},{2,18},{10... | collective-permute-start | bytes 9437192 | tf_op jit(solution)/shard_map/ppermute | solution.py:341
  204.3 214.6 %all-gather.17.cloned.1.call-start = ((), (), s32[]{:S(2)}) async-start(), calls=%async_computation.11 | async-start | bytes 2621440 | tf_op jit(solution)/shard_map/all_gather | solution.py:922
  253.9 39.6 %collective-permute-start.23 = (bf16[2,2,256,512]{3,2,1,0:T(8,128)(2,1)}, bf16[2,2,256,512]{3,2,1,0:T(8,128)(2,1)}, u32[]{:S(2)}, u32[]{:S(2)}) collective-permute-start(bf16[2,2,256,512]{3,2,1,0:T(8,128)(2,1)} %get-tuple-element.118), channel_id=1, source_target_pairs={{0,2},{1,3},{8,10},{9,11},{16,18},{17,19},{24,26},{25,27}} | collective-permute-start | bytes 3145736 | tf_op jit(solution)/shard_map/ppermute | solution.py:359
  263.6 41.6 %collective-permute-start.28 = (bf16[2,2,256,512]{3,2,1,0:T(8,128)(2,1)}, bf16[2,2,256,512]{3,2,1,0:T(8,128)(2,1)}, u32[]{:S(2)}, u32[]{:S(2)}) collective-permute-start(bf16[2,2,256,512]{3,2,1,0:T(8,128)(2,1)} %fusion.15), channel_id=1, source_target_pairs={{4,6},{5,7},{12,14},{13,15},{20,22},{21,23},{28,30},{29,31}} | collective-permute-start | bytes 3145736 | tf_op jit(solution)/shard_map/ppermute | solution.py:359
  268.6 47.1 %collective-permute-start.11 = (bf16[1024,1024]{1,0:T(8,128)(2,1)}, bf16[1024,1024]{1,0:T(8,128)(2,1)S(1)}, u32[]{:S(2)}, u32[]{:S(2)}) collective-permute-start(bf16[1024,1024]{1,0:T(8,128)(2,1)} %all-gather.11.cloned.1.call-done.refs_0_), channel_id=1, source_target_pairs={{0,16},{8,24},{16,0},{24,8},{1,17},{9,25},{17,1},{25,9},{2,18},{10... | collective-permute-start | bytes 6291464 | tf_op jit(solution)/shard_map/ppermute | solution.py:341
  295.5 40.7 %collective-permute-start.24 = (bf16[2,2,256,512]{3,2,1,0:T(8,128)(2,1)S(1)}, bf16[2,2,256,512]{3,2,1,0:T(8,128)(2,1)S(1)}, u32[]{:S(2)}, u32[]{:S(2)}) collective-permute-start(bf16[2,2,256,512]{3,2,1,0:T(8,128)(2,1)S(1)} %fusion.12), channel_id=1, source_target_pairs={{2,4},{3,5},{10,12},{11,13},{18,20},{19,21},{26,28},{27,29}} | collective-permute-start | bytes 3145736 | tf_op jit(solution)/shard_map/ppermute | solution.py:359
  341.4 424.6 %reduce-scatter.17.cloned.1.call-start = ((), (), s32[]{:S(2)}) async-start(), calls=%async_computation.17 | async-start | bytes 2621440 | tf_op jit(solution)/shard_map/reduce_scatter | solution.py:855
  341.5 48.3 %collective-permute-start.12 = (bf16[1024,1024]{1,0:T(8,128)(2,1)}, bf16[1024,1024]{1,0:T(8,128)(2,1)S(1)}, u32[]{:S(2)}, u32[]{:S(2)}) collective-permute-start(bf16[1024,1024]{1,0:T(8,128)(2,1)} %all-gather.9.cloned.1.call-done.refs_0_), channel_id=1, source_target_pairs={{0,16},{8,24},{16,0},{24,8},{1,17},{9,25},{17,1},{25,9},{2,18},{10... | collective-permute-start | bytes 6291464 | tf_op jit(solution)/shard_map/ppermute | solution.py:341
  363.0 64.2 %collective-permute-start.36 = (bf16[256,2048]{1,0:T(8,128)(2,1)}, bf16[256,2048]{1,0:T(8,128)(2,1)}, u32[]{:S(2)}, u32[]{:S(2)}) collective-permute-start(bf16[256,2048]{1,0:T(8,128)(2,1)} %add_convert_fusion.30), channel_id=1, source_target_pairs={{0,8},{8,0},{16,24},{24,16},{1,9},{9,1},{17,25},{25,17},{2,10},{10... | collective-permute-start | bytes 3145736 | tf_op jit(solution)/shard_map/ppermute | solution.py:341
  368.2 75.0 %collective-permute-start.29 = (bf16[512,2048]{1,0:T(8,128)(2,1)}, bf16[512,2048]{1,0:T(8,128)(2,1)}, u32[]{:S(2)}, u32[]{:S(2)}) collective-permute-start(bf16[512,2048]{1,0:T(8,128)(2,1)} %convolution_convert_fusion.9), channel_id=1, source_target_pairs={{0,1},{1,0},{2,3},{3,2},{4,5},{5,4},{6,7},{7,6},{8,9},{9,8},{10,11... | collective-permute-start | bytes 6291464 | tf_op jit(solution)/shard_map/ppermute | solution.py:341
  418.9 47.6 %collective-permute-start.34 = (bf16[1024,1024]{1,0:T(8,128)(2,1)}, bf16[1024,1024]{1,0:T(8,128)(2,1)S(1)}, u32[]{:S(2)}, u32[]{:S(2)}) collective-permute-start(bf16[1024,1024]{1,0:T(8,128)(2,1)} %all-gather.17.cloned.1.call-done.refs_0_), channel_id=1, source_target_pairs={{0,16},{8,24},{16,0},{24,8},{1,17},{9,25},{17,1},{25,9},{2,18},{10... | collective-permute-start | bytes 6291464 | tf_op jit(solution)/shard_map/ppermute | solution.py:341
  431.1 26.1 %collective-permute-start.37 = (bf16[256,2048]{1,0:T(8,128)(2,1)S(1)}, bf16[256,2048]{1,0:T(8,128)(2,1)S(1)}, u32[]{:S(2)}, u32[]{:S(2)}) collective-permute-start(bf16[256,2048]{1,0:T(8,128)(2,1)S(1)} %get-tuple-element.133.refs_0_), channel_id=1, source_target_pairs={{0,8},{8,0},{16,24},{24,16},{1,9},{9,1},{17,25},{25,17},{2,10},{10... | collective-permute-start | bytes 3145736 | tf_op jit(solution)/shard_map/ppermute | solution.py:341
  443.2 38.9 %collective-permute-start.38 = (bf16[256,2048]{1,0:T(8,128)(2,1)S(1)}, bf16[256,2048]{1,0:T(8,128)(2,1)S(1)}, u32[]{:S(2)}, u32[]{:S(2)}) collective-permute-start(bf16[256,2048]{1,0:T(8,128)(2,1)S(1)} %get-tuple-element.133.refs_0_), channel_id=1, source_target_pairs={{0,1},{1,0},{2,3},{3,2},{4,5},{5,4},{6,7},{7,6},{8,9},{9,8},{10,11... | collective-permute-start | bytes 3145736 | tf_op jit(solution)/shard_map/ppermute | solution.py:341
  445.8 32.4 %collective-permute-start.30 = (bf16[256,2048]{1,0:T(8,128)(2,1)}, bf16[256,2048]{1,0:T(8,128)(2,1)S(1)}, u32[]{:S(2)}, u32[]{:S(2)}) collective-permute-start(bf16[256,2048]{1,0:T(8,128)(2,1)} %add_convert_fusion.31), channel_id=1, source_target_pairs={{0,8},{8,0},{16,24},{24,16},{1,9},{9,1},{17,25},{25,17},{2,10},{10... | collective-permute-start | bytes 3145736 | tf_op jit(solution)/shard_map/ppermute | solution.py:341
  482.1 32.6 %collective-permute-start.32 = (bf16[256,2048]{1,0:T(8,128)(2,1)S(1)}, bf16[256,2048]{1,0:T(8,128)(2,1)S(1)}, u32[]{:S(2)}, u32[]{:S(2)}) collective-permute-start(bf16[256,2048]{1,0:T(8,128)(2,1)S(1)} %get-tuple-element.128.refs_0_), channel_id=1, source_target_pairs={{0,1},{1,0},{2,3},{3,2},{4,5},{5,4},{6,7},{7,6},{8,9},{9,8},{10,11... | collective-permute-start | bytes 3145736 | tf_op jit(solution)/shard_map/ppermute | solution.py:341
  550.9 48.2 %collective-permute-start.50 = (bf16[1024,1024]{1,0:T(8,128)(2,1)}, bf16[1024,1024]{1,0:T(8,128)(2,1)}, u32[]{:S(2)}, u32[]{:S(2)}) collective-permute-start(bf16[1024,1024]{1,0:T(8,128)(2,1)} %add_convert_fusion.14), channel_id=1, source_target_pairs={{0,16},{8,24},{16,0},{24,8},{1,17},{9,25},{17,1},{25,9},{2,18},{10... | collective-permute-start | bytes 6291464 | tf_op jit(solution)/shard_map/ppermute | solution.py:341
  581.8 28.3 %collective-permute-start.45 = (bf16[256,2048]{1,0:T(8,128)(2,1)}, bf16[256,2048]{1,0:T(8,128)(2,1)}, u32[]{:S(2)}, u32[]{:S(2)}) collective-permute-start(bf16[256,2048]{1,0:T(8,128)(2,1)} %get-tuple-element.138.refs_0_), channel_id=1, source_target_pairs={{0,8},{8,0},{16,24},{24,16},{1,9},{9,1},{17,25},{25,17},{2,10},{10... | collective-permute-start | bytes 3145736 | tf_op jit(solution)/shard_map/ppermute | solution.py:341
  603.1 258.3 %reduce-scatter.13.cloned.1.call-start = ((), (), s32[]{:S(2)}) async-start(), calls=%async_computation.15 | async-start | bytes 2621440 | tf_op jit(solution)/shard_map/reduce_scatter | solution.py:855
  605.1 30.0 %collective-permute-start.46 = (bf16[256,2048]{1,0:T(8,128)(2,1)}, bf16[256,2048]{1,0:T(8,128)(2,1)S(1)}, u32[]{:S(2)}, u32[]{:S(2)}) collective-permute-start(bf16[256,2048]{1,0:T(8,128)(2,1)} %get-tuple-element.138.refs_0_), channel_id=1, source_target_pairs={{0,1},{1,0},{2,3},{3,2},{4,5},{5,4},{6,7},{7,6},{8,9},{9,8},{10,11... | collective-permute-start | bytes 3145736 | tf_op jit(solution)/shard_map/ppermute | solution.py:341
  614.4 55.6 %collective-permute-start.51 = (bf16[1024,1024]{1,0:T(8,128)(2,1)}, bf16[1024,1024]{1,0:T(8,128)(2,1)}, u32[]{:S(2)}, u32[]{:S(2)}) collective-permute-start(bf16[1024,1024]{1,0:T(8,128)(2,1)} %add_convert_fusion.11), channel_id=1, source_target_pairs={{0,16},{8,24},{16,0},{24,8},{1,17},{9,25},{17,1},{25,9},{2,18},{10... | collective-permute-start | bytes 6291464 | tf_op jit(solution)/shard_map/ppermute | solution.py:341
  634.5 30.5 %collective-permute-start.43 = (bf16[256,2048]{1,0:T(8,128)(2,1)}, bf16[256,2048]{1,0:T(8,128)(2,1)}, u32[]{:S(2)}, u32[]{:S(2)}) collective-permute-start(bf16[256,2048]{1,0:T(8,128)(2,1)} %get-tuple-element.135.refs_0_), channel_id=1, source_target_pairs={{0,8},{8,0},{16,24},{24,16},{1,9},{9,1},{17,25},{25,17},{2,10},{10... | collective-permute-start | bytes 3145736 | tf_op jit(solution)/shard_map/ppermute | solution.py:341
  635.1 39.5 %collective-permute-start.48 = (bf16[256,2048]{1,0:T(8,128)(2,1)}, bf16[256,2048]{1,0:T(8,128)(2,1)}, u32[]{:S(2)}, u32[]{:S(2)}) collective-permute-start(bf16[256,2048]{1,0:T(8,128)(2,1)} %get-tuple-element.135.refs_0_), channel_id=1, source_target_pairs={{0,1},{1,0},{2,3},{3,2},{4,5},{5,4},{6,7},{7,6},{8,9},{9,8},{10,11... | collective-permute-start | bytes 3145736 | tf_op jit(solution)/shard_map/ppermute | solution.py:341
  673.9 369.3 %reduce-scatter.15.cloned.1.call-start = ((), (), s32[]{:S(2)}) async-start(), calls=%async_computation.16 | async-start | bytes 2621440 | tf_op jit(solution)/shard_map/reduce_scatter | solution.py:855
  673.9 54.2 %collective-permute-start.56 = (bf16[2,2,256,512]{3,2,1,0:T(8,128)(2,1)}, bf16[2,2,256,512]{3,2,1,0:T(8,128)(2,1)S(1)}, u32[]{:S(2)}, u32[]{:S(2)}) collective-permute-start(bf16[2,2,256,512]{3,2,1,0:T(8,128)(2,1)} %get-tuple-element.141), channel_id=1, source_target_pairs={{6,4},{7,5},{14,12},{15,13},{22,20},{23,21},{30,28},{31,29}} | collective-permute-start | bytes 3145736 | tf_op jit(solution)/shard_map/ppermute | solution.py:359
  711.9 40.6 %collective-permute-start.59 = (bf16[2,2,256,512]{3,2,1,0:T(8,128)(2,1)S(1)}, bf16[2,2,256,512]{3,2,1,0:T(8,128)(2,1)S(1)}, u32[]{:S(2)}, u32[]{:S(2)}) collective-permute-start(bf16[2,2,256,512]{3,2,1,0:T(8,128)(2,1)S(1)} %get-tuple-element.152), channel_id=1, source_target_pairs={{6,4},{7,5},{14,12},{15,13},{22,20},{23,21},{30,28},{31,29}} | collective-permute-start | bytes 3145736 | tf_op jit(solution)/shard_map/ppermute | solution.py:359
  724.0 118.9 %collective-permute-start.73 = (bf16[1024,1024]{1,0:T(8,128)(2,1)}, bf16[1024,1024]{1,0:T(8,128)(2,1)}, u32[]{:S(2)}, u32[]{:S(2)}) collective-permute-start(bf16[1024,1024]{1,0:T(8,128)(2,1)} %add_convert_fusion.9), channel_id=1, source_target_pairs={{0,16},{8,24},{16,0},{24,8},{1,17},{9,25},{17,1},{25,9},{2,18},{10... | collective-permute-start | bytes 6291464 | tf_op jit(solution)/shard_map/ppermute | solution.py:341
  745.0 91.4 %collective-permute-start.54 = (bf16[512,2048]{1,0:T(8,128)(2,1)}, bf16[512,2048]{1,0:T(8,128)(2,1)}, u32[]{:S(2)}, u32[]{:S(2)}) collective-permute-start(bf16[512,2048]{1,0:T(8,128)(2,1)} %convolution_convert_fusion), channel_id=1, source_target_pairs={{0,1},{1,0},{2,3},{3,2},{4,5},{5,4},{6,7},{7,6},{8,9},{9,8},{10,11... | collective-permute-start | bytes 6291464 | tf_op jit(solution)/shard_map/ppermute | solution.py:341
  751.2 80.3 %collective-permute-start.58 = (bf16[2,2,256,512]{3,2,1,0:T(8,128)(2,1)}, bf16[2,2,256,512]{3,2,1,0:T(8,128)(2,1)}, u32[]{:S(2)}, u32[]{:S(2)}) collective-permute-start(bf16[2,2,256,512]{3,2,1,0:T(8,128)(2,1)} %fusion.17), channel_id=1, source_target_pairs={{2,0},{3,1},{10,8},{11,9},{18,16},{19,17},{26,24},{27,25}} | collective-permute-start | bytes 3145736 | tf_op jit(solution)/shard_map/ppermute | solution.py:359
  754.0 78.8 %collective-permute-start.60 = (bf16[2,2,256,512]{3,2,1,0:T(8,128)(2,1)}, bf16[2,2,256,512]{3,2,1,0:T(8,128)(2,1)}, u32[]{:S(2)}, u32[]{:S(2)}) collective-permute-start(bf16[2,2,256,512]{3,2,1,0:T(8,128)(2,1)} %fusion.18), channel_id=1, source_target_pairs={{4,2},{5,3},{12,10},{13,11},{20,18},{21,19},{28,26},{29,27}} | collective-permute-start | bytes 3145736 | tf_op jit(solution)/shard_map/ppermute | solution.py:359
  760.8 87.1 %collective-permute-start.52 = (bf16[512,2048]{1,0:T(8,128)(2,1)}, bf16[512,2048]{1,0:T(8,128)(2,1)}, u32[]{:S(2)}, u32[]{:S(2)}) collective-permute-start(bf16[512,2048]{1,0:T(8,128)(2,1)} %convolution_convert_fusion.2), channel_id=1, source_target_pairs={{0,1},{1,0},{2,3},{3,2},{4,5},{5,4},{6,7},{7,6},{8,9},{9,8},{10,11... | collective-permute-start | bytes 6291464 | tf_op jit(solution)/shard_map/ppermute | solution.py:341
  831.5 147.1 %collective-permute-start.66 = (bf16[1024,1536]{1,0:T(8,128)(2,1)}, bf16[1024,1536]{1,0:T(8,128)(2,1)}, u32[]{:S(2)}, u32[]{:S(2)}) collective-permute-start(bf16[1024,1536]{1,0:T(8,128)(2,1)} %add_convert_fusion.2), channel_id=1, source_target_pairs={{0,16},{8,24},{16,0},{24,8},{1,17},{9,25},{17,1},{25,9},{2,18},{10... | collective-permute-start | bytes 9437192 | tf_op jit(solution)/shard_map/ppermute | solution.py:341
  832.7 196.3 %collective-permute-start.75 = (bf16[128,1024]{1,0:T(8,128)(2,1)}, bf16[128,1024]{1,0:T(8,128)(2,1)S(1)}, u32[]{:S(2)}, u32[]{:S(2)}) collective-permute-start(bf16[128,1024]{1,0:T(8,128)(2,1)} %get-tuple-element.245), channel_id=1, source_target_pairs={{0,8},{8,0},{16,24},{24,16},{1,9},{9,1},{17,25},{25,17},{2,10},{10... | collective-permute-start | bytes 786440 | tf_op jit(solution)/shard_map/ppermute | solution.py:341
  836.5 49.4 %collective-permute-start.61 = (bf16[2,2,256,512]{3,2,1,0:T(8,128)(2,1)}, bf16[2,2,256,512]{3,2,1,0:T(8,128)(2,1)}, u32[]{:S(2)}, u32[]{:S(2)}) collective-permute-start(bf16[2,2,256,512]{3,2,1,0:T(8,128)(2,1)} %fusion.19), channel_id=1, source_target_pairs={{2,0},{3,1},{10,8},{11,9},{18,16},{19,17},{26,24},{27,25}} | collective-permute-start | bytes 3145736 | tf_op jit(solution)/shard_map/ppermute | solution.py:359
  842.9 191.6 %collective-permute-start.55 = (bf16[256,2048]{1,0:T(8,128)(2,1)}, bf16[256,2048]{1,0:T(8,128)(2,1)}, u32[]{:S(2)}, u32[]{:S(2)}) collective-permute-start(bf16[256,2048]{1,0:T(8,128)(2,1)} %add_convert_fusion.26), channel_id=1, source_target_pairs={{0,8},{8,0},{16,24},{24,16},{1,9},{9,1},{17,25},{25,17},{2,10},{10... | collective-permute-start | bytes 3145736 | tf_op jit(solution)/shard_map/ppermute | solution.py:341
  847.9 235.1 %reduce-scatter.9.cloned.1.call-start = ((), (), s32[]{:S(2)}) async-start(), calls=%async_computation.13 | async-start | bytes 1966080 | tf_op jit(solution)/shard_map/reduce_scatter | solution.py:855
  851.0 187.3 %collective-permute-start.53 = (bf16[256,2048]{1,0:T(8,128)(2,1)}, bf16[256,2048]{1,0:T(8,128)(2,1)}, u32[]{:S(2)}, u32[]{:S(2)}) collective-permute-start(bf16[256,2048]{1,0:T(8,128)(2,1)} %add_convert_fusion.27), channel_id=1, source_target_pairs={{0,8},{8,0},{16,24},{24,16},{1,9},{9,1},{17,25},{25,17},{2,10},{10... | collective-permute-start | bytes 3145736 | tf_op jit(solution)/shard_map/ppermute | solution.py:341
  899.5 35.1 %collective-permute-start.68 = (bf16[1024,768]{1,0:T(8,128)(2,1)S(1)}, bf16[1024,768]{1,0:T(8,128)(2,1)S(1)}, u32[]{:S(2)}, u32[]{:S(2)}) collective-permute-start(bf16[1024,768]{1,0:T(8,128)(2,1)S(1)} %add_convert_fusion.21), channel_id=1, source_target_pairs={{0,16},{8,24},{16,0},{24,8},{1,17},{9,25},{17,1},{25,9},{2,18},{10... | collective-permute-start | bytes 4718600 | tf_op jit(solution)/shard_map/ppermute | solution.py:341
  936.2 149.2 %reduce-scatter.11.cloned.1.call-start = ((), (), s32[]{:S(2)}) async-start(), calls=%async_computation.14 | async-start | bytes 1966080 | tf_op jit(solution)/shard_map/reduce_scatter | solution.py:855
  942.6 34.2 %collective-permute-start.70 = (bf16[1024,768]{1,0:T(8,128)(2,1)S(1)}, bf16[1024,768]{1,0:T(8,128)(2,1)S(1)}, u32[]{:S(2)}, u32[]{:S(2)}) collective-permute-start(bf16[1024,768]{1,0:T(8,128)(2,1)S(1)} %add_convert_fusion.19), channel_id=1, source_target_pairs={{0,16},{8,24},{16,0},{24,8},{1,17},{9,25},{17,1},{25,9},{2,18},{10... | collective-permute-start | bytes 4718600 | tf_op jit(solution)/shard_map/ppermute | solution.py:341
  976.8 46.0 %collective-permute-start.64 = (bf16[512,2048]{1,0:T(8,128)(2,1)}, bf16[512,2048]{1,0:T(8,128)(2,1)}, u32[]{:S(2)}, u32[]{:S(2)}) collective-permute-start(bf16[512,2048]{1,0:T(8,128)(2,1)} %add_convert_fusion.4), channel_id=1, source_target_pairs={{0,1},{1,0},{2,3},{3,2},{4,5},{5,4},{6,7},{7,6},{8,9},{9,8},{10,11... | collective-permute-start | bytes 6291464 | tf_op jit(solution)/shard_map/ppermute | solution.py:341
  978.5 115.8 %reduce-scatter.7.cloned.1.call-start = ((), (), s32[]{:S(2)}) async-start(), calls=%async_computation.12 | async-start | bytes 3932160 | tf_op jit(solution)/shard_map/reduce_scatter | solution.py:855
  1026.8 27.8 %collective-permute-start.65 = (bf16[256,2048]{1,0:T(8,128)(2,1)}, bf16[256,2048]{1,0:T(8,128)(2,1)}, u32[]{:S(2)}, u32[]{:S(2)}) collective-permute-start(bf16[256,2048]{1,0:T(8,128)(2,1)} %add_convert_fusion.24), channel_id=1, source_target_pairs={{0,8},{8,0},{16,24},{24,16},{1,9},{9,1},{17,25},{25,17},{2,10},{10... | collective-permute-start | bytes 3145736 | tf_op jit(solution)/shard_map/ppermute | solution.py:341
  1029.0 48.1 %collective-permute-start.63 = (bf16[256,2048]{1,0:T(8,128)(2,1)}, bf16[256,2048]{1,0:T(8,128)(2,1)}, u32[]{:S(2)}, u32[]{:S(2)}) collective-permute-start(bf16[256,2048]{1,0:T(8,128)(2,1)} %add_convert_fusion.25), channel_id=1, source_target_pairs={{0,8},{8,0},{16,24},{24,16},{1,9},{9,1},{17,25},{25,17},{2,10},{10... | collective-permute-start | bytes 3145736 | tf_op jit(solution)/shard_map/ppermute | solution.py:341
  1044.4 37.4 %collective-permute-start.74 = (bf16[128,1024]{1,0:T(8,128)(2,1)S(1)}, bf16[128,1024]{1,0:T(8,128)(2,1)S(1)}, u32[]{:S(2)}, u32[]{:S(2)}) collective-permute-start(bf16[128,1024]{1,0:T(8,128)(2,1)S(1)} %get-tuple-element.247), channel_id=1, source_target_pairs={{0,8},{8,0},{16,24},{24,16},{1,9},{9,1},{17,25},{25,17},{2,10},{10... | collective-permute-start | bytes 786440 | tf_op jit(solution)/shard_map/ppermute | solution.py:341
  (197 other events, 4294.7 us)
Sparse Core Ops, SparseCore 0:
  29.8 37.4 all-gather.6
  69.4 35.9 all-gather.14
  106.9 62.3 all-gather.12
  170.8 54.9 all-gather.10
  227.2 55.1 all-gather.8
  341.6 77.3 all-gather.16
  603.2 85.0 reduce-scatter.16
  690.6 100.6 reduce-scatter.12
  848.0 51.6 reduce-scatter.14
  936.3 32.5 reduce-scatter.8
  978.6 33.0 reduce-scatter.10
  1014.0 59.2 reduce-scatter.6

commit v2 on v1

--- a/solution.py
+++ b/solution.py
@@ -347,50 +347,27 @@
     )
 
 
-def pass_on(state, through, reverse, ties):
-    count = lax.axis_size("seq")
-    entering = []
-    for hop in range(1, count):
-        leaving = state
-        if entering:
-            before = tied(entering[-1], *ties.get(hop, ()))
-            leaving = narrow(wide(state) + through[..., None, None] * wide(before))
-        pair = (count - hop, count - 1 - hop) if reverse else (hop - 1, hop)
-        entering.append(lax.ppermute(leaving, "seq", [pair]))
-    return entering
-
-
-def arrive(entering, *before):
-    return sum(entering[:-1], tied(entering[-1], *before))
-
-
 LANES = 128
 
 
-def place_order(blocks):
-    return [(up, block, side) for up in range(2) for block in range(blocks) for side in range(2)]
-
-
-def group_of(place, upper, blocks):
-    up, block, side = place
-    start = (up ^ upper) if isinstance(upper, int) else lax.bitwise_xor(upper, up)
-    return (start * 2 + side) * blocks + block
-
-
-def load_groups(ref, upper, blocks):
-    width = ref.shape[1] // (4 * blocks)
+def group_of(place, upper):
+    return lax.bitwise_xor(upper * 2, place)
+
+
+def load_groups(ref, upper, groups):
+    width = ref.shape[1] // groups
     parts = []
-    for place in place_order(blocks):
-        at = pl.multiple_of(group_of(place, upper, blocks) * width, LANES)
+    for place in range(groups):
+        at = pl.multiple_of(group_of(place, upper) * width, LANES)
         parts.append(ref[:, pl.ds(at, width)])
     return jnp.concatenate(parts, axis=1)
 
 
-def store_groups(ref, values, upper, blocks):
-    width = ref.shape[1] // (4 * blocks)
-    for i, place in enumerate(place_order(blocks)):
-        at = pl.multiple_of(group_of(place, upper, blocks) * width, LANES)
-        ref[:, pl.ds(at, width)] = values[:, i * width : (i + 1) * width]
+def store_groups(ref, values, upper, groups):
+    width = ref.shape[1] // groups
+    for place in range(groups):
+        at = pl.multiple_of(group_of(place, upper) * width, LANES)
+        ref[:, pl.ds(at, width)] = values[:, place * width : (place + 1) * width]
 
 
 VMEM_BYTES = 48 << 20
@@ -501,11 +478,11 @@
     )
 
 
-def enter_tokens(upper, blocks, tokens, start, inputs, cotangent):
+def enter_tokens(upper, groups, tokens, start, inputs, cotangent):
     def kernel(up, x, c, normed, x_out, c_out):
-        values = load_groups(x, up[0], blocks)
+        values = load_groups(x, up[0], groups)
         x_out[...] = values
-        c_out[...] = load_groups(c, up[0], blocks)
+        c_out[...] = load_groups(c, up[0], groups)
         normed[...] = narrow(norm_rows(wide(values), EPSILON)[0])
 
     return row_call(
@@ -528,9 +505,9 @@
     )
 
 
-def output_tokens(upper, blocks, middle, parts, into):
+def output_tokens(upper, groups, middle, parts, into):
     def kernel(up, m, a, b, c, out):
-        store_groups(out, narrow(m[...] + total((a, b, c))), up[0], blocks)
+        store_groups(out, narrow(m[...] + total((a, b, c))), up[0], groups)
 
     return row_call(
         kernel, upper, middle.shape[0], (middle,) + parts, (jnp.bfloat16,), into=into
@@ -553,11 +530,11 @@
     )
 
 
-def back_inputs(upper, blocks, inputs, grad_middle, parts, into):
+def back_inputs(upper, groups, inputs, grad_middle, parts, into):
     def kernel(up, x, g, a, b, c, out):
         normed, inv = norm_rows(wide(x[...]), EPSILON)
         values = g[...] + norm_back(total((a, b, c)), normed, inv)
-        store_groups(out, narrow(values), up[0], blocks)
+        store_groups(out, narrow(values), up[0], groups)
 
     return row_call(
         kernel,
@@ -816,14 +793,17 @@
     def __init__(self, tensor_heads):
         self.rows = 2
         self.heads = tensor_heads // 2
-        self.side = lax.axis_index("dp") % 2
-        self.upper = (lax.axis_index("dp") // 2).astype(jnp.int32)
+        self.block = lax.axis_index("seq").astype(jnp.int32)
+        self.side = self.block % 2
+        self.upper = self.block // 2
         self.core = lax.axis_index("tensor")
-        self.blocks = lax.axis_size("seq")
+        self.groups = lax.axis_size("dp") * lax.axis_size("seq")
         self.first_head = self.core * tensor_heads + self.side * self.heads
 
     def gather_tokens(self, values, *before):
-        across = tied(swap(values, "dp", 1), *before)
+        return self.gather_from(values, tied(swap(values, "seq", 1), *before))
+
+    def gather_from(self, values, across):
         own = (values, swap(values, "tensor", 1))
         return join((own[0], across, own[1], swap(across, "tensor", 1)))
 
@@ -832,7 +812,7 @@
         here = product(0)
         half = here.shape[0] // 2
         across = narrow(wide(here[half:]) + wide(away[half:]))
-        return (here[:half], away[:half], swap(across, "dp", 1)), here, across
+        return (here[:half], away[:half], swap(across, "seq", 1)), here, across
 
     def halves(self, shard, which):
         width = shard.shape[1] // 2
@@ -841,22 +821,26 @@
     def swap_weight(self, shards, *before):
         here = jnp.concatenate([self.halves(w, self.side) for w in shards], axis=1)
         away = jnp.concatenate([self.halves(w, 1 - self.side) for w in shards], axis=1)
-        return here, swap(tied(away, *before), "dp", 1)
+        return here, swap(tied(away, *before), "seq", 1)
 
     def pair_weight(self, here, across):
         return in_order(here, across, self.side, 0).reshape(-1, here.shape[1])
 
-    def across_grad(self, away, here, *before):
-        return narrow(wide(tied(here, *before)) + wide(swap(away, "dp", 2)))
-
-    def scatter_grad(self, quads, widths):
+    def spread_weight(self, two, far):
+        return lax.all_gather(jnp.concatenate([two, far]), "dp", axis=0, tiled=True)
+
+    def collect_grad(self, product, *before):
+        return lax.psum_scatter(tied(product, *before), "dp", scatter_dimension=0, tiled=True)
+
+    def scatter_grad(self, fours, widths):
         mine, other = [], []
-        for quad in quads:
-            two = lax.psum_scatter(quad, "seq", scatter_dimension=0, tiled=True)
-            two = two.reshape(2, -1, quad.shape[1])
-            away = lax.dynamic_index_in_dim(two, 1 - self.side, 0, False)
-            mine.append(wide(lax.dynamic_index_in_dim(two, self.side, 0, False)))
-            other.append(wide(swap(away, "dp", 1)))
+        for four in fours:
+            half = four.shape[0] // 2
+            two = wide(four[:half]) + wide(swap(four[half:], "seq", 2))
+            two = two.reshape(2, -1, four.shape[1])
+            away = narrow(lax.dynamic_index_in_dim(two, 1 - self.side, 0, False))
+            mine.append(lax.dynamic_index_in_dim(two, self.side, 0, False))
+            other.append(wide(swap(away, "seq", 1)))
         mine, other = jnp.concatenate(mine, axis=1), jnp.concatenate(other, axis=1)
         out, at = [], 0
         for width in widths:
@@ -864,6 +848,29 @@
             out.append(part.reshape(mine.shape[0], -1))
             at += width
         return out
+
+    def in_blocks(self, values):
+        first = jnp.where(self.side == 0, values[0], values[1])
+        return first, jnp.where(self.side == 0, values[1], values[0])
+
+    def own_first(self, earlier, later):
+        return in_order(earlier, later, self.side, 0)
+
+    def states(self, own, through, reverse):
+        early, late = self.in_blocks(own)
+        kept_early, kept_late = self.in_blocks(through[..., None, None])
+        if reverse:
+            early, late, kept_early, kept_late = late, early, kept_late, kept_early
+        leaving = narrow(wide(late) + kept_late * wide(early))
+        hops = [(2, 0), (3, 1)] if reverse else [(0, 2), (1, 3)]
+        return (early, kept_early), leaving, lax.ppermute(leaving, "seq", hops)
+
+    def arrive(self, early, entering, reverse, *before):
+        state, kept = early
+        entering = tied(entering, *before)
+        inner = narrow(wide(state) + kept * wide(entering))
+        pair = (inner, entering) if reverse else (entering, inner)
+        return self.own_first(*pair)
 
 
 def paired_body(
@@ -883,15 +890,14 @@
     micro = inputs.shape[0]
     shard_len, features = inputs.shape[2:]
     block_len = shard_len * 2
-    block_start = lax.axis_index("seq") * block_len
     plan = Paired(query_weight.shape[1] // QK)
-    rows, heads, blocks = plan.rows, plan.heads, plan.blocks
+    rows, heads, groups = plan.rows, plan.heads, plan.groups
+    starts = jnp.stack([plan.block, lax.bitwise_xor(plan.block, 1)]) * block_len
     upper = plan.upper[None]
     head_index = (plan.first_head + jnp.arange(heads, dtype=jnp.int32)).astype(jnp.float32)
     log_gamma = jnp.log1p(-jnp.exp2(-5.0 - head_index))
     gain_one = wide(first_gain)[:, None]
     gain_two = wide(second_gain)[:, None]
-    row_lengths = jnp.concatenate([lengths, swap(lengths, "dp", 1)], axis=1)
 
     def scaled(weight, gain):
         return narrow(wide(weight) * gain)
@@ -908,7 +914,7 @@
     entered = [
         enter_tokens(
             upper,
-            blocks,
+            groups,
             shard_len,
             i * shard_len,
             inputs.reshape(flat),
@@ -918,38 +924,29 @@
     ]
     across = tied(across, *[e[0] for e in entered])
 
-    def spread(two, *before):
-        return lax.all_gather(tied(two, *before), "seq", axis=0, tiled=True)
-
+    def far(two, *before):
+        return swap(tied(two, *before), "seq", 2)
+
+    first_across = [swap(e[0], "seq", 1) for e in entered]
+    cot_across = [swap(e[2], "seq", 1) for e in entered]
     two_kv = plan.pair_weight(here, across)
-    cut = two_kv.shape[1] // 2
-    quads_kv = [spread(two_kv[:, :cut]), spread(two_kv[:, cut:])]
-    hidden_first = [plan.gather_tokens(e[0]) for e in entered]
+    weight_kv = plan.spread_weight(two_kv, tied(far(two_kv), first_across[0]))
     two_qg = plan.pair_weight(*plan.swap_weight(units[1], two_kv))
-    quad_qg = spread(two_qg)
-    two_o = plan.pair_weight(*plan.swap_weight(units[2], two_qg))
-    quad_o = spread(two_o)
-    quads_kv[0] = quad_kv = tied(quads_kv[0], two_o)
-    others_kv = [swap(quad_kv, "dp", 2)]
-    others_kv.append(swap(tied(quads_kv[1], *others_kv), "dp", 2))
-    two_d = plan.pair_weight(*plan.swap_weight(units[3], quad_kv))
-    two_u = plan.pair_weight(*plan.swap_weight(units[4], two_d))
-    grad_rows = [plan.gather_tokens(tied(e[2], quad_kv)) for e in entered]
-    others_kv[1] = tied(others_kv[1], two_u)
-    other_qg = swap(tied(quad_qg, others_kv[1]), "dp", 2)
-    other_o = swap(tied(quad_o, other_qg), "dp", 2)
-    weight_kv = join(*zip(quads_kv, others_kv))
-    weight_qg = join((quad_qg, other_qg))
-    weight_o = join((quad_o, other_o))
-
-    def row_plan(lengths_row):
-        documents, places = layout(lengths_row, block_start, block_len)
-        previous, unused = layout(lengths_row, block_start - 1, 1)
+    far_qg = tied(far(two_qg), first_across[1])
+    weight_qg = plan.spread_weight(two_qg, far_qg)
+    hidden_first = [plan.gather_from(e[0], a) for e, a in zip(entered, first_across)]
+    two_o = plan.pair_weight(*plan.swap_weight(units[2], far_qg))
+
+    def row_plan(start, lengths_row):
+        documents, places = layout(lengths_row, start, block_len)
+        previous, unused = layout(lengths_row, start - 1, 1)
         return (documents, places, previous[0])
 
     kernels, throughs = [], []
     for i in range(micro):
-        documents, places, previous = jax.vmap(row_plan)(row_lengths[i])
+        documents, places, previous = jax.vmap(row_plan, in_axes=(0, None))(
+            starts, lengths[i, 0]
+        )
         tables = [
             table.reshape(rows, block_len, QK // 2)
             for sign in (1.0, -1.0)
@@ -971,122 +968,136 @@
     def product_t(values, weight):
         return lambda away: narrow(matmul_t(rows_of(values, away), weight))
 
-    def products(left, right, columns=slice(None)):
-        middle = features // 2
-        return [
-            narrow(sum(tmatmul(left[i][:, rows_cut], right[i][:, columns]) for i in each))
-            for rows_cut in (slice(middle, None), slice(None, middle))
-        ]
-
-    def first_product(i):
-        def run(away):
-            part = matmul_t(rows_of(first_qg[i], away), weight_qg)
-            return narrow(part + matmul_t(rows_of(first_kv[i], away), weight_kv))
-
-        return run
+    def product(left, right, columns=slice(None)):
+        return narrow(sum(tmatmul(left[i], right[i][:, columns]) for i in each))
 
     kv_pre = [matmul(hidden_first[i], weight_kv) for i in each]
     kvs = [kernels[0].keys(kv_pre[0])]
-    kv_pre[1] = tied(kv_pre[1], *grad_rows, kvs[0][2])
+    kv_pre[1] = tied(kv_pre[1], kvs[0][2])
     kvs.append(kernels[1].keys(kv_pre[1]))
-    qg_pre = [matmul(hidden_first[i], weight_qg) for i in each]
-    ties = [{}, {2: (other_qg,), 3: (other_o,)}]
-    states = [pass_on(kvs[i][2], throughs[i], False, ties[i]) for i in each]
-    quad_d = spread(two_d)
-    quad_u = spread(two_u, states[0][1])
-    other_d = swap(tied(quad_d, other_o), "dp", 2)
-    other_u = swap(tied(quad_u, other_d), "dp", 2)
-    weight_d = join((quad_d, other_d))
-    weight_u = join((quad_u, other_u))
+    passing = [plan.states(kvs[i][2], throughs[i], False) for i in each]
+    far_o = tied(far(two_o), kvs[1][2], cot_across[0])
+    weight_o = plan.spread_weight(two_o, far_o)
+    two_d = plan.pair_weight(*plan.swap_weight(units[3], far_o))
+    qg_pre = [matmul(tied(hidden_first[i], two_d), weight_qg) for i in each]
+    far_d = tied(far(two_d), qg_pre[1], cot_across[1])
+    weight_d = plan.spread_weight(two_d, far_d)
+    two_u = plan.pair_weight(*plan.swap_weight(units[4], far_d))
+    grad_rows = [plan.gather_from(e[2], a) for e, a in zip(entered, cot_across)]
+
+    def held(parts, *before):
+        return (parts[0], parts[1], tied(parts[2], *before))
+
     mixes, attn, state_in = [], [], []
-    before = (*qg_pre, other_o)
     for i in each:
-        state_in.append(arrive(states[i], *before))
+        early, leaving, entering = passing[i]
+        state_in.append(plan.arrive(early, entering, False, two_u))
         mixes.append(kernels[i].mix(qg_pre[i], kvs[i][0], kvs[i][1], state_in[i]))
-        parts, here, across = plan.scatter_tokens(product_t(mixes[i][1], weight_o))
+    far_u = tied(far(two_u), mixes[1][1])
+    weight_u = plan.spread_weight(two_u, far_u)
+    before = (far_u,)
+    for i in each:
+        source = tied(mixes[i][1], *before)
+        parts, here, across = plan.scatter_tokens(product_t(source, weight_o))
         attn.append(parts)
-        before = (here,)
-    residual = [e[1] for e in entered]
+        before = (across,)
+    middles = [middle_tokens(upper, entered[0][1], attn[0])]
     grad_act = [matmul(grad_rows[i], weight_d) for i in each]
-    residual[0] = tied(residual[0], other_d)
-    residual[1] = tied(residual[1], *grad_act)
-    middles = [middle_tokens(upper, residual[i], attn[i]) for i in each]
-    hidden_second = [plan.gather_tokens(middles[i][1]) for i in each]
-    up_pre = [matmul(hidden_second[i], weight_u) for i in each]
-    activated = [narrow(gelu_exact(up_pre[i])) for i in each]
-    grad_up_pre = [
-        narrow(jax.vjp(gelu_exact, up_pre[i])[1](grad_act[i])[0]) for i in each
-    ]
-    second, before = [], ()
-    for i in each:
-        product = product_t(tied(grad_up_pre[i], *before), weight_u)
-        parts, here, across = plan.scatter_tokens(product)
-        second.append(parts)
-        before = (across,)
-    down_products = products(grad_rows, [tied(a, here) for a in activated])
-    middles[0] = (tied(middles[0][0], across), middles[0][1])
-    grad_middle = [
-        back_middle(upper, middles[i][0], entered[i][2], second[i]) for i in each
-    ]
-    up_products = products(
-        hidden_second, [tied(g, grad_middle[0][1]) for g in grad_up_pre]
-    )
-    quad_down = plan.across_grad(*down_products, grad_middle[0][1])
-    quad_up = plan.across_grad(*up_products, grad_middle[1][1])
-    grad_attn, backs = [], []
+    hidden_second, activated, grad_up_pre, second = [], [], [], []
     before = ()
     for i in each:
-        grad_attn.append(plan.gather_tokens(grad_middle[i][1], *before))
-        source = tied(grad_attn[i], grad_middle[1][1])
-        grad_mixed = tied(matmul(source, weight_o), *((quad_down, quad_up) if i else ()))
+        if i:
+            attn[1] = held(attn[1], *before)
+            middles.append(middle_tokens(upper, entered[1][1], attn[1]))
+        hidden_second.append(plan.gather_tokens(middles[i][1]))
+        source = tied(hidden_second[i], *((across,) if i else grad_act))
+        up_pre = matmul(source, weight_u)
+        activated.append(narrow(gelu_exact(up_pre)))
+        grad_up_pre.append(narrow(jax.vjp(gelu_exact, up_pre)[1](grad_act[i])[0]))
+        if i:
+            second[0] = held(second[0], activated[1])
+            grad_middle = [back_middle(upper, middles[0][0], entered[0][2], second[0])]
+            towards = product_t(tied(grad_up_pre[1], grad_middle[0][1]), weight_u)
+        else:
+            towards = product_t(grad_up_pre[0], weight_u)
+        parts, here, across = plan.scatter_tokens(towards)
+        second.append(parts)
+        before = (here,)
+    down_product = product(grad_rows, [tied(a, here) for a in activated])
+    down_four = plan.collect_grad(down_product)
+    grad_attn = [plan.gather_tokens(grad_middle[0][1], down_product)]
+    grad_mixed = matmul(grad_attn[0], weight_o)
+    second[1] = held(second[1], grad_mixed)
+    grad_middle.append(back_middle(upper, middles[1][0], entered[1][2], second[1]))
+    backs = []
+    for i in each:
         kv = kvs[i]
+        source = tied(grad_mixed, down_four if i else grad_middle[1][1])
         backs.append(
-            kernels[i].back(qg_pre[i], grad_mixed, mixes[i][0], kv[0], kv[1], state_in[i])
-        )
-        before = (backs[i][1],)
+            kernels[i].back(qg_pre[i], source, mixes[i][0], kv[0], kv[1], state_in[i])
+        )
+        if not i:
+            up_product = product(
+                hidden_second, [tied(g, backs[0][1]) for g in grad_up_pre]
+            )
+            grad_attn.append(plan.gather_tokens(grad_middle[1][1], up_product))
+            grad_mixed = matmul(grad_attn[1], weight_o)
     after_back = backs[-1][1]
+    up_four = plan.collect_grad(up_product)
     grad_qg_pre = [b[0].reshape(-1, b[0].shape[-1]) for b in backs]
-    out_products = products(grad_attn, [tied(m[1], after_back) for m in mixes])
-    qg_products = products(hidden_first, [tied(g, out_products[1]) for g in grad_qg_pre])
-    late = [tied(a, after_back) for a in activated]
+    passing = [plan.states(backs[i][1], throughs[i], True) for i in each]
+    out_product = product(grad_attn, [tied(m[1], after_back) for m in mixes])
+    out_four = plan.collect_grad(out_product)
+    qg_product = product(hidden_first, [tied(g, out_product) for g in grad_qg_pre])
+    qg_four = plan.collect_grad(qg_product)
+    state_out = []
+    before = (qg_product, up_four)
+    for i in each:
+        early, leaving, entering = passing[i]
+        state_out.append(plan.arrive(early, entering, True, *before))
+    late = [tied(a, qg_product) for a in activated]
     ffn = [plan.scatter_tokens(product_t(late[i], weight_d)) for i in each]
-    states = [
-        pass_on(backs[i][1], throughs[i], True, {2: (out_products[i],), 3: (qg_products[i],)})
-        for i in each
-    ]
-    state_out = [arrive(states[i], ffn[0][1], ffn[1][1]) for i in each]
     outputs = grad_inputs = None
     for i in each:
         into = (outputs, i * shard_len, flat[0])
-        outputs = output_tokens(upper, blocks, middles[i][0], ffn[i][0], into)
+        outputs = output_tokens(upper, groups, middles[i][0], ffn[i][0], into)
     grad_kv_pre = [
         kernels[i].back_keys(kvs[i][0], kvs[i][1], state_out[i], backs[i][2], backs[i][3])
         for i in each
     ]
     cut = grad_kv_pre[0].shape[1] // 2
     kv_products = [
-        products(hidden_first, grad_kv_pre, columns)
+        product(hidden_first, grad_kv_pre, columns)
         for columns in (slice(None, cut), slice(cut, None))
     ]
-    first_qg = [tied(g, kv_products[1][1]) for g in grad_qg_pre]
-    first_kv = [tied(g, kv_products[1][1]) for g in grad_kv_pre]
-    first = [plan.scatter_tokens(first_product(i))[0] for i in each]
+    kv_fours = [
+        plan.collect_grad(kv_products[0], out_four),
+        plan.collect_grad(kv_products[1], qg_four),
+    ]
+    first = []
+    for i in each:
+        first_kv = tied(grad_kv_pre[i], *kv_products)
+
+        def first_product(away):
+            part = matmul_t(rows_of(grad_qg_pre[i], away), weight_qg)
+            return narrow(part + matmul_t(rows_of(first_kv, away), weight_kv))
+
+        first.append(plan.scatter_tokens(first_product)[0])
     for i in each:
         into = (grad_inputs, i * shard_len, flat[0])
         grad_inputs = back_inputs(
-            upper, blocks, entered[i][1], grad_middle[i][0], first[i], into
+            upper, groups, entered[i][1], grad_middle[i][0], first[i], into
         )
 
     width_q, width_v = heads * QK, heads * HV
     width_f = up_weight.shape[1] // 2
-    grad_down = plan.scatter_grad([quad_down], [width_f])[0]
-    grad_up = plan.scatter_grad([quad_up], [width_f])[0]
-    quad_out = plan.across_grad(*out_products, state_out[0])
-    grad_out = plan.scatter_grad([quad_out], [width_v])[0]
-    quad_qg = plan.across_grad(*qg_products, *state_out)
-    grad_query, grad_gate = plan.scatter_grad([quad_qg], [width_q, width_v])
-    quads_kv = [plan.across_grad(*p) for p in kv_products]
-    grad_key, grad_value = plan.scatter_grad(quads_kv, [width_q, width_v])
+
+    wide_four = jnp.concatenate([down_four, up_four, out_four], axis=1)
+    grad_down, grad_up, grad_out = plan.scatter_grad([wide_four], [width_f, width_f, width_v])
+    grad_query, grad_gate = plan.scatter_grad([qg_four], [width_q, width_v])
+    grad_key, grad_value = plan.scatter_grad(
+        [jnp.concatenate(kv_fours, axis=1)], [width_q, width_v]
+    )
 
     def along(weight, grad):
         return jnp.sum(wide(weight) * grad, axis=1)
@@ -1118,11 +1129,11 @@
 
 def body(inputs, lengths, first_gain, second_gain, query_weight, *rest):
     paired = (
-        lax.axis_size("dp") == 4
+        lax.axis_size("seq") == 4
         and lax.axis_size("tensor") == 2
         and inputs.shape[1] == 1
         and query_weight.shape[1] % (2 * QK) == 0
-        and inputs.shape[3] % (4 * lax.axis_size("seq") * LANES) == 0
+        and query_weight.shape[0] % LANES == 0
         and inputs.shape[2] % ROWS_STEP == 0
     )
     run = paired_body if paired else plain_body

time: 1130 us -> 1060 us (0.938)
  waiting for transfers between devices: 432 us -> 374 us
  matrix products: 271 us -> 311 us
  other arithmetic: 103 us -> 66.9 us
  Pallas kernels: 159 us -> 134 us
  starting transfers between devices: 67 us -> 90 us
  local copies, waits for them, and re-layouts: 67.1 us -> 54.9 us
    ppermute x12 -> x4, waiting for transfers between devices: 115 us -> 5.43 us  [states(): return ((early, kept_early), leaving, lax.ppermute(leaving, 'seq', hops))]
    ppermute x64 -> x56, waiting for transfers between devices: 263 us -> 348 us  [swap(): lax.ppermute(values, axis, [(i, i ^ bit) for i in range(lax.axis_size(axi...]
    ppermute x64 -> x56, starting transfers between devices: 44.4 us -> 80.5 us  [swap(): lax.ppermute(values, axis, [(i, i ^ bit) for i in range(lax.axis_size(axi...]
    convert_element_type x27 -> x17, other arithmetic: 64.1 us -> 31 us  [narrow(): return values.astype(jnp.bfloat16)]
    all_gather x6 -> x5, waiting for transfers between devices: 53.3 us -> 21 us  [spread_weight(): return lax.all_gather(jnp.concatenate([two, far]), 'dp', axis=0, tiled=True)]
    pallas_call x13 -> x8, Pallas kernels: 43.6 us -> 23.5 us  [join(): pl.pallas_call(kernel, out_shape=jax.ShapeDtypeStruct(shape, dtype), in_s...]
    dot_general x10, matrix products: 107 us -> 125 us  [matmul(): return jnp.dot(left_side, right_side, preferred_element_type=jnp.float32)]
    dot_general x20, matrix products: 85.2 us -> 99.8 us  [matmul_t(): lax.dot_general(left_side, right_side, (((1,), (1,)), ((), ())), preferre...]
  transfers between devices with their start and end apart: 88 -> 71, of which waited for: 28 -> 26; matrix products, arithmetic and copies ran while one was open for 34% -> 36% of each run, Pallas kernels for 14% -> 12%
where the time goes in v2:
time: 1060 us; the launch traced here: 1050 us
  waiting for transfers between devices  374 us (35%)
  matrix products  311 us (29%)
  Pallas kernels  134 us (13%)
  starting transfers between devices  90 us (8%)
  other arithmetic  66.9 us (6%)
  local copies, waits for them, and re-layouts  54.9 us (5%)
  between operations  16.7 us (2%)
    ppermute x56, waiting for transfers between devices, swap(): lax.ppermute(values, axis, [(i, i ^ bit) for i in range(lax.axis_size(axi...  348 us
    dot_general x10, matrix products, matmul(): return jnp.dot(left_side, right_side, preferred_element_type=jnp.float32)  125 us
    pallas_call x18, Pallas kernels, call(): pl.pallas_call(kernel, out_shape=out_shape, grid_spec=pltpu.PrefetchScala...  111 us
    dot_general x20, matrix products, matmul_t(): lax.dot_general(left_side, right_side, (((1,), (1,)), ((), ())), preferre...  99.8 us
    dot_general x12, matrix products, tmatmul(): lax.dot_general(left_side, right_side, (((0,), (0,)), ((), ())), preferre...  85.5 us
    ppermute x56, starting transfers between devices, swap(): lax.ppermute(values, axis, [(i, i ^ bit) for i in range(lax.axis_size(axi...  80.5 us
    convert_element_type x17, other arithmetic, narrow(): return values.astype(jnp.bfloat16)  31 us
    unnamed x311, local copies, waits for them, and re-layouts  25.9 us
  transfers between devices with their start and end apart: 71, of which 26 were waited for; matrix products, arithmetic and copies ran while one was open for 36% of the time, Pallas kernels for 12%

profile of v2, /device:TPU:0, one launch (start us, length us, event | category | flops | bytes accessed | tf_op | source)
XLA Modules:
  0.0 1051.1 jit_solution(9932270143599851226)
XLA Ops:
  31.6 33.3 %collective-permute-done.9.refs_1_ = bf16[256,2048]{1,0:T(8,128)(2,1)} collective-permute-done((bf16[256,2048]{1,0:T(8,128)(2,1)S(1)}, bf16[256,2048]{1,0:T(8,128)(2,1)}, u32[]{:S(2)}, u32[]{:S(2)}) %collective-permute-start.9) | collective-permute-done | bytes 1048608 | tf_op jit(solution)/shard_map/ppermute | solution.py:341
  69.2 9.9 collective-permute-done.4
  79.2 10.2 collective-permute-start.5
  89.4 27.3 %collective-permute-done.refs_1_ = bf16[256,2048]{1,0:T(8,128)(2,1)} collective-permute-done((bf16[256,2048]{1,0:T(8,128)(2,1)}, bf16[256,2048]{1,0:T(8,128)(2,1)}, u32[]{:S(2)}, u32[]{:S(2)}) %collective-permute-start) | collective-permute-done | bytes 1048608 | tf_op jit(solution)/shard_map/ppermute | solution.py:341
  122.6 5.7 fusion.60
  141.9 12.0 %fusion.97 = f32[1024,1536]{1,0:T(8,128)} fusion(bf16[1024,2048]{1,0:T(8,128)(2,1)} %shard_map.204, bf16[2048,1536]{1,0:T(8,128)(2,1)} %all-gather.6.cloned.1.call-done), kind=kOutput, calls=%fused_computation.290 | convolution fusion | flops 6442450944 | bytes 16777216 | tf_op jit(solution)/shard_map/dot_general | solution.py:96
  153.9 8.6 fusion.98
  181.9 7.2 collective-permute-done.13
  190.1 20.9 %all-gather.8.cloned.1.call-done = bf16[2048,1536]{1,0:T(8,128)(2,1)} async-done(((bf16[512,1536]{1,0:T(8,128)(2,1)}), bf16[2048,1536]{1,0:T(8,128)(2,1)}) %all-gather.8.cloned.1.call-update) | async-done | bytes 6291472 | tf_op jit(solution)/shard_map/all_gather | solution.py:830
  211.0 11.7 %fusion.99 = f32[1024,1536]{1,0:T(8,128)} fusion(bf16[1024,2048]{1,0:T(8,128)(2,1)} %shard_map.204, bf16[2048,1536]{1,0:T(8,128)(2,1)} %all-gather.8.cloned.1.call-done), kind=kOutput, calls=%fused_computation.292 | convolution fusion | flops 6442450944 | bytes 16777216 | tf_op jit(solution)/shard_map/dot_general | solution.py:96
  236.4 10.6 %fusion.100 = f32[1024,1536]{1,0:T(8,128)} fusion(bf16[1024,2048]{1,0:T(8,128)(2,1)S(1)} %copy-done.70, bf16[2048,1536]{1,0:T(8,128)(2,1)} %all-gather.8.cloned.1.call-done), kind=kOutput, calls=%fused_computation.293 | convolution fusion | flops 6442450944 | bytes 16777216 | tf_op jit(solution)/shard_map/dot_general | solution.py:96
  247.0 14.6 %collective-permute-done.17 = bf16[128,1024]{1,0:T(8,128)(2,1)S(1)} collective-permute-done((bf16[128,1024]{1,0:T(8,128)(2,1)S(1)}, bf16[128,1024]{1,0:T(8,128)(2,1)S(1)}, u32[]{:S(2)}, u32[]{:S(2)}) %collective-permute-start.17) | collective-permute-done | bytes 262176 | tf_op jit(solution)/shard_map/ppermute | solution.py:341
  262.3 8.9 shard_map.209
  272.8 9.0 shard_map.210
  283.7 6.3 convolution_convert_fusion.10
  311.4 32.3 %collective-permute-start.23 = (bf16[256,2048]{1,0:T(8,128)(2,1)}, bf16[256,2048]{1,0:T(8,128)(2,1)}, u32[]{:S(2)}, u32[]{:S(2)}) collective-permute-start(bf16[256,2048]{1,0:T(8,128)(2,1)} %add_convert_fusion.19), channel_id=1, source_target_pairs={{0,2},{2,0},{4,6},{6,4},{1,3},{3,1},{5,7},{7,5},{8,10},{10,8},{12,... | collective-permute-start | bytes 3145736 | tf_op jit(solution)/shard_map/ppermute | solution.py:341
  347.4 10.1 fusion.102
  359.1 8.5 collective-permute-done.23.c
  373.2 8.6 fusion.101
  381.8 14.3 %collective-permute-done.24.refs_1_ = bf16[256,2048]{1,0:T(8,128)(2,1)S(1)} collective-permute-done((bf16[256,2048]{1,0:T(8,128)(2,1)S(1)}, bf16[256,2048]{1,0:T(8,128)(2,1)S(1)}, u32[]{:S(2)}, u32[]{:S(2)}) %collective-permute-start.24) | collective-permute-done | bytes 1048608 | tf_op jit(solution)/shard_map/ppermute | solution.py:341
  408.3 17.1 %multiply_convert_fusion = (bf16[1024,1024]{1,0:T(8,128)(2,1)}, f32[1024,1024]{1,0:T(8,128)S(1)}, f32[1024,1024]{1,0:T(8,128)S(1)}) fusion(bf16[1024,2048]{1,0:T(8,128)(2,1)} %shard_map.212, bf16[2048,1024]{1,0:T(8,128)(2,1)} %all-gather.14.cloned.1.call-done), kind=kOutput, calls=%fused_computation.15 | convolution fusion | flops 4363124736 | bytes 18874368 | tf_op jit(solution)/shard_map/dot_general | solution.py:96
  438.4 24.7 %collective-permute-done.31.refs_1_ = bf16[256,2048]{1,0:T(8,128)(2,1)S(1)} collective-permute-done((bf16[256,2048]{1,0:T(8,128)(2,1)S(1)}, bf16[256,2048]{1,0:T(8,128)(2,1)S(1)}, u32[]{:S(2)}, u32[]{:S(2)}) %collective-permute-start.31) | collective-permute-done | bytes 1048608 | tf_op jit(solution)/shard_map/ppermute | solution.py:341
  468.2 28.3 %add_convert_fusion.10 = (bf16[1024,1024]{1,0:T(8,128)(2,1)}, f32[1024,1024]{1,0:T(8,128)S(1)}, f32[1024,1024]{1,0:T(8,128)S(1)}) fusion(f32[1024,1024]{1,0:T(8,128)} %fusion.102, bf16[1024,2048]{1,0:T(8,128)(2,1)} %shard_map.216, bf16[2048,1024]{1,0:T(8,128)(2,1)} %all-gather.14.cloned.1.call-done), kind=kOutput, calls=%fused_computation.14 | convolution fusion | flops 4370464768 | bytes 23068672 | tf_op jit(solution)/shard_map/dot_general | solution.py:96
  499.0 5.1 shard_map.217
  504.1 5.4 convolution_convert_fusion.5
  509.5 4.7 fusion.103
  514.2 6.2 add_convert_fusion.3
  520.5 5.0 convolution_convert_fusion.4
  526.8 24.4 %collective-permute-done.36.refs_1_ = bf16[256,2048]{1,0:T(8,128)(2,1)S(1)} collective-permute-done((bf16[256,2048]{1,0:T(8,128)(2,1)S(1)}, bf16[256,2048]{1,0:T(8,128)(2,1)S(1)}, u32[]{:S(2)}, u32[]{:S(2)}) %collective-permute-start.36) | collective-permute-done | bytes 1048608 | tf_op jit(solution)/shard_map/ppermute | solution.py:341
  556.6 10.1 fusion.104
  566.7 10.5 %collective-permute-done.40.c = bf16[256,2048]{1,0:T(8,128)(2,1)S(1)} collective-permute-done((bf16[256,2048]{1,0:T(8,128)(2,1)S(1)}, bf16[256,2048]{1,0:T(8,128)(2,1)S(1)}, u32[]{:S(2)}, u32[]{:S(2)}) %collective-permute-start.40) | collective-permute-done | bytes 1048608 | tf_op jit(solution)/shard_map/ppermute | solution.py:341
  577.3 4.7 shard_map.219
  583.0 17.1 %shard_map.220 = (bf16[2,2,256,1536]{3,2,1,0:T(8,128)(2,1)}, bf16[2,2,256,512]{3,2,1,0:T(8,128)(2,1)S(1)}, f32[2,2,512,256]{3,2,1,0:T(8,128)}, f32[2,2,512,512]{3,2,1,0:T(8,128)}) custom-call(s32[5]{0:T(128)S(1)} %pad_add_fusion.1.numbers, f32[2]{0:T(128)S(1)} %negate_log-plus-one_fusion.log_gamma, f32[2,2,256,1536]{3,2,1,0:T(8,128)} %bitcast.243, ...), custom_call_target="tpu_custom_call" | custom-call | tf_op jit(solution)/shard_map/pallas_call | solution.py:431
  600.1 7.0 fusion.105
  607.1 8.5 add_convert_fusion.2
  617.9 23.8 %collective-permute-done.41.refs_1_ = bf16[256,2048]{1,0:T(8,128)(2,1)S(1)} collective-permute-done((bf16[256,2048]{1,0:T(8,128)(2,1)S(1)}, bf16[256,2048]{1,0:T(8,128)(2,1)S(1)}, u32[]{:S(2)}, u32[]{:S(2)}) %collective-permute-start.41) | collective-permute-done | bytes 1048608 | tf_op jit(solution)/shard_map/ppermute | solution.py:341
  646.7 8.4 fusion.106
  657.4 17.1 %shard_map.222 = (bf16[2,2,256,1536]{3,2,1,0:T(8,128)(2,1)}, bf16[2,2,256,512]{3,2,1,0:T(8,128)(2,1)S(1)}, f32[2,2,512,256]{3,2,1,0:T(8,128)}, f32[2,2,512,512]{3,2,1,0:T(8,128)}) custom-call(s32[5]{0:T(128)S(1)} %pad_add_fusion.numbers, f32[2]{0:T(128)S(1)} %negate_log-plus-one_fusion.log_gamma, f32[2,2,256,1536]{3,2,1,0:T(8,128)} %bitcast.241, ...), custom_call_target="tpu_custom_call" | custom-call | tf_op jit(solution)/shard_map/pallas_call | solution.py:431
  674.5 6.8 fusion.107
  681.4 8.3 add_convert_fusion.1
  691.6 12.4 %fusion.108 = f32[2048,1536]{1,0:T(8,128)} fusion(bf16[1024,2048]{1,0:T(8,128)(2,1)} %shard_map.204, bf16[1024,1536]{1,0:T(8,128)(2,1)S(1)} %bitcast.262), kind=kOutput, calls=%fused_computation.301 | convolution fusion | flops 6442450944 | bytes 19922944 | tf_op jit(solution)/shard_map/dot_general | solution.py:106
  704.0 11.8 %add_convert_fusion = bf16[2048,1536]{1,0:T(8,128)(2,1)} fusion(f32[2048,1536]{1,0:T(8,128)} %fusion.108, bf16[1024,2048]{1,0:T(8,128)(2,1)S(1)} %copy-done.71, bf16[1024,1536]{1,0:T(8,128)(2,1)S(1)} %bitcast.261), kind=kOutput, calls=%fused_computation | convolution fusion | flops 6448742400 | bytes 26214400 | tf_op jit(solution)/shard_map/dot_general | solution.py:106
  720.9 7.9 fusion.111
  728.9 5.0 fusion.112
  748.4 5.2 fusion.109
  753.6 5.0 fusion.110
  762.3 5.4 collective-permute-done.48
  772.6 5.9 shard_map.226
  779.9 5.7 shard_map.225
  785.7 5.2 fusion.15
  791.0 5.4 add_convert_fusion.5
  809.7 5.4 add_convert_fusion.4
  815.2 9.3 add_convert_fusion.8
  824.5 8.4 add_convert_fusion.6
  833.8 4.7 add_convert_fusion.7
  842.7 8.1 add_convert_fusion.9
  858.9 54.1 %collective-permute-done.58 = bf16[256,3072]{1,0:T(8,128)(2,1)} collective-permute-done((bf16[256,3072]{1,0:T(8,128)(2,1)}, bf16[256,3072]{1,0:T(8,128)(2,1)}, u32[]{:S(2)}, u32[]{:S(2)}) %collective-permute-start.58) | collective-permute-done | bytes 1572896 | tf_op jit(solution)/shard_map/ppermute | solution.py:341
  933.2 4.8 shard_map.227.refs_6_
  938.1 4.9 shard_map.228
  943.2 5.7 collective-permute-done.59
  954.3 31.1 %collective-permute-done.54 = bf16[256,1536]{1,0:T(8,128)(2,1)S(1)} collective-permute-done((bf16[256,1536]{1,0:T(8,128)(2,1)S(1)}, bf16[256,1536]{1,0:T(8,128)(2,1)S(1)}, u32[]{:S(2)}, u32[]{:S(2)}) %collective-permute-start.54) | collective-permute-done | bytes 786464 | tf_op jit(solution)/shard_map/ppermute | solution.py:341
  991.0 10.8 %collective-permute-done.55 = bf16[128,1536]{1,0:T(8,128)(2,1)S(1)} collective-permute-done((bf16[128,1536]{1,0:T(8,128)(2,1)}, bf16[128,1536]{1,0:T(8,128)(2,1)S(1)}, u32[]{:S(2)}, u32[]{:S(2)}) %collective-permute-start.55) | collective-permute-done | bytes 393248 | tf_op jit(solution)/shard_map/ppermute | solution.py:341
  1002.2 24.2 %collective-permute-done.56 = bf16[256,1536]{1,0:T(8,128)(2,1)S(1)} collective-permute-done((bf16[256,1536]{1,0:T(8,128)(2,1)S(1)}, bf16[256,1536]{1,0:T(8,128)(2,1)S(1)}, u32[]{:S(2)}, u32[]{:S(2)}) %collective-permute-start.56) | collective-permute-done | bytes 786464 | tf_op jit(solution)/shard_map/ppermute | solution.py:341
  1026.9 10.1 collective-permute-done.57
  (612 shorter events, 264.4 us)
Async XLA Ops:
  7.2 134.7 %all-gather.6.cloned.1.call-start = ((), (), s32[]{:S(2)}) async-start(), calls=%async_computation.6 | async-start | bytes 7864320 | tf_op jit(solution)/shard_map/all_gather | solution.py:830
  13.2 14.0 %collective-permute-start.3 = (bf16[128,1536]{1,0:T(8,128)(2,1)}, bf16[128,1536]{1,0:T(8,128)(2,1)}, u32[]{:S(2)}, u32[]{:S(2)}) collective-permute-start(bf16[128,1536]{1,0:T(8,128)(2,1)} %pad_maximum_fusion.6), channel_id=1, source_target_pairs={{0,2},{2,0},{4,6},{6,4},{1,3},{3,1},{5,7},{7,5},{8,10},{10,8},{12,... | collective-permute-start | bytes 1179656 | tf_op jit(solution)/shard_map/ppermute | solution.py:341
  21.2 43.8 %collective-permute-start.9 = (bf16[256,2048]{1,0:T(8,128)(2,1)S(1)}, bf16[256,2048]{1,0:T(8,128)(2,1)}, u32[]{:S(2)}, u32[]{:S(2)}) collective-permute-start(bf16[256,2048]{1,0:T(8,128)(2,1)S(1)} %get-tuple-element.88.refs_0_), channel_id=1, source_target_pairs={{0,2},{2,0},{4,6},{6,4},{1,3},{3,1},{5,7},{7,5},{8,10},{10,8},{12,... | collective-permute-start | bytes 3145736 | tf_op jit(solution)/shard_map/ppermute | solution.py:341
  28.5 36.4 %collective-permute-start.8 = (bf16[256,1536]{1,0:T(8,128)(2,1)S(1)}, bf16[256,1536]{1,0:T(8,128)(2,1)S(1)}, u32[]{:S(2)}, u32[]{:S(2)}) collective-permute-start(bf16[256,1536]{1,0:T(8,128)(2,1)S(1)} %bitcast.263), channel_id=1, source_target_pairs={{0,4},{2,6},{4,0},{6,2},{1,5},{3,7},{5,1},{7,3},{8,12},{10,14},{12... | collective-permute-start | bytes 2359304 | tf_op jit(solution)/shard_map/ppermute | solution.py:341
  66.2 144.8 %all-gather.8.cloned.1.call-start = ((), (), s32[]{:S(2)}) async-start(), calls=%async_computation.7 | async-start | bytes 7864320 | tf_op jit(solution)/shard_map/all_gather | solution.py:830
  66.3 12.7 %collective-permute-start.4 = (bf16[128,1536]{1,0:T(8,128)(2,1)S(1)}, bf16[128,1536]{1,0:T(8,128)(2,1)S(1)}, u32[]{:S(2)}, u32[]{:S(2)}) collective-permute-start(bf16[128,1536]{1,0:T(8,128)(2,1)S(1)} %pad_maximum_fusion.5), channel_id=1, source_target_pairs={{0,2},{2,0},{4,6},{6,4},{1,3},{3,1},{5,7},{7,5},{8,10},{10,8},{12,... | collective-permute-start | bytes 1179656 | tf_op jit(solution)/shard_map/ppermute | solution.py:341
  69.1 47.7 %collective-permute-start = (bf16[256,2048]{1,0:T(8,128)(2,1)}, bf16[256,2048]{1,0:T(8,128)(2,1)}, u32[]{:S(2)}, u32[]{:S(2)}) collective-permute-start(bf16[256,2048]{1,0:T(8,128)(2,1)} %get-tuple-element.87.refs_0_), channel_id=1, source_target_pairs={{0,2},{2,0},{4,6},{6,4},{1,3},{3,1},{5,7},{7,5},{8,10},{10,8},{12,... | collective-permute-start | bytes 3145736 | tf_op jit(solution)/shard_map/ppermute | solution.py:341
  79.2 37.5 %collective-permute-start.5 = (bf16[256,1536]{1,0:T(8,128)(2,1)S(1)}, bf16[256,1536]{1,0:T(8,128)(2,1)S(1)}, u32[]{:S(2)}, u32[]{:S(2)}) collective-permute-start(bf16[256,1536]{1,0:T(8,128)(2,1)S(1)} %bitcast.265), channel_id=1, source_target_pairs={{0,4},{2,6},{4,0},{6,2},{1,5},{3,7},{5,1},{7,3},{8,12},{10,14},{12... | collective-permute-start | bytes 2359304 | tf_op jit(solution)/shard_map/ppermute | solution.py:341
  118.0 165.7 %all-gather.10.cloned.1.call-start = ((), (), s32[]{:S(2)}) async-start(), calls=%async_computation.8 | async-start | bytes 5242880 | tf_op jit(solution)/shard_map/all_gather | solution.py:830
  118.1 13.7 %collective-permute-start.10 = (bf16[256,2048]{1,0:T(8,128)(2,1)S(1)}, bf16[256,2048]{1,0:T(8,128)(2,1)}, u32[]{:S(2)}, u32[]{:S(2)}) collective-permute-start(bf16[256,2048]{1,0:T(8,128)(2,1)S(1)} %get-tuple-element.88.refs_0_), channel_id=1, source_target_pairs={{0,1},{1,0},{2,3},{3,2},{4,5},{5,4},{6,7},{7,6},{8,9},{9,8},{10,11... | collective-permute-start | bytes 3145736 | tf_op jit(solution)/shard_map/ppermute | solution.py:341
  118.1 20.4 %collective-permute-start.1 = (bf16[256,2048]{1,0:T(8,128)(2,1)}, bf16[256,2048]{1,0:T(8,128)(2,1)}, u32[]{:S(2)}, u32[]{:S(2)}) collective-permute-start(bf16[256,2048]{1,0:T(8,128)(2,1)} %get-tuple-element.87.refs_0_), channel_id=1, source_target_pairs={{0,1},{1,0},{2,3},{3,2},{4,5},{5,4},{6,7},{7,6},{8,9},{9,8},{10,11... | collective-permute-start | bytes 3145736 | tf_op jit(solution)/shard_map/ppermute | solution.py:341
  119.8 15.3 %collective-permute-start.11 = (bf16[256,2048]{1,0:T(8,128)(2,1)}, bf16[256,2048]{1,0:T(8,128)(2,1)}, u32[]{:S(2)}, u32[]{:S(2)}) collective-permute-start(bf16[256,2048]{1,0:T(8,128)(2,1)} %collective-permute-done.9.refs_1_), channel_id=1, source_target_pairs={{0,1},{1,0},{2,3},{3,2},{4,5},{5,4},{6,7},{7,6},{8,9},{9,8},{10,11... | collective-permute-start | bytes 3145736 | tf_op jit(solution)/shard_map/ppermute | solution.py:341
  119.9 18.6 %collective-permute-start.2 = (bf16[256,2048]{1,0:T(8,128)(2,1)}, bf16[256,2048]{1,0:T(8,128)(2,1)}, u32[]{:S(2)}, u32[]{:S(2)}) collective-permute-start(bf16[256,2048]{1,0:T(8,128)(2,1)} %collective-permute-done.refs_1_), channel_id=1, source_target_pairs={{0,1},{1,0},{2,3},{3,2},{4,5},{5,4},{6,7},{7,6},{8,9},{9,8},{10,11... | collective-permute-start | bytes 3145736 | tf_op jit(solution)/shard_map/ppermute | solution.py:341
  129.4 46.3 %collective-permute-start.12 = (bf16[256,2048]{1,0:T(8,128)(2,1)}, bf16[256,2048]{1,0:T(8,128)(2,1)}, u32[]{:S(2)}, u32[]{:S(2)}) collective-permute-start(bf16[256,2048]{1,0:T(8,128)(2,1)} %get-tuple-element.97.refs_0_.g), channel_id=1, source_target_pairs={{0,2},{2,0},{4,6},{6,4},{1,3},{3,1},{5,7},{7,5},{8,10},{10,8},{12,... | collective-permute-start | bytes 3145736 | tf_op jit(solution)/shard_map/ppermute | solution.py:341
  131.8 43.8 %collective-permute-start.7 = (bf16[256,1024]{1,0:T(8,128)(2,1)}, bf16[256,1024]{1,0:T(8,128)(2,1)}, u32[]{:S(2)}, u32[]{:S(2)}) collective-permute-start(bf16[256,1024]{1,0:T(8,128)(2,1)} %bitcast.16), channel_id=1, source_target_pairs={{0,4},{2,6},{4,0},{6,2},{1,5},{3,7},{5,1},{7,3},{8,12},{10,14},{12... | collective-permute-start | bytes 1572872 | tf_op jit(solution)/shard_map/ppermute | solution.py:341
  178.4 169.1 %all-gather.12.cloned.1.call-start = ((), (), s32[]{:S(2)}) async-start(), calls=%async_computation.9 | async-start | bytes 5242880 | tf_op jit(solution)/shard_map/all_gather | solution.py:830
  179.8 9.3 collective-permute-start.13
  180.3 42.4 %collective-permute-start.16 = (bf16[256,2048]{1,0:T(8,128)(2,1)}, bf16[256,2048]{1,0:T(8,128)(2,1)}, u32[]{:S(2)}, u32[]{:S(2)}) collective-permute-start(bf16[256,2048]{1,0:T(8,128)(2,1)} %copy-done.52), channel_id=1, source_target_pairs={{0,2},{2,0},{4,6},{6,4},{1,3},{3,1},{5,7},{7,5},{8,10},{10,8},{12,... | collective-permute-start | bytes 3145736 | tf_op jit(solution)/shard_map/ppermute | solution.py:341
  190.0 32.7 %collective-permute-start.15 = (bf16[256,1024]{1,0:T(8,128)(2,1)}, bf16[256,1024]{1,0:T(8,128)(2,1)}, u32[]{:S(2)}, u32[]{:S(2)}) collective-permute-start(bf16[256,1024]{1,0:T(8,128)(2,1)} %bitcast.24), channel_id=1, source_target_pairs={{0,4},{2,6},{4,0},{6,2},{1,5},{3,7},{5,1},{7,3},{8,12},{10,14},{12... | collective-permute-start | bytes 1572872 | tf_op jit(solution)/shard_map/ppermute | solution.py:341
  225.0 183.3 %all-gather.14.cloned.1.call-start = ((), (), s32[]{:S(2)}) async-start(), calls=%async_computation.10 | async-start | bytes 5242880 | tf_op jit(solution)/shard_map/all_gather | solution.py:830
  228.7 33.0 %collective-permute-start.18 = (bf16[2,256,512]{2,1,0:T(8,128)(2,1)S(1)}, bf16[2,256,512]{2,1,0:T(8,128)(2,1)S(1)}, u32[]{:S(2)}, u32[]{:S(2)}) collective-permute-start(bf16[2,256,512]{2,1,0:T(8,128)(2,1)S(1)} %fusion.32), channel_id=1, source_target_pairs={{0,4},{2,6},{1,5},{3,7},{8,12},{10,14},{9,13},{11,15},{16,20},{18,... | collective-permute-start | bytes 1572872 | tf_op jit(solution)/shard_map/ppermute | solution.py:866
  233.5 28.2 %collective-permute-start.14 = (bf16[2,256,512]{2,1,0:T(8,128)(2,1)S(1)}, bf16[2,256,512]{2,1,0:T(8,128)(2,1)S(1)}, u32[]{:S(2)}, u32[]{:S(2)}) collective-permute-start(bf16[2,256,512]{2,1,0:T(8,128)(2,1)S(1)} %fusion.29), channel_id=1, source_target_pairs={{0,4},{2,6},{1,5},{3,7},{8,12},{10,14},{9,13},{11,15},{16,20},{18,... | collective-permute-start | bytes 1572872 | tf_op jit(solution)/shard_map/ppermute | solution.py:866
  234.8 26.8 %collective-permute-start.17 = (bf16[128,1024]{1,0:T(8,128)(2,1)S(1)}, bf16[128,1024]{1,0:T(8,128)(2,1)S(1)}, u32[]{:S(2)}, u32[]{:S(2)}) collective-permute-start(bf16[128,1024]{1,0:T(8,128)(2,1)S(1)} %get-tuple-element.105), channel_id=1, source_target_pairs={{0,2},{2,0},{4,6},{6,4},{1,3},{3,1},{5,7},{7,5},{8,10},{10,8},{12,... | collective-permute-start | bytes 786440 | tf_op jit(solution)/shard_map/ppermute | solution.py:341
  261.7 21.1 %collective-permute-start.19 = (bf16[256,1024]{1,0:T(8,128)(2,1)S(1)}, bf16[256,1024]{1,0:T(8,128)(2,1)S(1)}, u32[]{:S(2)}, u32[]{:S(2)}) collective-permute-start(bf16[256,1024]{1,0:T(8,128)(2,1)S(1)} %bitcast.279), channel_id=1, source_target_pairs={{0,4},{2,6},{4,0},{6,2},{1,5},{3,7},{5,1},{7,3},{8,12},{10,14},{12... | collective-permute-start | bytes 1572872 | tf_op jit(solution)/shard_map/ppermute | solution.py:341
  290.0 18.8 %collective-permute-start.20 = (bf16[512,2048]{1,0:T(8,128)(2,1)}, bf16[512,2048]{1,0:T(8,128)(2,1)}, u32[]{:S(2)}, u32[]{:S(2)}) collective-permute-start(bf16[512,2048]{1,0:T(8,128)(2,1)} %convolution_convert_fusion.10), channel_id=1, source_target_pairs={{0,1},{1,0},{2,3},{3,2},{4,5},{5,4},{6,7},{7,6},{8,9},{9,8},{10,11... | collective-permute-start | bytes 6291464 | tf_op jit(solution)/shard_map/ppermute | solution.py:341
  291.1 364.0 %reduce-scatter.7.cloned.1.call-start = ((), (), s32[]{:S(2)}) async-start(), calls=%async_computation.11 | async-start | bytes 5242880 | tf_op jit(solution)/shard_map/reduce_scatter | solution.py:833
  292.0 8.7 collective-permute-start.29
  311.4 56.1 %collective-permute-start.23 = (bf16[256,2048]{1,0:T(8,128)(2,1)}, bf16[256,2048]{1,0:T(8,128)(2,1)}, u32[]{:S(2)}, u32[]{:S(2)}) collective-permute-start(bf16[256,2048]{1,0:T(8,128)(2,1)} %add_convert_fusion.19), channel_id=1, source_target_pairs={{0,2},{2,0},{4,6},{6,4},{1,3},{3,1},{5,7},{7,5},{8,10},{10,8},{12,... | collective-permute-start | bytes 3145736 | tf_op jit(solution)/shard_map/ppermute | solution.py:341
  347.4 52.2 %collective-permute-start.21 = (bf16[512,2048]{1,0:T(8,128)(2,1)}, bf16[512,2048]{1,0:T(8,128)(2,1)}, u32[]{:S(2)}, u32[]{:S(2)}) collective-permute-start(bf16[512,2048]{1,0:T(8,128)(2,1)} %convolution_convert_fusion.8), channel_id=1, source_target_pairs={{0,1},{1,0},{2,3},{3,2},{4,5},{5,4},{6,7},{7,6},{8,9},{9,8},{10,11... | collective-permute-start | bytes 6291464 | tf_op jit(solution)/shard_map/ppermute | solution.py:341
  371.4 24.7 %collective-permute-start.24 = (bf16[256,2048]{1,0:T(8,128)(2,1)S(1)}, bf16[256,2048]{1,0:T(8,128)(2,1)S(1)}, u32[]{:S(2)}, u32[]{:S(2)}) collective-permute-start(bf16[256,2048]{1,0:T(8,128)(2,1)S(1)} %get-tuple-element.117.refs_0_), channel_id=1, source_target_pairs={{0,2},{2,0},{4,6},{6,4},{1,3},{3,1},{5,7},{7,5},{8,10},{10,8},{12,... | collective-permute-start | bytes 3145736 | tf_op jit(solution)/shard_map/ppermute | solution.py:341
  381.7 24.2 %collective-permute-start.25 = (bf16[256,2048]{1,0:T(8,128)(2,1)S(1)}, bf16[256,2048]{1,0:T(8,128)(2,1)S(1)}, u32[]{:S(2)}, u32[]{:S(2)}) collective-permute-start(bf16[256,2048]{1,0:T(8,128)(2,1)S(1)} %get-tuple-element.117.refs_0_), channel_id=1, source_target_pairs={{0,1},{1,0},{2,3},{3,2},{4,5},{5,4},{6,7},{7,6},{8,9},{9,8},{10,11... | collective-permute-start | bytes 3145736 | tf_op jit(solution)/shard_map/ppermute | solution.py:341
  396.1 9.8 collective-permute-start.26
  402.2 31.7 %collective-permute-start.22 = (bf16[256,2048]{1,0:T(8,128)(2,1)}, bf16[256,2048]{1,0:T(8,128)(2,1)}, u32[]{:S(2)}, u32[]{:S(2)}) collective-permute-start(bf16[256,2048]{1,0:T(8,128)(2,1)} %add_convert_fusion.18), channel_id=1, source_target_pairs={{0,2},{2,0},{4,6},{6,4},{1,3},{3,1},{5,7},{7,5},{8,10},{10,8},{12,... | collective-permute-start | bytes 3145736 | tf_op jit(solution)/shard_map/ppermute | solution.py:341
  431.3 32.0 %collective-permute-start.34 = (bf16[512,2048]{1,0:T(8,128)(2,1)}, bf16[512,2048]{1,0:T(8,128)(2,1)S(1)}, u32[]{:S(2)}, u32[]{:S(2)}) collective-permute-start(bf16[512,2048]{1,0:T(8,128)(2,1)} %convolution_convert_fusion.6), channel_id=1, source_target_pairs={{0,1},{1,0},{2,3},{3,2},{4,5},{5,4},{6,7},{7,6},{8,9},{9,8},{10,11... | collective-permute-start | bytes 6291464 | tf_op jit(solution)/shard_map/ppermute | solution.py:341
  437.8 25.3 %collective-permute-start.31 = (bf16[256,2048]{1,0:T(8,128)(2,1)S(1)}, bf16[256,2048]{1,0:T(8,128)(2,1)S(1)}, u32[]{:S(2)}, u32[]{:S(2)}) collective-permute-start(bf16[256,2048]{1,0:T(8,128)(2,1)S(1)} %get-tuple-element.121.refs_0_), channel_id=1, source_target_pairs={{0,2},{2,0},{4,6},{6,4},{1,3},{3,1},{5,7},{7,5},{8,10},{10,8},{12,... | collective-permute-start | bytes 3145736 | tf_op jit(solution)/shard_map/ppermute | solution.py:341
  438.4 27.0 %collective-permute-start.32 = (bf16[256,2048]{1,0:T(8,128)(2,1)S(1)}, bf16[256,2048]{1,0:T(8,128)(2,1)S(1)}, u32[]{:S(2)}, u32[]{:S(2)}) collective-permute-start(bf16[256,2048]{1,0:T(8,128)(2,1)S(1)} %get-tuple-element.121.refs_0_), channel_id=1, source_target_pairs={{0,1},{1,0},{2,3},{3,2},{4,5},{5,4},{6,7},{7,6},{8,9},{9,8},{10,11... | collective-permute-start | bytes 3145736 | tf_op jit(solution)/shard_map/ppermute | solution.py:341
  464.6 34.4 %collective-permute-start.35 = (bf16[256,2048]{1,0:T(8,128)(2,1)}, bf16[256,2048]{1,0:T(8,128)(2,1)S(1)}, u32[]{:S(2)}, u32[]{:S(2)}) collective-permute-start(bf16[256,2048]{1,0:T(8,128)(2,1)} %add_convert_fusion.17), channel_id=1, source_target_pairs={{0,2},{2,0},{4,6},{6,4},{1,3},{3,1},{5,7},{7,5},{8,10},{10,8},{12,... | collective-permute-start | bytes 3145736 | tf_op jit(solution)/shard_map/ppermute | solution.py:341
  520.4 241.9 %reduce-scatter.9.cloned.1.call-start = ((), (), s32[]{:S(2)}) async-start(), calls=%async_computation.12 | async-start | bytes 5242880 | tf_op jit(solution)/shard_map/reduce_scatter | solution.py:833
  525.5 25.8 %collective-permute-start.39 = (bf16[512,2048]{1,0:T(8,128)(2,1)S(1)}, bf16[512,2048]{1,0:T(8,128)(2,1)S(1)}, u32[]{:S(2)}, u32[]{:S(2)}) collective-permute-start(bf16[512,2048]{1,0:T(8,128)(2,1)S(1)} %convolution_convert_fusion.4), channel_id=1, source_target_pairs={{0,1},{1,0},{2,3},{3,2},{4,5},{5,4},{6,7},{7,6},{8,9},{9,8},{10,11... | collective-permute-start | bytes 6291464 | tf_op jit(solution)/shard_map/ppermute | solution.py:341
  525.7 25.4 %collective-permute-start.36 = (bf16[256,2048]{1,0:T(8,128)(2,1)S(1)}, bf16[256,2048]{1,0:T(8,128)(2,1)S(1)}, u32[]{:S(2)}, u32[]{:S(2)}) collective-permute-start(bf16[256,2048]{1,0:T(8,128)(2,1)S(1)} %copy-done.60), channel_id=1, source_target_pairs={{0,2},{2,0},{4,6},{6,4},{1,3},{3,1},{5,7},{7,5},{8,10},{10,8},{12,... | collective-permute-start | bytes 3145736 | tf_op jit(solution)/shard_map/ppermute | solution.py:341
  526.8 26.0 %collective-permute-start.37 = (bf16[256,2048]{1,0:T(8,128)(2,1)S(1)}, bf16[256,2048]{1,0:T(8,128)(2,1)S(1)}, u32[]{:S(2)}, u32[]{:S(2)}) collective-permute-start(bf16[256,2048]{1,0:T(8,128)(2,1)S(1)} %copy-done.60), channel_id=1, source_target_pairs={{0,1},{1,0},{2,3},{3,2},{4,5},{5,4},{6,7},{7,6},{8,9},{9,8},{10,11... | collective-permute-start | bytes 3145736 | tf_op jit(solution)/shard_map/ppermute | solution.py:341
  551.7 25.6 %collective-permute-start.40 = (bf16[256,2048]{1,0:T(8,128)(2,1)S(1)}, bf16[256,2048]{1,0:T(8,128)(2,1)S(1)}, u32[]{:S(2)}, u32[]{:S(2)}) collective-permute-start(bf16[256,2048]{1,0:T(8,128)(2,1)S(1)} %add_convert_fusion.16), channel_id=1, source_target_pairs={{0,2},{2,0},{4,6},{6,4},{1,3},{3,1},{5,7},{7,5},{8,10},{10,8},{12,... | collective-permute-start | bytes 3145736 | tf_op jit(solution)/shard_map/ppermute | solution.py:341
  615.7 180.6 %reduce-scatter.13.cloned.1.call-start = ((), (), s32[]{:S(2)}) async-start(), calls=%async_computation.14 | async-start | bytes 5242880 | tf_op jit(solution)/shard_map/reduce_scatter | solution.py:833
  616.9 24.8 %collective-permute-start.41 = (bf16[256,2048]{1,0:T(8,128)(2,1)S(1)}, bf16[256,2048]{1,0:T(8,128)(2,1)S(1)}, u32[]{:S(2)}, u32[]{:S(2)}) collective-permute-start(bf16[256,2048]{1,0:T(8,128)(2,1)S(1)} %copy-done.62), channel_id=1, source_target_pairs={{0,2},{2,0},{4,6},{6,4},{1,3},{3,1},{5,7},{7,5},{8,10},{10,8},{12,... | collective-permute-start | bytes 3145736 | tf_op jit(solution)/shard_map/ppermute | solution.py:341
  617.9 23.8 %collective-permute-start.42 = (bf16[256,2048]{1,0:T(8,128)(2,1)S(1)}, bf16[256,2048]{1,0:T(8,128)(2,1)S(1)}, u32[]{:S(2)}, u32[]{:S(2)}) collective-permute-start(bf16[256,2048]{1,0:T(8,128)(2,1)S(1)} %copy-done.62), channel_id=1, source_target_pairs={{0,1},{1,0},{2,3},{3,2},{4,5},{5,4},{6,7},{7,6},{8,9},{9,8},{10,11... | collective-permute-start | bytes 3145736 | tf_op jit(solution)/shard_map/ppermute | solution.py:341
  689.7 152.9 %reduce-scatter.11.cloned.1.call-start = ((), (), s32[]{:S(2)}) async-start(), calls=%async_computation.13 | async-start | bytes 7864320 | tf_op jit(solution)/shard_map/reduce_scatter | solution.py:833
  715.8 270.8 %reduce-scatter.15.cloned.1.call-start = ((), (), s32[]{:S(2)}) async-start(), calls=%async_computation.15 | async-start | bytes 3932160 | tf_op jit(solution)/shard_map/reduce_scatter | solution.py:833
  717.3 45.0 %collective-permute-start.49 = (bf16[2,256,512]{2,1,0:T(8,128)(2,1)S(1)}, bf16[2,256,512]{2,1,0:T(8,128)(2,1)}, u32[]{:S(2)}, u32[]{:S(2)}) collective-permute-start(bf16[2,256,512]{2,1,0:T(8,128)(2,1)S(1)} %fusion.38), channel_id=1, source_target_pairs={{4,0},{6,2},{5,1},{7,3},{12,8},{14,10},{13,9},{15,11},{20,16},{22,... | collective-permute-start | bytes 1572872 | tf_op jit(solution)/shard_map/ppermute | solution.py:866
  735.0 32.8 %collective-permute-start.48 = (bf16[2,256,512]{2,1,0:T(8,128)(2,1)}, bf16[2,256,512]{2,1,0:T(8,128)(2,1)}, u32[]{:S(2)}, u32[]{:S(2)}) collective-permute-start(bf16[2,256,512]{2,1,0:T(8,128)(2,1)} %fusion.35), channel_id=1, source_target_pairs={{4,0},{6,2},{5,1},{7,3},{12,8},{14,10},{13,9},{15,11},{20,16},{22,... | collective-permute-start | bytes 1572872 | tf_op jit(solution)/shard_map/ppermute | solution.py:866
  740.1 57.5 %collective-permute-start.46 = (bf16[512,2048]{1,0:T(8,128)(2,1)}, bf16[512,2048]{1,0:T(8,128)(2,1)}, u32[]{:S(2)}, u32[]{:S(2)}) collective-permute-start(bf16[512,2048]{1,0:T(8,128)(2,1)} %convolution_convert_fusion), channel_id=1, source_target_pairs={{0,1},{1,0},{2,3},{3,2},{4,5},{5,4},{6,7},{7,6},{8,9},{9,8},{10,11... | collective-permute-start | bytes 6291464 | tf_op jit(solution)/shard_map/ppermute | solution.py:341
  744.0 57.3 %collective-permute-start.44 = (bf16[512,2048]{1,0:T(8,128)(2,1)}, bf16[512,2048]{1,0:T(8,128)(2,1)}, u32[]{:S(2)}, u32[]{:S(2)}) collective-permute-start(bf16[512,2048]{1,0:T(8,128)(2,1)} %convolution_convert_fusion.2), channel_id=1, source_target_pairs={{0,1},{1,0},{2,3},{3,2},{4,5},{5,4},{6,7},{7,6},{8,9},{9,8},{10,11... | collective-permute-start | bytes 6291464 | tf_op jit(solution)/shard_map/ppermute | solution.py:341
  796.3 191.5 %reduce-scatter.17.cloned.1.call-start = ((), (), s32[]{:S(2)}) async-start(), calls=%async_computation.16 | async-start | bytes 3932160 | tf_op jit(solution)/shard_map/reduce_scatter | solution.py:833
  801.3 122.4 %collective-permute-start.47 = (bf16[256,2048]{1,0:T(8,128)(2,1)}, bf16[256,2048]{1,0:T(8,128)(2,1)S(1)}, u32[]{:S(2)}, u32[]{:S(2)}) collective-permute-start(bf16[256,2048]{1,0:T(8,128)(2,1)} %add_convert_fusion.14), channel_id=1, source_target_pairs={{0,2},{2,0},{4,6},{6,4},{1,3},{3,1},{5,7},{7,5},{8,10},{10,8},{12,... | collective-permute-start | bytes 3145736 | tf_op jit(solution)/shard_map/ppermute | solution.py:341
  803.9 121.6 %collective-permute-start.45 = (bf16[256,2048]{1,0:T(8,128)(2,1)}, bf16[256,2048]{1,0:T(8,128)(2,1)S(1)}, u32[]{:S(2)}, u32[]{:S(2)}) collective-permute-start(bf16[256,2048]{1,0:T(8,128)(2,1)} %add_convert_fusion.15), channel_id=1, source_target_pairs={{0,2},{2,0},{4,6},{6,4},{1,3},{3,1},{5,7},{7,5},{8,10},{10,8},{12,... | collective-permute-start | bytes 3145736 | tf_op jit(solution)/shard_map/ppermute | solution.py:341
  824.5 26.3 %collective-permute-start.50 = (bf16[512,2048]{1,0:T(8,128)(2,1)}, bf16[512,2048]{1,0:T(8,128)(2,1)}, u32[]{:S(2)}, u32[]{:S(2)}) collective-permute-start(bf16[512,2048]{1,0:T(8,128)(2,1)} %add_convert_fusion.8), channel_id=1, source_target_pairs={{0,1},{1,0},{2,3},{3,2},{4,5},{5,4},{6,7},{7,6},{8,9},{9,8},{10,11... | collective-permute-start | bytes 6291464 | tf_op jit(solution)/shard_map/ppermute | solution.py:341
  833.0 22.0 %collective-permute-start.52 = (bf16[512,2048]{1,0:T(8,128)(2,1)}, bf16[512,2048]{1,0:T(8,128)(2,1)}, u32[]{:S(2)}, u32[]{:S(2)}) collective-permute-start(bf16[512,2048]{1,0:T(8,128)(2,1)} %add_convert_fusion.6), channel_id=1, source_target_pairs={{0,1},{1,0},{2,3},{3,2},{4,5},{5,4},{6,7},{7,6},{8,9},{9,8},{10,11... | collective-permute-start | bytes 6291464 | tf_op jit(solution)/shard_map/ppermute | solution.py:341
  841.6 71.4 %collective-permute-start.58 = (bf16[256,3072]{1,0:T(8,128)(2,1)}, bf16[256,3072]{1,0:T(8,128)(2,1)}, u32[]{:S(2)}, u32[]{:S(2)}) collective-permute-start(bf16[256,3072]{1,0:T(8,128)(2,1)} %slice.463), channel_id=1, source_target_pairs={{0,4},{2,6},{4,0},{6,2},{1,5},{3,7},{5,1},{7,3},{8,12},{10,14},{12... | collective-permute-start | bytes 4718600 | tf_op jit(solution)/shard_map/ppermute | solution.py:341
  854.2 83.8 %collective-permute-start.51 = (bf16[256,2048]{1,0:T(8,128)(2,1)}, bf16[256,2048]{1,0:T(8,128)(2,1)}, u32[]{:S(2)}, u32[]{:S(2)}) collective-permute-start(bf16[256,2048]{1,0:T(8,128)(2,1)} %add_convert_fusion.13), channel_id=1, source_target_pairs={{0,2},{2,0},{4,6},{6,4},{1,3},{3,1},{5,7},{7,5},{8,10},{10,8},{12,... | collective-permute-start | bytes 3145736 | tf_op jit(solution)/shard_map/ppermute | solution.py:341
  857.5 75.7 %collective-permute-start.53 = (bf16[256,2048]{1,0:T(8,128)(2,1)}, bf16[256,2048]{1,0:T(8,128)(2,1)S(1)}, u32[]{:S(2)}, u32[]{:S(2)}) collective-permute-start(bf16[256,2048]{1,0:T(8,128)(2,1)} %add_convert_fusion.12), channel_id=1, source_target_pairs={{0,2},{2,0},{4,6},{6,4},{1,3},{3,1},{5,7},{7,5},{8,10},{10,8},{12,... | collective-permute-start | bytes 3145736 | tf_op jit(solution)/shard_map/ppermute | solution.py:341
  917.7 31.3 %collective-permute-start.59 = (bf16[128,3072]{1,0:T(8,128)(2,1)}, bf16[128,3072]{1,0:T(8,128)(2,1)}, u32[]{:S(2)}, u32[]{:S(2)}) collective-permute-start(bf16[128,3072]{1,0:T(8,128)(2,1)} %fusion.57), channel_id=1, source_target_pairs={{0,2},{2,0},{4,6},{6,4},{1,3},{3,1},{5,7},{7,5},{8,10},{10,8},{12,... | collective-permute-start | bytes 2359304 | tf_op jit(solution)/shard_map/ppermute | solution.py:341
  950.3 35.1 %collective-permute-start.54 = (bf16[256,1536]{1,0:T(8,128)(2,1)S(1)}, bf16[256,1536]{1,0:T(8,128)(2,1)S(1)}, u32[]{:S(2)}, u32[]{:S(2)}) collective-permute-start(bf16[256,1536]{1,0:T(8,128)(2,1)S(1)} %slice.451), channel_id=1, source_target_pairs={{0,4},{2,6},{4,0},{6,2},{1,5},{3,7},{5,1},{7,3},{8,12},{10,14},{12... | collective-permute-start | bytes 2359304 | tf_op jit(solution)/shard_map/ppermute | solution.py:341
  986.5 15.3 %collective-permute-start.55 = (bf16[128,1536]{1,0:T(8,128)(2,1)}, bf16[128,1536]{1,0:T(8,128)(2,1)S(1)}, u32[]{:S(2)}, u32[]{:S(2)}) collective-permute-start(bf16[128,1536]{1,0:T(8,128)(2,1)} %fusion.76), channel_id=1, source_target_pairs={{0,2},{2,0},{4,6},{6,4},{1,3},{3,1},{5,7},{7,5},{8,10},{10,8},{12,... | collective-permute-start | bytes 1179656 | tf_op jit(solution)/shard_map/ppermute | solution.py:341
  989.1 37.3 %collective-permute-start.56 = (bf16[256,1536]{1,0:T(8,128)(2,1)S(1)}, bf16[256,1536]{1,0:T(8,128)(2,1)S(1)}, u32[]{:S(2)}, u32[]{:S(2)}) collective-permute-start(bf16[256,1536]{1,0:T(8,128)(2,1)S(1)} %slice.455), channel_id=1, source_target_pairs={{0,4},{2,6},{4,0},{6,2},{1,5},{3,7},{5,1},{7,3},{8,12},{10,14},{12... | collective-permute-start | bytes 2359304 | tf_op jit(solution)/shard_map/ppermute | solution.py:341
  1026.8 10.3 collective-permute-start.57
  (161 other events, 3591.8 us)
Sparse Core Ops, SparseCore 0:
  66.3 72.0 all-gather.5
  140.8 70.1 all-gather.7
  213.4 52.6 all-gather.9
  268.5 52.6 all-gather.11
  322.9 52.6 all-gather.13
  520.5 50.3 reduce-scatter.6
  615.8 50.3 reduce-scatter.8
  689.9 50.3 reduce-scatter.12
  743.5 70.1 reduce-scatter.10
  816.9 43.9 reduce-scatter.14
  864.1 43.9 reduce-scatter.16
